TPU v7x, 32 devices: a whole 2x2x4 slice. The times are simulated.
32 devices in a mesh: groups: 2 (over y), gx: 4 (over z), gy: 2 (over x), sa: 2 (over core).
Axes of the slice: x: 2, y: 2, z: 4, core: 2. Of those that a mesh axis runs over, the one named last changes fastest.
Arguments:
- source_now: float32 [4, 128, 48, 128], P(('groups', 'sa'), 'gx', 'gy'), parts along dimension 0, may hold values from -6 to 6
- source_later: float32 [4, 128, 48, 128], P(('groups', 'sa'), 'gx', 'gy'), parts along dimension 0, may hold values from -6 to 6
- receiver_now: float32 [4, 128, 48, 128], P(('groups', 'sa'), 'gx', 'gy'), parts along dimension 0, may hold values from -6 to 6
- receiver_later: float32 [4, 128, 48, 128], P(('groups', 'sa'), 'gx', 'gy'), parts along dimension 0, may hold values from -6 to 6
- courant: float32 [128, 48, 128], P('gx', 'gy'), may hold values from 0.05 to 0.19
- wavelet: float32 [4, 12], P(('groups', 'sa')), parts along dimension 0, may hold values from -8 to 8
- traces: float32 [4, 12, 64], P(('groups', 'sa')), parts along dimension 0, may hold values from -6 to 6
- source_inline: int32 [4], P(('groups', 'sa')), parts along dimension 0, may hold values from 0 to 127
- source_crossline: int32 [4], P(('groups', 'sa')), parts along dimension 0, may hold values from 0 to 47
- receiver_inline: int32 [4, 64], P(('groups', 'sa')), parts along dimension 0, may hold values from 0 to 127
- receiver_crossline: int32 [4, 64], P(('groups', 'sa')), parts along dimension 0, may hold values from 0 to 47
Outputs:
- source_first: float32 [4, 128, 48, 128], P(('groups', 'sa'), 'gx', 'gy'), parts along dimension 0
- source_second: float32 [4, 128, 48, 128], P(('groups', 'sa'), 'gx', 'gy'), parts along dimension 0
- receiver_first: float32 [4, 128, 48, 128], P(('groups', 'sa'), 'gx', 'gy'), parts along dimension 0
- receiver_second: float32 [4, 128, 48, 128], P(('groups', 'sa'), 'gx', 'gy'), parts along dimension 0
- image_stack: float32 [256, 48, 128], P(('groups', 'gx', 'sa'), 'gy'), parts along dimension 0
There are 2 independent parts, one for each index of `groups`. A program takes and returns all parts, laid end to end along the dimension named above; an argument that names none is the same for every part. Nothing has to cross between parts.
All inputs are finite; a program needn't handle non-finite values.
Results may differ from a plain program's by a relative error of at most 0.0003.
Values sent between devices are 32-bit elements; how exact they have to be, the bound alone decides.
No kernel may reach another device: no remote copies, remote signals or barrier semaphores. Data moves between devices by JAX's collectives and lax.ppermute only.
A program may use at most 128 MiB of HBM per device.

v0:
```python
import itertools

import jax
import jax.numpy as jnp
from jax import lax
from jax.experimental import pallas as pl
from jax.experimental.pallas import tpu as pltpu
from jax.sharding import PartitionSpec as P

SRC_DEPTH = 3
REC_DEPTH = 2
STEPS = 12
COEFFS = (-205.0 / 72.0, 8.0 / 5.0, -1.0 / 5.0, 8.0 / 315.0, -1.0 / 560.0)
RADIUS = 4
LANES = 128
SUB = 8
DEEP = 2
HALO = RADIUS * DEEP
CHUNK = 8
GENERAL_BLOCK = 4
GENERAL_BLOCKS = 3
VMEM_LIMIT = 24 << 20

VM = pl.BlockSpec(memory_space=pltpu.VMEM)
SM = pl.BlockSpec(memory_space=pltpu.SMEM)
ANY = pl.BlockSpec(memory_space=pl.ANY)
F32 = jnp.float32


class Geometry:
    def __init__(self, mesh, nx, ny):
        self.mesh = mesh
        self.nx, self.ny = nx, ny
        self.xe = nx + 2 * HALO
        self.win = ny + HALO
        self.jn = self.win // SUB
        self.gx = mesh.shape["gx"]
        self.srows = ny // self.jn

    def place(self):
        p = lax.axis_index("gy")
        g = lax.axis_index("gx")
        odd = g % 2
        even_right = odd == 0
        even_ok = jnp.logical_or(odd == 1, g + 1 < self.gx)
        odd_right = odd == 1
        odd_ok = jnp.logical_or(jnp.logical_and(odd == 1, g + 1 < self.gx), jnp.logical_and(odd == 0, g > 0))
        return p, g, ((even_right, even_ok), (odd_right, odd_ok))


def permutation(mesh, move):
    names = mesh.axis_names
    sizes = [mesh.shape[n] for n in names]
    pairs = []
    for idx in itertools.product(*[range(s) for s in sizes]):
        at = dict(zip(names, idx))
        to = move(dict(at))
        if to is None:
            to = dict(at)
            to["sa"] = (mesh.shape["sa"] - 1) - at["sa"]
        a = b = 0
        for n, s in zip(names, sizes):
            a, b = a * s + at[n], b * s + to[n]
        pairs.append((a, b))
    return pairs


def neighbour(mesh, parity, flip_y, step_x):
    count = mesh.shape["gx"]

    def move(at):
        if step_x:
            to = at["gx"] + 1 if at["gx"] % 2 == parity else at["gx"] - 1
            if to < 0 or to >= count:
                return None
            at["gx"] = to
        if flip_y:
            at["gy"] = 1 - at["gy"]
        return at

    return permutation(mesh, move)


def call(body, out_shapes, specs, args, out_specs=None, scratch=(), aliases=None):
    return pl.pallas_call(
        body,
        out_shape=out_shapes,
        in_specs=specs,
        out_specs=out_specs if out_specs is not None else [VM] * len(out_shapes),
        scratch_shapes=list(scratch),
        input_output_aliases=aliases or {},
        compiler_params=pltpu.CompilerParams(vmem_limit_bytes=VMEM_LIMIT),
    )(*args)


def shape(*dims):
    return jax.ShapeDtypeStruct(dims, F32)


def message_shapes(geo, first):
    extra = 3 if first else 0
    y = shape(2 * geo.nx + extra * geo.nx // 2, SUB, LANES)
    x = shape(2 * HALO + extra * RADIUS, geo.ny, LANES)
    d = shape(2 * RADIUS // 2, SUB, LANES)
    return [y, x, x, d, d]


def pack(geo, fields, extras, messages):
    p, _, sides = geo.place()
    my, me, mo, de, do = messages
    nx = geo.nx

    def ybody(x, carry):
        for f, u in enumerate(fields):
            for i in range(2):
                my[f * nx + x, 4 * i : 4 * i + 4, :] = u[x + HALO, pl.ds(4 + i - 2 * p, 4, stride=SUB), :]
        return carry

    lax.fori_loop(0, nx, ybody, 0, unroll=4)
    if extras:

        def yextra(h, carry):
            for f, u in enumerate(extras):
                for i in range(2):
                    rows = u[2 * h + i + HALO, pl.ds(5 - 3 * p, 4, stride=SUB), :]
                    my[2 * nx + f * (nx // 2) + h, 4 * i : 4 * i + 4, :] = rows
            return carry

        lax.fori_loop(0, nx // 2, yextra, 0, unroll=2)
    for (right, _), mx, md in zip(sides, (me, mo), (de, do)):
        wide = jnp.where(right, nx, HALO)
        thin = jnp.where(right, nx + HALO - RADIUS, HALO)

        def xbody(i, carry, mx=mx, wide=wide):
            for f, u in enumerate(fields):
                for q in range(geo.srows):
                    mx[f * HALO + i, 4 * q : 4 * q + 4, :] = u[wide + i, pl.ds(2 * p + q, 4, stride=SUB), :]
            return carry

        lax.fori_loop(0, HALO, xbody, 0, unroll=2)
        for i in range(RADIUS):
            for f, u in enumerate(extras):
                for q in range(geo.srows):
                    mx[2 * HALO + f * RADIUS + i, 4 * q : 4 * q + 4, :] = u[thin + i, pl.ds(2 * p + q, 4, stride=SUB), :]
            for f, u in enumerate(fields):
                rows = u[thin + i, pl.ds(5 - 3 * p, 4, stride=SUB), :]
                md[2 * f + i // 2, 4 * (i % 2) : 4 * (i % 2) + 4, :] = rows


def unpack(geo, fields, extras, messages):
    p, _, sides = geo.place()
    my, me, mo, de, do = messages
    nx = geo.nx

    def ybody(x, carry):
        for f, u in enumerate(fields):
            for i in range(2):
                u[x + HALO, pl.ds(6 + i - 6 * p, 4, stride=SUB), :] = my[f * nx + x, 4 * i : 4 * i + 4, :]
        return carry

    lax.fori_loop(0, nx, ybody, 0, unroll=4)
    if extras:

        def yextra(h, carry):
            for f, u in enumerate(extras):
                for i in range(2):
                    rows = my[2 * nx + f * (nx // 2) + h, 4 * i : 4 * i + 4, :]
                    u[2 * h + i + HALO, pl.ds(6 - 5 * p, 4, stride=SUB), :] = rows
            return carry

        lax.fori_loop(0, nx // 2, yextra, 0, unroll=2)
    for (right, ok), mx, md in zip(sides, (me, mo), (de, do)):

        @pl.when(ok)
        def _(right=right, mx=mx, md=md):
            wide = jnp.where(right, nx + HALO, 0)
            thin = jnp.where(right, nx + HALO, HALO - RADIUS)

            def xbody(i, carry):
                for f, u in enumerate(fields):
                    for q in range(geo.srows):
                        u[wide + i, pl.ds(2 * p + q, 4, stride=SUB), :] = mx[f * HALO + i, 4 * q : 4 * q + 4, :]
                return carry

            lax.fori_loop(0, HALO, xbody, 0, unroll=2)
            for i in range(RADIUS):
                for f, u in enumerate(extras):
                    for q in range(geo.srows):
                        rows = mx[2 * HALO + f * RADIUS + i, 4 * q : 4 * q + 4, :]
                        u[thin + i, pl.ds(2 * p + q, 4, stride=SUB), :] = rows
                for f, u in enumerate(fields):
                    rows = md[2 * f + i // 2, 4 * (i % 2) : 4 * (i % 2) + 4, :]
                    u[thin + i, pl.ds(6 - 5 * p, 4, stride=SUB), :] = rows


def load_kernel(geo):
    nx, ny, xe = geo.nx, geo.ny, geo.xe

    def body(s0, s1, r0, r1, c0, us, ur, ps, pr, cc, dw, my, me, mo, de, do, pad, sem):
        p, _, _ = geo.place()
        inside = pl.ds(pl.multiple_of(SUB * p, SUB), ny)
        sources = (s0.at[0], r0.at[0], s1.at[0], r1.at[0], c0)
        copies = [
            pltpu.make_async_copy(src, pad.at[f, :, inside, :], sem.at[f]) for f, src in enumerate(sources)
        ]
        for copy in copies:
            copy.start()
        outside = pl.ds(pl.multiple_of(ny - ny * p, SUB), SUB)
        targets = (us, ur, ps, pr, cc)
        row = lax.broadcasted_iota(jnp.int32, (LANES, LANES), 0)
        col = lax.broadcasted_iota(jnp.int32, (LANES, LANES), 1)
        gap = jnp.abs(row - col)
        d = jnp.zeros((LANES, LANES), F32)
        for k in range(1, RADIUS + 1):
            d = jnp.where(gap == k, COEFFS[k], d)
        hi = d.astype(jnp.bfloat16)
        lo = (d - hi.astype(F32)).astype(jnp.bfloat16)
        dw[0:LANES, 0:LANES] = hi
        dw[0:LANES, LANES : 2 * LANES] = lo
        dw[LANES : 2 * LANES, 0:LANES] = hi
        dw[LANES : 2 * LANES, LANES : 2 * LANES] = jnp.zeros_like(lo)
        zero = jnp.zeros((geo.win, LANES), F32)
        for f, u in enumerate(targets):
            for x in range(nx):
                pad[f, x, outside, :] = jnp.zeros((SUB, LANES), F32)
            for x in range(HALO):
                u[x] = zero
                u[nx + HALO + x] = zero
        for f, (u, copy) in enumerate(zip(targets, copies)):
            copy.wait()

            def turn(x, carry, f=f, u=u):
                for j in range(geo.jn):
                    u[x + HALO, SUB * j : SUB * j + SUB, :] = pad[f, x, pl.ds(j, SUB, stride=geo.jn), :]
                return carry

            lax.fori_loop(0, nx, turn, 0, unroll=4)
        pack(geo, (us, ur), (ps, pr, cc), (my, me, mo, de, do))

    return body


def receiver_kernel(geo, nrec):
    rows_all = geo.xe * geo.win
    block = 128

    def body(ri, rc, traces, out, table):
        p, g, _ = geo.place()
        x = ri[...] - g * geo.nx + HALO
        w = rc[...] - p * geo.ny + SUB * p
        ok = (x >= 0) & (x < geo.xe) & (w >= 0) & (w < geo.win)
        shift = geo.jn.bit_length() - 1
        row = x * geo.win + (w & (geo.jn - 1)) * SUB + (w >> shift)
        row = jnp.where(ok, row, -1)
        table[...] = jnp.zeros_like(table)
        table[0:STEPS, :] = traces[0]
        tab = table[...]

        def chunk(i, carry):
            at = i * block + lax.broadcasted_iota(jnp.int32, (block, nrec), 0)
            hot = jnp.where(at == row, 1.0, 0.0).astype(F32)
            plane = lax.dot_general(
                hot, tab, (((1,), (1,)), ((), ())), precision=lax.Precision.HIGHEST, preferred_element_type=F32
            )
            planes = block // geo.win
            out[pl.ds(i * planes, planes)] = plane.reshape(planes, geo.win, LANES)
            return carry

        lax.fori_loop(0, rows_all // block, chunk, 0)

    return body


def depth_part(geo, u, z, dw, first, count):
    w = dw[...]

    def chunk(i, carry):
        at = first + i * CHUNK
        rows = u[pl.ds(at, CHUNK)].reshape(CHUNK * geo.win, LANES)
        hi = rows.astype(jnp.bfloat16)
        lo = (rows - hi.astype(F32)).astype(jnp.bfloat16)
        both = jnp.dot(jnp.concatenate([hi, lo], axis=1), w, preferred_element_type=F32)
        z[pl.ds(at, CHUNK)] = (both[:, :LANES] + both[:, LANES:]).reshape(CHUNK, geo.win, LANES)
        return carry

    lax.fori_loop(0, count // CHUNK, chunk, 0)


def update_plane(geo, u, prior, cc, z, x, sub, extra):
    jn = geo.jn
    mid = [u[x, SUB * j : SUB * j + SUB, :] for j in range(jn)]
    first, last = sub == 0, sub == SUB - 1
    below = [jnp.where(first, 0.0, pltpu.roll(v, 1, 0)) for v in mid]
    above = [jnp.where(last, 0.0, pltpu.roll(v, SUB - 1, 0)) for v in mid]
    line = below + mid + above
    news = []
    for j in range(jn):
        tile = slice(SUB * j, SUB * j + SUB)
        acc = z[x, tile, :] + (3.0 * COEFFS[0]) * mid[j]
        for k in range(1, RADIUS + 1):
            near = (u[x + k, tile, :] + u[x - k, tile, :]) + (line[jn + j + k] + line[jn + j - k])
            acc = acc + COEFFS[k] * near
        if extra is not None:
            acc = acc + extra(j)
        new = (2.0 * mid[j] - prior[x, tile, :]) + cc[x, tile, :] * acc
        prior[x, tile, :] = new
        news.append(new)
    return news


def one_step(geo, moment, us, ur, ps, pr, cc, gg, corr, zs, zr, dw, wavelet, src, first, count, fresh):
    nx = geo.nx
    depth_part(geo, us, zs, dw, first, count)
    depth_part(geo, ur, zr, dw, first, count)
    sub = lax.broadcasted_iota(jnp.int32, (SUB, LANES), 0)
    lane = lax.broadcasted_iota(jnp.int32, (SUB, LANES), 1)
    at_depth = lane == REC_DEPTH

    def plane(x, carry, inner):
        def fed(j):
            rows = gg[x, SUB * j : SUB * j + SUB, :]
            return jnp.where(at_depth, pltpu.roll(rows, (REC_DEPTH - moment) % LANES, 1), 0.0)

        news = update_plane(geo, us, ps, cc, zs, x, sub, None)
        newr = update_plane(geo, ur, pr, cc, zr, x, sub, fed)
        if inner:
            for j in range(geo.jn):
                tile = slice(SUB * j, SUB * j + SUB)
                product = news[j] * newr[j]
                if not fresh:
                    product = product + corr[x - HALO, tile, :]
                corr[x - HALO, tile, :] = product
        return carry

    edge = HALO - first
    if edge > 0:
        lax.fori_loop(first, HALO, lambda x, c: plane(x, c, False), 0)
        lax.fori_loop(nx + HALO, first + count, lambda x, c: plane(x, c, False), 0)
    lax.fori_loop(HALO, nx + HALO, lambda x, c: plane(x, c, True), 0)
    xs, row, ok = src

    @pl.when(ok & (xs >= first) & (xs < first + count))
    def _():
        shot = jnp.where(lane[0:1] == SRC_DEPTH, wavelet[0, moment], 0.0)
        add = cc[xs, pl.ds(row, 1), :] * shot
        ps[xs, pl.ds(row, 1), :] = ps[xs, pl.ds(row, 1), :] + add

        @pl.when((xs >= HALO) & (xs < nx + HALO))
        def _():
            corr[xs - HALO, pl.ds(row, 1), :] = (
                corr[xs - HALO, pl.ds(row, 1), :] + add * pr[xs, pl.ds(row, 1), :]
            )


def round_kernel(geo, block, last):
    first_round = block == 0

    def body(*refs):
        refs = list(refs)
        take = lambda n: [refs.pop(0) for _ in range(n)]
        us0, ur0, ps0, pr0, cc0, dw, gg = take(7)
        if not first_round:
            take(1)
        inputs = take(5)
        wavelet, sx, sy = take(3)
        us, ur, ps, pr, cc, corr = take(6)
        outs = [] if last else take(5)
        zs, zr = take(2)
        p, g, _ = geo.place()
        xs = sx[0] - g * geo.nx + HALO
        w = sy[0] - p * geo.ny + SUB * p
        ok = (w >= 0) & (w < geo.win) & (xs >= 0) & (xs < geo.xe)
        shift = geo.jn.bit_length() - 1
        src = (xs, (w & (geo.jn - 1)) * SUB + (w >> shift), ok)
        unpack(geo, (us, ur), (ps, pr, cc) if first_round else (), inputs)
        common = (cc, gg, corr, zs, zr, dw, wavelet, src)
        one_step(geo, DEEP * block, us, ur, ps, pr, *common, HALO - RADIUS, geo.nx + 2 * RADIUS, first_round)
        one_step(geo, DEEP * block + 1, ps, pr, us, ur, *common, HALO, geo.nx, False)
        if not last:
            pack(geo, (us, ur), (), outs)

    return body


def corr_kernel(geo, halves):
    part = geo.nx // halves

    def body(corr, mine, other, pad):
        p, _, _ = geo.place()
        q = lax.axis_index("sa")

        def turn(x, carry):
            for j in range(geo.jn):
                pad[x, pl.ds(j, SUB, stride=geo.jn), :] = corr[x, SUB * j : SUB * j + SUB, :]
            return carry

        lax.fori_loop(0, geo.nx, turn, 0, unroll=4)
        inside = pl.ds(pl.multiple_of(SUB * p, SUB), geo.ny)

        def split(x, carry):
            mine[x] = pad[q * part + x, inside, :]
            other[x] = pad[(halves - 1 - q) * part + x, inside, :]
            return carry

        lax.fori_loop(0, part, split, 0, unroll=2)

    return body


def store_kernel(geo):
    def body(us, ur, ps, pr, o0, o1, o2, o3, pad, sem):
        p, _, _ = geo.place()
        inside = pl.ds(pl.multiple_of(SUB * p, SUB), geo.ny)
        copies = []
        for f, (u, o) in enumerate(((us, o0), (ps, o1), (ur, o2), (pr, o3))):

            def turn(x, carry, f=f, u=u):
                for j in range(geo.jn):
                    pad[f, x, pl.ds(j, SUB, stride=geo.jn), :] = u[x + HALO, SUB * j : SUB * j + SUB, :]
                return carry

            lax.fori_loop(0, geo.nx, turn, 0, unroll=4)
            copy = pltpu.make_async_copy(pad.at[f, :, inside, :], o.at[0], sem.at[f])
            copy.start()
            copies.append(copy)
        for copy in copies:
            copy.wait()

    return body


def fast_body(mesh):
    def run(sn, sl, rn, rl, courant, wavelet, traces, si, sc, ri, rc):
        nx, ny, nz = courant.shape
        geo = Geometry(mesh, nx, ny)
        state = shape(geo.xe, geo.win, nz)
        names = mesh.axis_names
        routes = [
            neighbour(mesh, 0, True, False),
            neighbour(mesh, 0, False, True),
            neighbour(mesh, 1, False, True),
            neighbour(mesh, 0, True, True),
            neighbour(mesh, 1, True, True),
        ]
        send = lambda ms: [lax.ppermute(m, names, route) for m, route in zip(ms, routes)]
        loaded = call(
            load_kernel(geo),
            [state] * 5
            + [jax.ShapeDtypeStruct((2 * LANES, 2 * LANES), jnp.bfloat16)]
            + message_shapes(geo, True),
            [ANY] * 5,
            (sn, sl, rn, rl, courant),
            scratch=[pltpu.VMEM((5, nx, geo.win, nz), F32), pltpu.SemaphoreType.DMA((5,))],
        )
        us, ur, ps, pr, cc, dw = loaded[:6]
        messages = send(loaded[6:])
        nrec = traces.shape[2]
        (gg,) = call(
            receiver_kernel(geo, nrec),
            [state],
            [VM] * 3,
            (ri, rc, traces),
            scratch=[pltpu.VMEM((LANES, nrec), F32)],
        )
        corr = None
        blocks = STEPS // DEEP
        for block in range(blocks):
            last = block == blocks - 1
            args = [us, ur, ps, pr, cc, dw, gg] + ([] if corr is None else [corr]) + messages
            specs = [VM] * len(args) + [SM] * 3
            aliases = {i: i for i in range(5)}
            if corr is not None:
                aliases[7] = 5
            outs = call(
                round_kernel(geo, block, last),
                [state] * 5 + [shape(nx, geo.win, nz)] + ([] if last else message_shapes(geo, False)),
                specs,
                args + [wavelet, si, sc],
                scratch=[pltpu.VMEM((geo.xe, geo.win, nz), F32)] * 2,
                aliases=aliases,
            )
            us, ur, ps, pr, cc, corr = outs[:6]
            if not last:
                messages = send(outs[6:])
        halves = mesh.shape["sa"]
        part = shape(nx // halves, ny, nz)
        mine, other = call(
            corr_kernel(geo, halves), [part] * 2, [VM], (corr,), scratch=[pltpu.VMEM((nx, geo.win, nz), F32)]
        )
        pairs = [(i, halves - 1 - i) for i in range(halves)]
        image = (mine + lax.ppermute(other, "sa", pairs)) / STEPS
        fields = call(
            store_kernel(geo),
            [shape(1, nx, ny, nz)] * 4,
            [VM] * 4,
            (us, ur, ps, pr),
            out_specs=[ANY] * 4,
            scratch=[pltpu.VMEM((4, nx, geo.win, nz), F32), pltpu.SemaphoreType.DMA((4,))],
        )
        return (*fields, image)

    return run


def padded_2(cells, sides, width):
    for axis, dim in sides:
        count = lax.axis_size(axis)
        ends = count - 1
        head = lax.slice_in_dim(cells, 0, width, axis=dim)
        tail = lax.slice_in_dim(cells, cells.shape[dim] - width, cells.shape[dim], axis=dim)
        cells = jnp.concatenate(
            [
                lax.ppermute(tail, axis, [(i, (i + 1) % count) for i in range(ends)]),
                cells,
                lax.ppermute(head, axis, [((i + 1) % count, i) for i in range(ends)]),
            ],
            axis=dim,
        )
    return cells


def laplace(padded):
    inline_span = padded.shape[0] - 8
    cross_span = padded.shape[1] - 8
    center = padded[4 : 4 + inline_span, 4 : 4 + cross_span]
    depth_span = center.shape[2]
    depth_padded = jnp.pad(center, ((0, 0), (0, 0), (4, 4)))
    summed = 3.0 * COEFFS[0] * center
    for distance in range(1, 5):
        neighbours = (
            padded[4 + distance : 4 + distance + inline_span, 4 : 4 + cross_span]
            + padded[4 - distance : 4 - distance + inline_span, 4 : 4 + cross_span]
        )
        neighbours = (
            neighbours
            + padded[4 : 4 + inline_span, 4 + distance : 4 + distance + cross_span]
            + padded[4 : 4 + inline_span, 4 - distance : 4 - distance + cross_span]
        )
        neighbours = (
            neighbours
            + depth_padded[:, :, 4 + distance : 4 + distance + depth_span]
            + depth_padded[:, :, 4 - distance : 4 - distance + depth_span]
        )
        summed = summed + COEFFS[distance] * neighbours
    return summed


def crop_margin(values, margin_cut):
    if margin_cut == 0:
        return values
    return values[
        margin_cut : values.shape[0] - margin_cut, margin_cut : values.shape[1] - margin_cut
    ]


def general_body(
    source_now,
    source_later,
    receiver_now,
    receiver_later,
    courant,
    wavelet,
    traces,
    source_inline,
    source_crossline,
    receiver_inline,
    receiver_crossline,
):
    inline_count, cross_count, depth_count = courant.shape
    inline_anchor = lax.axis_index("gx") * inline_count
    cross_anchor = lax.axis_index("gy") * cross_count
    inline_extent = inline_count * lax.axis_size("gx")
    cross_extent = cross_count * lax.axis_size("gy")
    depth_axis = jnp.arange(depth_count)
    source_layer = (depth_axis == SRC_DEPTH).astype(jnp.float32)
    receiver_layer = (depth_axis == REC_DEPTH).astype(jnp.float32)
    wavelet_row = wavelet[0]
    records = traces[0]
    source_field = source_now[0]
    source_prior = source_later[0]
    receiver_field = receiver_now[0]
    receiver_prior = receiver_later[0]
    correlation = jnp.zeros(courant.shape, jnp.float32)
    widest = 4 * (GENERAL_BLOCK - 1)
    speed_wide = padded_2(courant, (("gx", 0), ("gy", 1)), widest)
    inline_cells = inline_anchor - widest + jnp.arange(inline_count + 2 * widest)
    cross_cells = cross_anchor - widest + jnp.arange(cross_count + 2 * widest)
    inline_hot = (inline_cells[:, None] == receiver_inline[0][None, :]).astype(jnp.float32)
    cross_hot = (receiver_crossline[0][:, None] == cross_cells[None, :]).astype(jnp.float32)
    receivers = cross_hot.shape[0]
    weighted = (records.T[:, :, None] * cross_hot[:, None, :]).reshape(
        receivers, STEPS * cross_hot.shape[1]
    )
    planes = jnp.dot(inline_hot, weighted, precision=lax.Precision.HIGHEST).reshape(
        inline_hot.shape[0], STEPS, cross_hot.shape[1]
    )
    source_spot = (inline_cells == source_inline[0]).astype(jnp.float32)[:, None] * (
        cross_cells == source_crossline[0]
    ).astype(jnp.float32)[None, :]
    inline_in = ((inline_cells >= 0) & (inline_cells < inline_extent)).astype(jnp.float32)
    cross_in = ((cross_cells >= 0) & (cross_cells < cross_extent)).astype(jnp.float32)
    inside = inline_in[:, None, None] * cross_in[None, :, None]
    planes, source_spot, inside = (planes, source_spot, inside)
    for segment in range(GENERAL_BLOCKS):
        source_wide, receiver_wide = (
            padded_2(source_field, (("gx", 0), ("gy", 1)), 4 * GENERAL_BLOCK),
            padded_2(receiver_field, (("gx", 0), ("gy", 1)), 4 * GENERAL_BLOCK),
        )
        source_back, receiver_back = (
            padded_2(source_prior, (("gx", 0), ("gy", 1)), widest),
            padded_2(receiver_prior, (("gx", 0), ("gy", 1)), widest),
        )
        for substep in range(GENERAL_BLOCK):
            margin = 4 * (GENERAL_BLOCK - 1 - substep)
            offset = widest - margin
            moment = segment * GENERAL_BLOCK + substep
            speed = crop_margin(speed_wide, offset)
            region = crop_margin(inside, offset)
            record_plane = crop_margin(planes[:, moment, :], offset)
            spot_plane = crop_margin(source_spot, offset)
            source_centre = crop_margin(source_wide, 4)
            receiver_centre = crop_margin(receiver_wide, 4)
            source_new = region * (
                2.0 * source_centre
                - source_back
                + speed
                * (
                    laplace(source_wide)
                    + (wavelet_row[moment] * spot_plane)[:, :, None] * source_layer
                )
            )
            receiver_new = region * (
                2.0 * receiver_centre
                - receiver_back
                + speed * (laplace(receiver_wide) + record_plane[:, :, None] * receiver_layer)
            )
            correlation = correlation + crop_margin(source_new, margin) * crop_margin(
                receiver_new, margin
            )
            source_wide, receiver_wide = (source_new, receiver_new)
            if margin > 0:
                source_back = crop_margin(source_centre, 4)
                receiver_back = crop_margin(receiver_centre, 4)
            else:
                source_back = source_centre
                receiver_back = receiver_centre
        source_field, source_prior = (source_wide, source_back)
        receiver_field, receiver_prior = (receiver_wide, receiver_back)
    image_part = lax.psum_scatter(correlation, "sa", scatter_dimension=0, tiled=True) / STEPS
    return (
        source_field[None],
        source_prior[None],
        receiver_field[None],
        receiver_prior[None],
        image_part,
    )


def any_body(mesh):
    fast = fast_body(mesh)

    def run(*args):
        nx, ny, nz = args[4].shape
        fits = mesh.shape["gy"] == 2 and mesh.shape["sa"] == 2 and nz == LANES
        fits = fits and (ny + HALO) == RADIUS * SUB and nx % (2 * CHUNK) == 0
        return (fast if fits else general_body)(*args)

    return run


def solution(mesh):
    in_specs = (
        P(("groups", "sa"), "gx", "gy", None),
        P(("groups", "sa"), "gx", "gy", None),
        P(("groups", "sa"), "gx", "gy", None),
        P(("groups", "sa"), "gx", "gy", None),
        P("gx", "gy", None),
        P(("groups", "sa"), None),
        P(("groups", "sa"), None, None),
        P(("groups", "sa")),
        P(("groups", "sa")),
        P(("groups", "sa"), None),
        P(("groups", "sa"), None),
    )
    out_specs = (
        P(("groups", "sa"), "gx", "gy", None),
        P(("groups", "sa"), "gx", "gy", None),
        P(("groups", "sa"), "gx", "gy", None),
        P(("groups", "sa"), "gx", "gy", None),
        P(("groups", "gx", "sa"), "gy", None),
    )
    return jax.shard_map(any_body(mesh), mesh=mesh, in_specs=in_specs, out_specs=out_specs, check_vma=False)
```

profile of v0, /device:TPU:0, one launch (start us, length us, event | category | flops | bytes accessed | tf_op | source)
XLA Modules:
  0.0 125.3 jit_solution(17575243673385865897)
XLA Ops:
  0.6 1.0 copy-done
  1.6 1.0 copy-done.1
  2.6 1.0 copy-done.2
  3.6 1.0 copy-done.3
  4.6 1.0 copy-done.4
  5.6 1.2 shard_map.146
  6.8 0.0 copy-start.8
  6.8 3.0 %collective-permute-start = (f32[112,8,128]{2,1,0:T(8,128)S(1)}, f32[112,8,128]{2,1,0:T(8,128)S(1)}, u32[]{:S(2)}, u32[]{:S(2)}) collective-permute-start(f32[112,8,128]{2,1,0:T(8,128)S(1)} %get-tuple-element.88), channel_id=1, source_target_pairs={{0,2},{1,3},{2,0},{3,1},{4,6},{5,7},{6,4},{7,5},{8,10},{9,11},{10,... | collective-permute-start | bytes 1376264 | tf_op jit(solution)/shard_map/ppermute | solution.py:445
  9.8 1.6 %collective-permute-start.1 = (f32[28,24,128]{2,1,0:T(8,128)S(1)}, f32[28,24,128]{2,1,0:T(8,128)S(1)}, u32[]{:S(2)}, u32[]{:S(2)}) collective-permute-start(f32[28,24,128]{2,1,0:T(8,128)S(1)} %get-tuple-element.89), channel_id=1, source_target_pairs={{0,4},{1,5},{2,6},{3,7},{4,0},{5,1},{6,2},{7,3},{8,12},{9,13},{10,... | collective-permute-start | bytes 1032200 | tf_op jit(solution)/shard_map/ppermute | solution.py:445
  11.4 3.1 %collective-permute-start.3 = (f32[4,8,128]{2,1,0:T(8,128)S(1)}, f32[4,8,128]{2,1,0:T(8,128)S(1)}, u32[]{:S(2)}, u32[]{:S(2)}) collective-permute-start(f32[4,8,128]{2,1,0:T(8,128)S(1)} %get-tuple-element.91), channel_id=1, source_target_pairs={{0,6},{1,7},{2,4},{3,5},{4,2},{5,3},{6,0},{7,1},{8,14},{9,15},{10,... | collective-permute-start | bytes 49160 | tf_op jit(solution)/shard_map/ppermute | solution.py:445
  15.8 0.0 copy-start.6
  15.9 0.0 copy-start.7
  15.9 0.6 copy-done.6
  16.5 0.0 copy-done.7
  16.5 3.2 %shard_map.147.refs_6_ = f32[48,32,128]{2,1,0:T(8,128)S(1)} custom-call(s32[1,64]{1,0:T(1,128)S(1)} %copy-done.6, s32[1,64]{1,0:T(1,128)S(1)} %copy-done.7, f32[1,12,64]{2,1,0:T(8,128)S(1)} %copy.51.traces), custom_call_target="tpu_custom_call" | custom-call | tf_op jit(solution)/shard_map/pallas_call | solution.py:85
  19.8 0.9 collective-permute-done.refs_7_
  20.7 0.7 copy-done.5
  21.4 10.3 %shard_map.148 = (f32[48,32,128]{2,1,0:T(8,128)S(1)}, f32[48,32,128]{2,1,0:T(8,128)S(1)}, f32[48,32,128]{2,1,0:T(8,128)S(1)}, f32[48,32,128]{2,1,0:T(8,128)S(1)}...) custom-call(f32[48,32,128]{2,1,0:T(8,128)S(1)} %get-tuple-element.82, ...), custom_call_target="tpu_custom_call", output_to_operand_aliasing={{0}: (0, {}), {1}: (1, {}), {2}: (2, {}), {3}: (3, {}), {4}... | custom-call | tf_op jit(solution)/shard_map/pallas_call | solution.py:85
  31.7 1.8 %collective-permute-start.5 = (f32[64,8,128]{2,1,0:T(8,128)S(1)}, f32[64,8,128]{2,1,0:T(8,128)S(1)}, u32[]{:S(2)}, u32[]{:S(2)}) collective-permute-start(f32[64,8,128]{2,1,0:T(8,128)S(1)} %get-tuple-element.99), channel_id=1, source_target_pairs={{0,2},{1,3},{2,0},{3,1},{4,6},{5,7},{6,4},{7,5},{8,10},{9,11},{10,... | collective-permute-start | bytes 786440 | tf_op jit(solution)/shard_map/ppermute | solution.py:445
  33.5 2.0 %collective-permute-start.6 = (f32[16,24,128]{2,1,0:T(8,128)S(1)}, f32[16,24,128]{2,1,0:T(8,128)S(1)}, u32[]{:S(2)}, u32[]{:S(2)}) collective-permute-start(f32[16,24,128]{2,1,0:T(8,128)S(1)} %get-tuple-element.100), channel_id=1, source_target_pairs={{0,4},{1,5},{2,6},{3,7},{4,0},{5,1},{6,2},{7,3},{8,12},{9,13},{10,... | collective-permute-start | bytes 589832 | tf_op jit(solution)/shard_map/ppermute | solution.py:445
  35.5 2.7 %collective-permute-start.8 = (f32[4,8,128]{2,1,0:T(8,128)S(1)}, f32[4,8,128]{2,1,0:T(8,128)S(1)}, u32[]{:S(2)}, u32[]{:S(2)}) collective-permute-start(f32[4,8,128]{2,1,0:T(8,128)S(1)} %get-tuple-element.102), channel_id=1, source_target_pairs={{0,6},{1,7},{2,4},{3,5},{4,2},{5,3},{6,0},{7,1},{8,14},{9,15},{10,... | collective-permute-start | bytes 49160 | tf_op jit(solution)/shard_map/ppermute | solution.py:445
  38.2 2.0 %collective-permute-done.8.refs_11_ = f32[4,8,128]{2,1,0:T(8,128)S(1)} collective-permute-done((f32[4,8,128]{2,1,0:T(8,128)S(1)}, f32[4,8,128]{2,1,0:T(8,128)S(1)}, u32[]{:S(2)}, u32[]{:S(2)}) %collective-permute-start.8) | collective-permute-done | bytes 16416 | tf_op jit(solution)/shard_map/ppermute | solution.py:445
  40.2 8.6 %shard_map.149 = (f32[48,32,128]{2,1,0:T(8,128)S(1)}, f32[48,32,128]{2,1,0:T(8,128)S(1)}, f32[48,32,128]{2,1,0:T(8,128)S(1)}, f32[48,32,128]{2,1,0:T(8,128)S(1)}...) custom-call(f32[48,32,128]{2,1,0:T(8,128)S(1)} %get-tuple-element.93, ...), custom_call_target="tpu_custom_call", output_to_operand_aliasing={{0}: (0, {}), {1}: (1, {}), {2}: (2, {}), {3}: (3, {}), {4}... | custom-call | tf_op jit(solution)/shard_map/pallas_call | solution.py:85
  48.8 1.3 %collective-permute-start.10 = (f32[64,8,128]{2,1,0:T(8,128)S(1)}, f32[64,8,128]{2,1,0:T(8,128)S(1)}, u32[]{:S(2)}, u32[]{:S(2)}) collective-permute-start(f32[64,8,128]{2,1,0:T(8,128)S(1)} %get-tuple-element.110), channel_id=1, source_target_pairs={{0,2},{1,3},{2,0},{3,1},{4,6},{5,7},{6,4},{7,5},{8,10},{9,11},{10,... | collective-permute-start | bytes 786440 | tf_op jit(solution)/shard_map/ppermute | solution.py:445
  50.1 2.3 %collective-permute-start.11 = (f32[16,24,128]{2,1,0:T(8,128)S(1)}, f32[16,24,128]{2,1,0:T(8,128)S(1)}, u32[]{:S(2)}, u32[]{:S(2)}) collective-permute-start(f32[16,24,128]{2,1,0:T(8,128)S(1)} %get-tuple-element.111), channel_id=1, source_target_pairs={{0,4},{1,5},{2,6},{3,7},{4,0},{5,1},{6,2},{7,3},{8,12},{9,13},{10,... | collective-permute-start | bytes 589832 | tf_op jit(solution)/shard_map/ppermute | solution.py:445
  52.5 2.0 %collective-permute-start.13 = (f32[4,8,128]{2,1,0:T(8,128)S(1)}, f32[4,8,128]{2,1,0:T(8,128)S(1)}, u32[]{:S(2)}, u32[]{:S(2)}) collective-permute-start(f32[4,8,128]{2,1,0:T(8,128)S(1)} %get-tuple-element.113), channel_id=1, source_target_pairs={{0,6},{1,7},{2,4},{3,5},{4,2},{5,3},{6,0},{7,1},{8,14},{9,15},{10,... | collective-permute-start | bytes 49160 | tf_op jit(solution)/shard_map/ppermute | solution.py:445
  54.5 2.8 %collective-permute-done.13.refs_11_ = f32[4,8,128]{2,1,0:T(8,128)S(1)} collective-permute-done((f32[4,8,128]{2,1,0:T(8,128)S(1)}, f32[4,8,128]{2,1,0:T(8,128)S(1)}, u32[]{:S(2)}, u32[]{:S(2)}) %collective-permute-start.13) | collective-permute-done | bytes 16416 | tf_op jit(solution)/shard_map/ppermute | solution.py:445
  57.3 10.2 %shard_map.150 = (f32[48,32,128]{2,1,0:T(8,128)S(1)}, f32[48,32,128]{2,1,0:T(8,128)S(1)}, f32[48,32,128]{2,1,0:T(8,128)S(1)}, f32[48,32,128]{2,1,0:T(8,128)S(1)}...) custom-call(f32[48,32,128]{2,1,0:T(8,128)S(1)} %get-tuple-element.10, ...), custom_call_target="tpu_custom_call", output_to_operand_aliasing={{0}: (0, {}), {1}: (1, {}), {2}: (2, {}), {3}: (3, {}), {4}... | custom-call | tf_op jit(solution)/shard_map/pallas_call | solution.py:85
  67.5 1.3 %collective-permute-start.15 = (f32[64,8,128]{2,1,0:T(8,128)S(1)}, f32[64,8,128]{2,1,0:T(8,128)S(1)}, u32[]{:S(2)}, u32[]{:S(2)}) collective-permute-start(f32[64,8,128]{2,1,0:T(8,128)S(1)} %get-tuple-element.121), channel_id=1, source_target_pairs={{0,2},{1,3},{2,0},{3,1},{4,6},{5,7},{6,4},{7,5},{8,10},{9,11},{10,... | collective-permute-start | bytes 786440 | tf_op jit(solution)/shard_map/ppermute | solution.py:445
  68.8 2.2 %collective-permute-start.16 = (f32[16,24,128]{2,1,0:T(8,128)S(1)}, f32[16,24,128]{2,1,0:T(8,128)S(1)}, u32[]{:S(2)}, u32[]{:S(2)}) collective-permute-start(f32[16,24,128]{2,1,0:T(8,128)S(1)} %get-tuple-element.122), channel_id=1, source_target_pairs={{0,4},{1,5},{2,6},{3,7},{4,0},{5,1},{6,2},{7,3},{8,12},{9,13},{10,... | collective-permute-start | bytes 589832 | tf_op jit(solution)/shard_map/ppermute | solution.py:445
  70.9 2.0 %collective-permute-start.18 = (f32[4,8,128]{2,1,0:T(8,128)S(1)}, f32[4,8,128]{2,1,0:T(8,128)S(1)}, u32[]{:S(2)}, u32[]{:S(2)}) collective-permute-start(f32[4,8,128]{2,1,0:T(8,128)S(1)} %get-tuple-element.124), channel_id=1, source_target_pairs={{0,6},{1,7},{2,4},{3,5},{4,2},{5,3},{6,0},{7,1},{8,14},{9,15},{10,... | collective-permute-start | bytes 49160 | tf_op jit(solution)/shard_map/ppermute | solution.py:445
  73.0 3.2 %collective-permute-done.18.refs_11_ = f32[4,8,128]{2,1,0:T(8,128)S(1)} collective-permute-done((f32[4,8,128]{2,1,0:T(8,128)S(1)}, f32[4,8,128]{2,1,0:T(8,128)S(1)}, u32[]{:S(2)}, u32[]{:S(2)}) %collective-permute-start.18) | collective-permute-done | bytes 16416 | tf_op jit(solution)/shard_map/ppermute | solution.py:445
  76.2 10.2 %shard_map.151 = (f32[48,32,128]{2,1,0:T(8,128)S(1)}, f32[48,32,128]{2,1,0:T(8,128)S(1)}, f32[48,32,128]{2,1,0:T(8,128)S(1)}, f32[48,32,128]{2,1,0:T(8,128)S(1)}...) custom-call(f32[48,32,128]{2,1,0:T(8,128)S(1)} %get-tuple-element.11, ...), custom_call_target="tpu_custom_call", output_to_operand_aliasing={{0}: (0, {}), {1}: (1, {}), {2}: (2, {}), {3}: (3, {}), {4}... | custom-call | tf_op jit(solution)/shard_map/pallas_call | solution.py:85
  86.5 0.8 collective-permute-start.20
  87.3 2.3 %collective-permute-start.21 = (f32[16,24,128]{2,1,0:T(8,128)S(1)}, f32[16,24,128]{2,1,0:T(8,128)S(1)}, u32[]{:S(2)}, u32[]{:S(2)}) collective-permute-start(f32[16,24,128]{2,1,0:T(8,128)S(1)} %get-tuple-element.133), channel_id=1, source_target_pairs={{0,4},{1,5},{2,6},{3,7},{4,0},{5,1},{6,2},{7,3},{8,12},{9,13},{10,... | collective-permute-start | bytes 589832 | tf_op jit(solution)/shard_map/ppermute | solution.py:445
  89.6 1.9 %collective-permute-start.23 = (f32[4,8,128]{2,1,0:T(8,128)S(1)}, f32[4,8,128]{2,1,0:T(8,128)S(1)}, u32[]{:S(2)}, u32[]{:S(2)}) collective-permute-start(f32[4,8,128]{2,1,0:T(8,128)S(1)} %get-tuple-element.135), channel_id=1, source_target_pairs={{0,6},{1,7},{2,4},{3,5},{4,2},{5,3},{6,0},{7,1},{8,14},{9,15},{10,... | collective-permute-start | bytes 49160 | tf_op jit(solution)/shard_map/ppermute | solution.py:445
  91.5 3.4 %collective-permute-done.23.refs_11_ = f32[4,8,128]{2,1,0:T(8,128)S(1)} collective-permute-done((f32[4,8,128]{2,1,0:T(8,128)S(1)}, f32[4,8,128]{2,1,0:T(8,128)S(1)}, u32[]{:S(2)}, u32[]{:S(2)}) %collective-permute-start.23) | collective-permute-done | bytes 16416 | tf_op jit(solution)/shard_map/ppermute | solution.py:445
  94.9 10.2 %shard_map.152 = (f32[48,32,128]{2,1,0:T(8,128)S(1)}, f32[48,32,128]{2,1,0:T(8,128)S(1)}, f32[48,32,128]{2,1,0:T(8,128)S(1)}, f32[48,32,128]{2,1,0:T(8,128)S(1)}...) custom-call(f32[48,32,128]{2,1,0:T(8,128)S(1)} %get-tuple-element.12, ...), custom_call_target="tpu_custom_call", output_to_operand_aliasing={{0}: (0, {}), {1}: (1, {}), {2}: (2, {}), {3}: (3, {}), {4}... | custom-call | tf_op jit(solution)/shard_map/pallas_call | solution.py:85
  105.1 0.7 collective-permute-start.25
  105.8 2.2 %collective-permute-start.26 = (f32[16,24,128]{2,1,0:T(8,128)S(1)}, f32[16,24,128]{2,1,0:T(8,128)S(1)}, u32[]{:S(2)}, u32[]{:S(2)}) collective-permute-start(f32[16,24,128]{2,1,0:T(8,128)S(1)} %get-tuple-element.144), channel_id=1, source_target_pairs={{0,4},{1,5},{2,6},{3,7},{4,0},{5,1},{6,2},{7,3},{8,12},{9,13},{10,... | collective-permute-start | bytes 589832 | tf_op jit(solution)/shard_map/ppermute | solution.py:445
  108.1 2.1 %collective-permute-start.28 = (f32[4,8,128]{2,1,0:T(8,128)S(1)}, f32[4,8,128]{2,1,0:T(8,128)S(1)}, u32[]{:S(2)}, u32[]{:S(2)}) collective-permute-start(f32[4,8,128]{2,1,0:T(8,128)S(1)} %get-tuple-element.146), channel_id=1, source_target_pairs={{0,6},{1,7},{2,4},{3,5},{4,2},{5,3},{6,0},{7,1},{8,14},{9,15},{10,... | collective-permute-start | bytes 49160 | tf_op jit(solution)/shard_map/ppermute | solution.py:445
  110.2 3.1 %collective-permute-done.28.refs_11_ = f32[4,8,128]{2,1,0:T(8,128)S(1)} collective-permute-done((f32[4,8,128]{2,1,0:T(8,128)S(1)}, f32[4,8,128]{2,1,0:T(8,128)S(1)}, u32[]{:S(2)}, u32[]{:S(2)}) %collective-permute-start.28) | collective-permute-done | bytes 16416 | tf_op jit(solution)/shard_map/ppermute | solution.py:445
  113.2 9.7 %shard_map.153 = (f32[48,32,128]{2,1,0:T(8,128)S(1)}, f32[48,32,128]{2,1,0:T(8,128)S(1)}, f32[48,32,128]{2,1,0:T(8,128)S(1)}, f32[48,32,128]{2,1,0:T(8,128)S(1)}...) custom-call(f32[48,32,128]{2,1,0:T(8,128)S(1)} %get-tuple-element.13, ...), custom_call_target="tpu_custom_call", output_to_operand_aliasing={{0}: (0, {}), {1}: (1, {}), {2}: (2, {}), {3}: (3, {}), {4}... | custom-call | tf_op jit(solution)/shard_map/pallas_call | solution.py:85
  123.0 0.1 shard_map.155
  123.1 0.1 collective-permute-start.30
  123.2 1.2 shard_map.154
  124.5 0.2 collective-permute-done.30
  124.6 0.7 add_multiply_fusion
  (44 shorter events, 0.1 us)
Async XLA Ops:
  0.6 1.0 copy-start
  1.6 1.0 copy-start.1
  2.6 1.0 copy-start.2
  3.6 1.0 copy-start.3
  4.6 1.0 copy-start.4
  6.8 9.1 %copy-start.8 = (f32[1,12,64]{2,0,1:T(1,128)S(1)}, f32[1,12,64]{2,0,1:T(1,128)}, u32[]{:S(2)}) copy-start(f32[1,12,64]{2,0,1:T(1,128)} %param.17) | copy-start | bytes 9220
  6.8 13.9 %collective-permute-start = (f32[112,8,128]{2,1,0:T(8,128)S(1)}, f32[112,8,128]{2,1,0:T(8,128)S(1)}, u32[]{:S(2)}, u32[]{:S(2)}) collective-permute-start(f32[112,8,128]{2,1,0:T(8,128)S(1)} %get-tuple-element.88), channel_id=1, source_target_pairs={{0,2},{1,3},{2,0},{3,1},{4,6},{5,7},{6,4},{7,5},{8,10},{9,11},{10,... | collective-permute-start | bytes 1376264 | tf_op jit(solution)/shard_map/ppermute | solution.py:445
  9.8 9.9 %collective-permute-start.1 = (f32[28,24,128]{2,1,0:T(8,128)S(1)}, f32[28,24,128]{2,1,0:T(8,128)S(1)}, u32[]{:S(2)}, u32[]{:S(2)}) collective-permute-start(f32[28,24,128]{2,1,0:T(8,128)S(1)} %get-tuple-element.89), channel_id=1, source_target_pairs={{0,4},{1,5},{2,6},{3,7},{4,0},{5,1},{6,2},{7,3},{8,12},{9,13},{10,... | collective-permute-start | bytes 1032200 | tf_op jit(solution)/shard_map/ppermute | solution.py:445
  11.4 8.3 %collective-permute-start.2 = (f32[28,24,128]{2,1,0:T(8,128)S(1)}, f32[28,24,128]{2,1,0:T(8,128)S(1)}, u32[]{:S(2)}, u32[]{:S(2)}) collective-permute-start(f32[28,24,128]{2,1,0:T(8,128)S(1)} %get-tuple-element.90), channel_id=1, source_target_pairs={{0,1},{1,0},{2,3},{3,2},{4,8},{5,9},{6,10},{7,11},{8,4},{9,5},{10,... | collective-permute-start | bytes 1032200 | tf_op jit(solution)/shard_map/ppermute | solution.py:445
  11.4 8.3 %collective-permute-start.3 = (f32[4,8,128]{2,1,0:T(8,128)S(1)}, f32[4,8,128]{2,1,0:T(8,128)S(1)}, u32[]{:S(2)}, u32[]{:S(2)}) collective-permute-start(f32[4,8,128]{2,1,0:T(8,128)S(1)} %get-tuple-element.91), channel_id=1, source_target_pairs={{0,6},{1,7},{2,4},{3,5},{4,2},{5,3},{6,0},{7,1},{8,14},{9,15},{10,... | collective-permute-start | bytes 49160 | tf_op jit(solution)/shard_map/ppermute | solution.py:445
  14.5 5.2 %collective-permute-start.4 = (f32[4,8,128]{2,1,0:T(8,128)S(1)}, f32[4,8,128]{2,1,0:T(8,128)S(1)}, u32[]{:S(2)}, u32[]{:S(2)}) collective-permute-start(f32[4,8,128]{2,1,0:T(8,128)S(1)} %get-tuple-element.92), channel_id=1, source_target_pairs={{0,1},{1,0},{2,3},{3,2},{4,10},{5,11},{6,8},{7,9},{8,6},{9,7},{10,... | collective-permute-start | bytes 49160 | tf_op jit(solution)/shard_map/ppermute | solution.py:445
  15.8 0.7 copy-start.6
  15.9 0.7 copy-start.7
  20.7 0.7 copy-start.5
  31.7 8.5 %collective-permute-start.5 = (f32[64,8,128]{2,1,0:T(8,128)S(1)}, f32[64,8,128]{2,1,0:T(8,128)S(1)}, u32[]{:S(2)}, u32[]{:S(2)}) collective-permute-start(f32[64,8,128]{2,1,0:T(8,128)S(1)} %get-tuple-element.99), channel_id=1, source_target_pairs={{0,2},{1,3},{2,0},{3,1},{4,6},{5,7},{6,4},{7,5},{8,10},{9,11},{10,... | collective-permute-start | bytes 786440 | tf_op jit(solution)/shard_map/ppermute | solution.py:445
  33.5 6.7 %collective-permute-start.6 = (f32[16,24,128]{2,1,0:T(8,128)S(1)}, f32[16,24,128]{2,1,0:T(8,128)S(1)}, u32[]{:S(2)}, u32[]{:S(2)}) collective-permute-start(f32[16,24,128]{2,1,0:T(8,128)S(1)} %get-tuple-element.100), channel_id=1, source_target_pairs={{0,4},{1,5},{2,6},{3,7},{4,0},{5,1},{6,2},{7,3},{8,12},{9,13},{10,... | collective-permute-start | bytes 589832 | tf_op jit(solution)/shard_map/ppermute | solution.py:445
  35.5 4.7 %collective-permute-start.7 = (f32[16,24,128]{2,1,0:T(8,128)S(1)}, f32[16,24,128]{2,1,0:T(8,128)S(1)}, u32[]{:S(2)}, u32[]{:S(2)}) collective-permute-start(f32[16,24,128]{2,1,0:T(8,128)S(1)} %get-tuple-element.101), channel_id=1, source_target_pairs={{0,1},{1,0},{2,3},{3,2},{4,8},{5,9},{6,10},{7,11},{8,4},{9,5},{10,... | collective-permute-start | bytes 589832 | tf_op jit(solution)/shard_map/ppermute | solution.py:445
  35.5 4.6 %collective-permute-start.8 = (f32[4,8,128]{2,1,0:T(8,128)S(1)}, f32[4,8,128]{2,1,0:T(8,128)S(1)}, u32[]{:S(2)}, u32[]{:S(2)}) collective-permute-start(f32[4,8,128]{2,1,0:T(8,128)S(1)} %get-tuple-element.102), channel_id=1, source_target_pairs={{0,6},{1,7},{2,4},{3,5},{4,2},{5,3},{6,0},{7,1},{8,14},{9,15},{10,... | collective-permute-start | bytes 49160 | tf_op jit(solution)/shard_map/ppermute | solution.py:445
  38.2 2.0 %collective-permute-start.9 = (f32[4,8,128]{2,1,0:T(8,128)S(1)}, f32[4,8,128]{2,1,0:T(8,128)S(1)}, u32[]{:S(2)}, u32[]{:S(2)}) collective-permute-start(f32[4,8,128]{2,1,0:T(8,128)S(1)} %get-tuple-element.103), channel_id=1, source_target_pairs={{0,1},{1,0},{2,3},{3,2},{4,10},{5,11},{6,8},{7,9},{8,6},{9,7},{10,... | collective-permute-start | bytes 49160 | tf_op jit(solution)/shard_map/ppermute | solution.py:445
  48.8 8.5 %collective-permute-start.10 = (f32[64,8,128]{2,1,0:T(8,128)S(1)}, f32[64,8,128]{2,1,0:T(8,128)S(1)}, u32[]{:S(2)}, u32[]{:S(2)}) collective-permute-start(f32[64,8,128]{2,1,0:T(8,128)S(1)} %get-tuple-element.110), channel_id=1, source_target_pairs={{0,2},{1,3},{2,0},{3,1},{4,6},{5,7},{6,4},{7,5},{8,10},{9,11},{10,... | collective-permute-start | bytes 786440 | tf_op jit(solution)/shard_map/ppermute | solution.py:445
  50.1 7.2 %collective-permute-start.11 = (f32[16,24,128]{2,1,0:T(8,128)S(1)}, f32[16,24,128]{2,1,0:T(8,128)S(1)}, u32[]{:S(2)}, u32[]{:S(2)}) collective-permute-start(f32[16,24,128]{2,1,0:T(8,128)S(1)} %get-tuple-element.111), channel_id=1, source_target_pairs={{0,4},{1,5},{2,6},{3,7},{4,0},{5,1},{6,2},{7,3},{8,12},{9,13},{10,... | collective-permute-start | bytes 589832 | tf_op jit(solution)/shard_map/ppermute | solution.py:445
  52.4 4.8 %collective-permute-start.12 = (f32[16,24,128]{2,1,0:T(8,128)S(1)}, f32[16,24,128]{2,1,0:T(8,128)S(1)}, u32[]{:S(2)}, u32[]{:S(2)}) collective-permute-start(f32[16,24,128]{2,1,0:T(8,128)S(1)} %get-tuple-element.112), channel_id=1, source_target_pairs={{0,1},{1,0},{2,3},{3,2},{4,8},{5,9},{6,10},{7,11},{8,4},{9,5},{10,... | collective-permute-start | bytes 589832 | tf_op jit(solution)/shard_map/ppermute | solution.py:445
  52.5 4.8 %collective-permute-start.13 = (f32[4,8,128]{2,1,0:T(8,128)S(1)}, f32[4,8,128]{2,1,0:T(8,128)S(1)}, u32[]{:S(2)}, u32[]{:S(2)}) collective-permute-start(f32[4,8,128]{2,1,0:T(8,128)S(1)} %get-tuple-element.113), channel_id=1, source_target_pairs={{0,6},{1,7},{2,4},{3,5},{4,2},{5,3},{6,0},{7,1},{8,14},{9,15},{10,... | collective-permute-start | bytes 49160 | tf_op jit(solution)/shard_map/ppermute | solution.py:445
  54.5 2.8 %collective-permute-start.14 = (f32[4,8,128]{2,1,0:T(8,128)S(1)}, f32[4,8,128]{2,1,0:T(8,128)S(1)}, u32[]{:S(2)}, u32[]{:S(2)}) collective-permute-start(f32[4,8,128]{2,1,0:T(8,128)S(1)} %get-tuple-element.114), channel_id=1, source_target_pairs={{0,1},{1,0},{2,3},{3,2},{4,10},{5,11},{6,8},{7,9},{8,6},{9,7},{10,... | collective-permute-start | bytes 49160 | tf_op jit(solution)/shard_map/ppermute | solution.py:445
  67.5 8.7 %collective-permute-start.15 = (f32[64,8,128]{2,1,0:T(8,128)S(1)}, f32[64,8,128]{2,1,0:T(8,128)S(1)}, u32[]{:S(2)}, u32[]{:S(2)}) collective-permute-start(f32[64,8,128]{2,1,0:T(8,128)S(1)} %get-tuple-element.121), channel_id=1, source_target_pairs={{0,2},{1,3},{2,0},{3,1},{4,6},{5,7},{6,4},{7,5},{8,10},{9,11},{10,... | collective-permute-start | bytes 786440 | tf_op jit(solution)/shard_map/ppermute | solution.py:445
  68.8 7.4 %collective-permute-start.16 = (f32[16,24,128]{2,1,0:T(8,128)S(1)}, f32[16,24,128]{2,1,0:T(8,128)S(1)}, u32[]{:S(2)}, u32[]{:S(2)}) collective-permute-start(f32[16,24,128]{2,1,0:T(8,128)S(1)} %get-tuple-element.122), channel_id=1, source_target_pairs={{0,4},{1,5},{2,6},{3,7},{4,0},{5,1},{6,2},{7,3},{8,12},{9,13},{10,... | collective-permute-start | bytes 589832 | tf_op jit(solution)/shard_map/ppermute | solution.py:445
  70.9 5.3 %collective-permute-start.17 = (f32[16,24,128]{2,1,0:T(8,128)S(1)}, f32[16,24,128]{2,1,0:T(8,128)S(1)}, u32[]{:S(2)}, u32[]{:S(2)}) collective-permute-start(f32[16,24,128]{2,1,0:T(8,128)S(1)} %get-tuple-element.123), channel_id=1, source_target_pairs={{0,1},{1,0},{2,3},{3,2},{4,8},{5,9},{6,10},{7,11},{8,4},{9,5},{10,... | collective-permute-start | bytes 589832 | tf_op jit(solution)/shard_map/ppermute | solution.py:445
  70.9 5.3 %collective-permute-start.18 = (f32[4,8,128]{2,1,0:T(8,128)S(1)}, f32[4,8,128]{2,1,0:T(8,128)S(1)}, u32[]{:S(2)}, u32[]{:S(2)}) collective-permute-start(f32[4,8,128]{2,1,0:T(8,128)S(1)} %get-tuple-element.124), channel_id=1, source_target_pairs={{0,6},{1,7},{2,4},{3,5},{4,2},{5,3},{6,0},{7,1},{8,14},{9,15},{10,... | collective-permute-start | bytes 49160 | tf_op jit(solution)/shard_map/ppermute | solution.py:445
  73.0 3.2 %collective-permute-start.19 = (f32[4,8,128]{2,1,0:T(8,128)S(1)}, f32[4,8,128]{2,1,0:T(8,128)S(1)}, u32[]{:S(2)}, u32[]{:S(2)}) collective-permute-start(f32[4,8,128]{2,1,0:T(8,128)S(1)} %get-tuple-element.125), channel_id=1, source_target_pairs={{0,1},{1,0},{2,3},{3,2},{4,10},{5,11},{6,8},{7,9},{8,6},{9,7},{10,... | collective-permute-start | bytes 49160 | tf_op jit(solution)/shard_map/ppermute | solution.py:445
  86.5 8.4 %collective-permute-start.20 = (f32[64,8,128]{2,1,0:T(8,128)S(1)}, f32[64,8,128]{2,1,0:T(8,128)S(1)}, u32[]{:S(2)}, u32[]{:S(2)}) collective-permute-start(f32[64,8,128]{2,1,0:T(8,128)S(1)} %get-tuple-element.132), channel_id=1, source_target_pairs={{0,2},{1,3},{2,0},{3,1},{4,6},{5,7},{6,4},{7,5},{8,10},{9,11},{10,... | collective-permute-start | bytes 786440 | tf_op jit(solution)/shard_map/ppermute | solution.py:445
  87.3 7.6 %collective-permute-start.21 = (f32[16,24,128]{2,1,0:T(8,128)S(1)}, f32[16,24,128]{2,1,0:T(8,128)S(1)}, u32[]{:S(2)}, u32[]{:S(2)}) collective-permute-start(f32[16,24,128]{2,1,0:T(8,128)S(1)} %get-tuple-element.133), channel_id=1, source_target_pairs={{0,4},{1,5},{2,6},{3,7},{4,0},{5,1},{6,2},{7,3},{8,12},{9,13},{10,... | collective-permute-start | bytes 589832 | tf_op jit(solution)/shard_map/ppermute | solution.py:445
  89.6 5.3 %collective-permute-start.22 = (f32[16,24,128]{2,1,0:T(8,128)S(1)}, f32[16,24,128]{2,1,0:T(8,128)S(1)}, u32[]{:S(2)}, u32[]{:S(2)}) collective-permute-start(f32[16,24,128]{2,1,0:T(8,128)S(1)} %get-tuple-element.134), channel_id=1, source_target_pairs={{0,1},{1,0},{2,3},{3,2},{4,8},{5,9},{6,10},{7,11},{8,4},{9,5},{10,... | collective-permute-start | bytes 589832 | tf_op jit(solution)/shard_map/ppermute | solution.py:445
  89.6 5.3 %collective-permute-start.23 = (f32[4,8,128]{2,1,0:T(8,128)S(1)}, f32[4,8,128]{2,1,0:T(8,128)S(1)}, u32[]{:S(2)}, u32[]{:S(2)}) collective-permute-start(f32[4,8,128]{2,1,0:T(8,128)S(1)} %get-tuple-element.135), channel_id=1, source_target_pairs={{0,6},{1,7},{2,4},{3,5},{4,2},{5,3},{6,0},{7,1},{8,14},{9,15},{10,... | collective-permute-start | bytes 49160 | tf_op jit(solution)/shard_map/ppermute | solution.py:445
  91.5 3.4 %collective-permute-start.24 = (f32[4,8,128]{2,1,0:T(8,128)S(1)}, f32[4,8,128]{2,1,0:T(8,128)S(1)}, u32[]{:S(2)}, u32[]{:S(2)}) collective-permute-start(f32[4,8,128]{2,1,0:T(8,128)S(1)} %get-tuple-element.136), channel_id=1, source_target_pairs={{0,1},{1,0},{2,3},{3,2},{4,10},{5,11},{6,8},{7,9},{8,6},{9,7},{10,... | collective-permute-start | bytes 49160 | tf_op jit(solution)/shard_map/ppermute | solution.py:445
  105.1 8.1 %collective-permute-start.25 = (f32[64,8,128]{2,1,0:T(8,128)S(1)}, f32[64,8,128]{2,1,0:T(8,128)S(1)}, u32[]{:S(2)}, u32[]{:S(2)}) collective-permute-start(f32[64,8,128]{2,1,0:T(8,128)S(1)} %get-tuple-element.143), channel_id=1, source_target_pairs={{0,2},{1,3},{2,0},{3,1},{4,6},{5,7},{6,4},{7,5},{8,10},{9,11},{10,... | collective-permute-start | bytes 786440 | tf_op jit(solution)/shard_map/ppermute | solution.py:445
  105.8 7.4 %collective-permute-start.26 = (f32[16,24,128]{2,1,0:T(8,128)S(1)}, f32[16,24,128]{2,1,0:T(8,128)S(1)}, u32[]{:S(2)}, u32[]{:S(2)}) collective-permute-start(f32[16,24,128]{2,1,0:T(8,128)S(1)} %get-tuple-element.144), channel_id=1, source_target_pairs={{0,4},{1,5},{2,6},{3,7},{4,0},{5,1},{6,2},{7,3},{8,12},{9,13},{10,... | collective-permute-start | bytes 589832 | tf_op jit(solution)/shard_map/ppermute | solution.py:445
  108.1 5.1 %collective-permute-start.27 = (f32[16,24,128]{2,1,0:T(8,128)S(1)}, f32[16,24,128]{2,1,0:T(8,128)S(1)}, u32[]{:S(2)}, u32[]{:S(2)}) collective-permute-start(f32[16,24,128]{2,1,0:T(8,128)S(1)} %get-tuple-element.145), channel_id=1, source_target_pairs={{0,1},{1,0},{2,3},{3,2},{4,8},{5,9},{6,10},{7,11},{8,4},{9,5},{10,... | collective-permute-start | bytes 589832 | tf_op jit(solution)/shard_map/ppermute | solution.py:445
  108.1 5.1 %collective-permute-start.28 = (f32[4,8,128]{2,1,0:T(8,128)S(1)}, f32[4,8,128]{2,1,0:T(8,128)S(1)}, u32[]{:S(2)}, u32[]{:S(2)}) collective-permute-start(f32[4,8,128]{2,1,0:T(8,128)S(1)} %get-tuple-element.146), channel_id=1, source_target_pairs={{0,6},{1,7},{2,4},{3,5},{4,2},{5,3},{6,0},{7,1},{8,14},{9,15},{10,... | collective-permute-start | bytes 49160 | tf_op jit(solution)/shard_map/ppermute | solution.py:445
  110.2 3.1 %collective-permute-start.29 = (f32[4,8,128]{2,1,0:T(8,128)S(1)}, f32[4,8,128]{2,1,0:T(8,128)S(1)}, u32[]{:S(2)}, u32[]{:S(2)}) collective-permute-start(f32[4,8,128]{2,1,0:T(8,128)S(1)} %get-tuple-element.147), channel_id=1, source_target_pairs={{0,1},{1,0},{2,3},{3,2},{4,10},{5,11},{6,8},{7,9},{8,6},{9,7},{10,... | collective-permute-start | bytes 49160 | tf_op jit(solution)/shard_map/ppermute | solution.py:445
  123.1 1.5 %collective-permute-start.30 = (f32[16,24,128]{2,1,0:T(8,128)S(1)}, f32[16,24,128]{2,1,0:T(8,128)S(1)}, u32[]{:S(2)}, u32[]{:S(2)}) collective-permute-start(f32[16,24,128]{2,1,0:T(8,128)S(1)} %get-tuple-element.158), channel_id=1, source_target_pairs={{0,1},{1,0},{2,3},{3,2},{4,5},{5,4},{6,7},{7,6},{8,9},{9,8},{10,11... | collective-permute-start | bytes 589832 | tf_op jit(solution)/shard_map/ppermute | solution.py:491
where the time goes:
time: 126 us; the launch traced here: 125 us
  Pallas kernels  65.1 us (52%)
  starting transfers between devices  35.6 us (28%)
  waiting for transfers between devices  15.6 us (12%)
  local copies, waits for them, and re-layouts  6.28 us (5%)
  between operations  2.17 us (2%)
    pallas_call x10, Pallas kernels, call(): pl.pallas_call(body, out_shape=out_shapes, in_specs=specs, out_specs=out_...  65.1 us
    ppermute x30, starting transfers between devices, run(): lax.ppermute(m, names, route)  35.5 us
    ppermute x30, waiting for transfers between devices, run(): lax.ppermute(m, names, route)  15.4 us
    unnamed x19, local copies, waits for them, and re-layouts  6.28 us
  transfers between devices with their start and end apart: 31, of which 7 were waited for; matrix products, arithmetic and copies ran while one was open for 0% of the time, Pallas kernels for 4%

commit v1 on v0

--- a/solution.py
+++ b/solution.py
@@ -16,14 +16,15 @@
 SUB = 8
 DEEP = 2
 HALO = RADIUS * DEEP
-CHUNK = 8
+GROUP = 8
+RATIOS = [c / COEFFS[1] for c in COEFFS]
 GENERAL_BLOCK = 4
 GENERAL_BLOCKS = 3
 VMEM_LIMIT = 24 << 20
 
 VM = pl.BlockSpec(memory_space=pltpu.VMEM)
 SM = pl.BlockSpec(memory_space=pltpu.SMEM)
-ANY = pl.BlockSpec(memory_space=pl.ANY)
+HBM = pl.BlockSpec(memory_space=pltpu.HBM)
 F32 = jnp.float32
 
 
@@ -212,13 +213,9 @@
         gap = jnp.abs(row - col)
         d = jnp.zeros((LANES, LANES), F32)
         for k in range(1, RADIUS + 1):
-            d = jnp.where(gap == k, COEFFS[k], d)
-        hi = d.astype(jnp.bfloat16)
-        lo = (d - hi.astype(F32)).astype(jnp.bfloat16)
-        dw[0:LANES, 0:LANES] = hi
-        dw[0:LANES, LANES : 2 * LANES] = lo
-        dw[LANES : 2 * LANES, 0:LANES] = hi
-        dw[LANES : 2 * LANES, LANES : 2 * LANES] = jnp.zeros_like(lo)
+            d = jnp.where(gap == k, RATIOS[k], d)
+        dw[0:LANES, :] = d.astype(jnp.bfloat16)
+        dw[LANES : 2 * LANES, :] = d.astype(jnp.bfloat16)
         zero = jnp.zeros((geo.win, LANES), F32)
         for f, u in enumerate(targets):
             for x in range(nx):
@@ -244,7 +241,7 @@
     rows_all = geo.xe * geo.win
     block = 128
 
-    def body(ri, rc, traces, out, table):
+    def body(ri, rc, traces, wavelet, out, wav, table):
         p, g, _ = geo.place()
         x = ri[...] - g * geo.nx + HALO
         w = rc[...] - p * geo.ny + SUB * p
@@ -253,7 +250,9 @@
         row = x * geo.win + (w & (geo.jn - 1)) * SUB + (w >> shift)
         row = jnp.where(ok, row, -1)
         table[...] = jnp.zeros_like(table)
-        table[0:STEPS, :] = traces[0]
+        table[0:STEPS, :] = traces[0] * (1.0 / COEFFS[1])
+        wav[...] = jnp.zeros_like(wav)
+        wav[0:1, 0:STEPS] = wavelet[...] * (1.0 / COEFFS[1])
         tab = table[...]
 
         def chunk(i, carry):
@@ -271,85 +270,60 @@
     return body
 
 
-def depth_part(geo, u, z, dw, first, count):
-    w = dw[...]
-
-    def chunk(i, carry):
-        at = first + i * CHUNK
-        rows = u[pl.ds(at, CHUNK)].reshape(CHUNK * geo.win, LANES)
-        hi = rows.astype(jnp.bfloat16)
-        lo = (rows - hi.astype(F32)).astype(jnp.bfloat16)
-        both = jnp.dot(jnp.concatenate([hi, lo], axis=1), w, preferred_element_type=F32)
-        z[pl.ds(at, CHUNK)] = (both[:, :LANES] + both[:, LANES:]).reshape(CHUNK, geo.win, LANES)
+def update_planes(geo, pairs, cc, ee, dw, x, moment, gg, corr, fresh):
+    jn, span = geo.jn, GROUP * geo.win
+    sub = lax.broadcasted_iota(jnp.int32, (SUB, LANES), 0)
+    at_depth = lax.broadcasted_iota(jnp.int32, (SUB, LANES), 1) == REC_DEPTH
+    first, last = sub == 0, sub == SUB - 1
+    rows = jnp.concatenate([u[pl.ds(x, GROUP)].reshape(span, LANES) for u, _ in pairs], axis=0)
+    hi = rows.astype(jnp.bfloat16)
+    lo = (rows - hi.astype(F32)).astype(jnp.bfloat16)
+    deep = jnp.dot(jnp.concatenate([hi, lo], axis=1), dw[...], preferred_element_type=F32)
+    for i in range(GROUP):
+        news = []
+        for f, (u, prior) in enumerate(pairs):
+            mid = [u[x + i, SUB * j : SUB * j + SUB, :] for j in range(jn)]
+            below = [jnp.where(first, 0.0, pltpu.roll(v, 1, 0)) for v in mid]
+            above = [jnp.where(last, 0.0, pltpu.roll(v, SUB - 1, 0)) for v in mid]
+            line = below + mid + above
+            for j in range(jn):
+                tile = slice(SUB * j, SUB * j + SUB)
+                at = f * span + i * geo.win + SUB * j
+                acc = deep[at : at + SUB]
+                if f == 1:
+                    fed = pltpu.roll(gg[x + i, tile, :], (REC_DEPTH - moment) % LANES, 1)
+                    acc = acc + jnp.where(at_depth, fed, 0.0)
+                for k in range(1, RADIUS + 1):
+                    near = (u[x + i + k, tile, :] + u[x + i - k, tile, :]) + (line[jn + j + k] + line[jn + j - k])
+                    acc = acc + (near if k == 1 else RATIOS[k] * near)
+                new = (ee[x + i, tile, :] * mid[j] - prior[x + i, tile, :]) + cc[x + i, tile, :] * acc
+                prior[x + i, tile, :] = new
+                news.append(new)
+        for j in range(jn):
+            tile = slice(SUB * j, SUB * j + SUB)
+            product = news[j] * news[jn + j]
+            if not fresh:
+                product = product + corr[x + i - HALO + RADIUS, tile, :]
+            corr[x + i - HALO + RADIUS, tile, :] = product
+
+
+def one_step(geo, moment, us, ur, ps, pr, cc, ee, gg, corr, dw, wav, src, first, count, fresh):
+    def group(i, carry):
+        x = first + i * GROUP
+        update_planes(geo, ((us, ps), (ur, pr)), cc, ee, dw, x, moment, gg, corr, fresh)
         return carry
 
-    lax.fori_loop(0, count // CHUNK, chunk, 0)
-
-
-def update_plane(geo, u, prior, cc, z, x, sub, extra):
-    jn = geo.jn
-    mid = [u[x, SUB * j : SUB * j + SUB, :] for j in range(jn)]
-    first, last = sub == 0, sub == SUB - 1
-    below = [jnp.where(first, 0.0, pltpu.roll(v, 1, 0)) for v in mid]
-    above = [jnp.where(last, 0.0, pltpu.roll(v, SUB - 1, 0)) for v in mid]
-    line = below + mid + above
-    news = []
-    for j in range(jn):
-        tile = slice(SUB * j, SUB * j + SUB)
-        acc = z[x, tile, :] + (3.0 * COEFFS[0]) * mid[j]
-        for k in range(1, RADIUS + 1):
-            near = (u[x + k, tile, :] + u[x - k, tile, :]) + (line[jn + j + k] + line[jn + j - k])
-            acc = acc + COEFFS[k] * near
-        if extra is not None:
-            acc = acc + extra(j)
-        new = (2.0 * mid[j] - prior[x, tile, :]) + cc[x, tile, :] * acc
-        prior[x, tile, :] = new
-        news.append(new)
-    return news
-
-
-def one_step(geo, moment, us, ur, ps, pr, cc, gg, corr, zs, zr, dw, wavelet, src, first, count, fresh):
-    nx = geo.nx
-    depth_part(geo, us, zs, dw, first, count)
-    depth_part(geo, ur, zr, dw, first, count)
-    sub = lax.broadcasted_iota(jnp.int32, (SUB, LANES), 0)
-    lane = lax.broadcasted_iota(jnp.int32, (SUB, LANES), 1)
-    at_depth = lane == REC_DEPTH
-
-    def plane(x, carry, inner):
-        def fed(j):
-            rows = gg[x, SUB * j : SUB * j + SUB, :]
-            return jnp.where(at_depth, pltpu.roll(rows, (REC_DEPTH - moment) % LANES, 1), 0.0)
-
-        news = update_plane(geo, us, ps, cc, zs, x, sub, None)
-        newr = update_plane(geo, ur, pr, cc, zr, x, sub, fed)
-        if inner:
-            for j in range(geo.jn):
-                tile = slice(SUB * j, SUB * j + SUB)
-                product = news[j] * newr[j]
-                if not fresh:
-                    product = product + corr[x - HALO, tile, :]
-                corr[x - HALO, tile, :] = product
-        return carry
-
-    edge = HALO - first
-    if edge > 0:
-        lax.fori_loop(first, HALO, lambda x, c: plane(x, c, False), 0)
-        lax.fori_loop(nx + HALO, first + count, lambda x, c: plane(x, c, False), 0)
-    lax.fori_loop(HALO, nx + HALO, lambda x, c: plane(x, c, True), 0)
+    lax.fori_loop(0, count // GROUP, group, 0)
     xs, row, ok = src
 
     @pl.when(ok & (xs >= first) & (xs < first + count))
     def _():
-        shot = jnp.where(lane[0:1] == SRC_DEPTH, wavelet[0, moment], 0.0)
-        add = cc[xs, pl.ds(row, 1), :] * shot
+        lane = lax.broadcasted_iota(jnp.int32, (SUB, LANES), 1)
+        shot = jnp.where(lane == SRC_DEPTH, pltpu.roll(wav[...], (SRC_DEPTH - moment) % LANES, 1), 0.0)
+        add = cc[xs, pl.ds(row, 1), :] * shot[0:1]
         ps[xs, pl.ds(row, 1), :] = ps[xs, pl.ds(row, 1), :] + add
-
-        @pl.when((xs >= HALO) & (xs < nx + HALO))
-        def _():
-            corr[xs - HALO, pl.ds(row, 1), :] = (
-                corr[xs - HALO, pl.ds(row, 1), :] + add * pr[xs, pl.ds(row, 1), :]
-            )
+        at = xs - HALO + RADIUS
+        corr[at, pl.ds(row, 1), :] = corr[at, pl.ds(row, 1), :] + add * pr[xs, pl.ds(row, 1), :]
 
 
 def round_kernel(geo, block, last):
@@ -358,14 +332,20 @@
     def body(*refs):
         refs = list(refs)
         take = lambda n: [refs.pop(0) for _ in range(n)]
-        us0, ur0, ps0, pr0, cc0, dw, gg = take(7)
-        if not first_round:
+        take(4)
+        if first_round:
             take(1)
+        else:
+            take(1)
+            cc, ee = take(2)
+        dw, gg, wav = take(3)
         inputs = take(5)
-        wavelet, sx, sy = take(3)
-        us, ur, ps, pr, cc, corr = take(6)
+        sx, sy = take(2)
+        us, ur, ps, pr = take(4)
+        if first_round:
+            cc, ee = take(2)
+        (corr,) = take(1)
         outs = [] if last else take(5)
-        zs, zr = take(2)
         p, g, _ = geo.place()
         xs = sx[0] - g * geo.nx + HALO
         w = sy[0] - p * geo.ny + SUB * p
@@ -373,7 +353,16 @@
         shift = geo.jn.bit_length() - 1
         src = (xs, (w & (geo.jn - 1)) * SUB + (w >> shift), ok)
         unpack(geo, (us, ur), (ps, pr, cc) if first_round else (), inputs)
-        common = (cc, gg, corr, zs, zr, dw, wavelet, src)
+        if first_round:
+
+            def scale(x, carry):
+                speed = cc[x]
+                ee[x] = 2.0 + (3.0 * COEFFS[0]) * speed
+                cc[x] = COEFFS[1] * speed
+                return carry
+
+            lax.fori_loop(0, geo.xe, scale, 0, unroll=2)
+        common = (cc, ee, gg, corr, dw, wav, src)
         one_step(geo, DEEP * block, us, ur, ps, pr, *common, HALO - RADIUS, geo.nx + 2 * RADIUS, first_round)
         one_step(geo, DEEP * block + 1, ps, pr, us, ur, *common, HALO, geo.nx, False)
         if not last:
@@ -391,7 +380,7 @@
 
         def turn(x, carry):
             for j in range(geo.jn):
-                pad[x, pl.ds(j, SUB, stride=geo.jn), :] = corr[x, SUB * j : SUB * j + SUB, :]
+                pad[x, pl.ds(j, SUB, stride=geo.jn), :] = corr[x + RADIUS, SUB * j : SUB * j + SUB, :]
             return carry
 
         lax.fori_loop(0, geo.nx, turn, 0, unroll=4)
@@ -446,42 +435,50 @@
         loaded = call(
             load_kernel(geo),
             [state] * 5
-            + [jax.ShapeDtypeStruct((2 * LANES, 2 * LANES), jnp.bfloat16)]
+            + [jax.ShapeDtypeStruct((2 * LANES, LANES), jnp.bfloat16)]
             + message_shapes(geo, True),
-            [ANY] * 5,
+            [HBM] * 5,
             (sn, sl, rn, rl, courant),
             scratch=[pltpu.VMEM((5, nx, geo.win, nz), F32), pltpu.SemaphoreType.DMA((5,))],
         )
         us, ur, ps, pr, cc, dw = loaded[:6]
         messages = send(loaded[6:])
         nrec = traces.shape[2]
-        (gg,) = call(
+        gg, wav = call(
             receiver_kernel(geo, nrec),
-            [state],
-            [VM] * 3,
-            (ri, rc, traces),
+            [state, shape(SUB, LANES)],
+            [VM] * 4,
+            (ri, rc, traces, wavelet),
             scratch=[pltpu.VMEM((LANES, nrec), F32)],
         )
-        corr = None
+        corr_shape = shape(nx + 2 * RADIUS, geo.win, nz)
+        corr = ee = None
         blocks = STEPS // DEEP
         for block in range(blocks):
             last = block == blocks - 1
-            args = [us, ur, ps, pr, cc, dw, gg] + ([] if corr is None else [corr]) + messages
-            specs = [VM] * len(args) + [SM] * 3
-            aliases = {i: i for i in range(5)}
-            if corr is not None:
-                aliases[7] = 5
+            if block == 0:
+                args = [us, ur, ps, pr, cc]
+                outs = [state] * 6 + [corr_shape]
+                aliases = {i: i for i in range(5)}
+            else:
+                args = [us, ur, ps, pr, corr, cc, ee]
+                outs = [state] * 4 + [corr_shape]
+                aliases = {i: i for i in range(5)}
+            args = args + [dw, gg, wav] + messages
             outs = call(
                 round_kernel(geo, block, last),
-                [state] * 5 + [shape(nx, geo.win, nz)] + ([] if last else message_shapes(geo, False)),
-                specs,
-                args + [wavelet, si, sc],
-                scratch=[pltpu.VMEM((geo.xe, geo.win, nz), F32)] * 2,
+                outs + ([] if last else message_shapes(geo, False)),
+                [VM] * len(args) + [SM] * 2,
+                args + [si, sc],
                 aliases=aliases,
             )
-            us, ur, ps, pr, cc, corr = outs[:6]
+            us, ur, ps, pr = outs[:4]
+            if block == 0:
+                cc, ee, corr = outs[4:7]
+            else:
+                corr = outs[4]
             if not last:
-                messages = send(outs[6:])
+                messages = send(outs[-5:])
         halves = mesh.shape["sa"]
         part = shape(nx // halves, ny, nz)
         mine, other = call(
@@ -494,7 +491,7 @@
             [shape(1, nx, ny, nz)] * 4,
             [VM] * 4,
             (us, ur, ps, pr),
-            out_specs=[ANY] * 4,
+            out_specs=[HBM] * 4,
             scratch=[pltpu.VMEM((4, nx, geo.win, nz), F32), pltpu.SemaphoreType.DMA((4,))],
         )
         return (*fields, image)
@@ -662,7 +659,7 @@
     def run(*args):
         nx, ny, nz = args[4].shape
         fits = mesh.shape["gy"] == 2 and mesh.shape["sa"] == 2 and nz == LANES
-        fits = fits and (ny + HALO) == RADIUS * SUB and nx % (2 * CHUNK) == 0
+        fits = fits and (ny + HALO) == RADIUS * SUB and nx % (2 * HALO) == 0
         return (fast if fits else general_body)(*args)
 
     return run

time: 126 us -> 90 us (0.71)
  Pallas kernels: 65.1 us -> 29.6 us
    pallas_call x10, Pallas kernels: 65.1 us -> 29.6 us  [call(): pl.pallas_call(body, out_shape=out_shapes, in_specs=specs, out_specs=out_...]
  transfers between devices with their start and end apart: 31 -> 31, of which waited for: 7 -> 7; matrix products, arithmetic and copies ran while one was open for 0% -> 0% of each run, Pallas kernels for 4% -> 5%
where the time goes in v1:
time: 90 us; the launch traced here: 89.6 us
  starting transfers between devices  35.1 us (39%)
  Pallas kernels  29.6 us (33%)
  waiting for transfers between devices  16.3 us (18%)
  local copies, waits for them, and re-layouts  5.63 us (6%)
  between operations  2.18 us (2%)
    ppermute x30, starting transfers between devices, run(): lax.ppermute(m, names, route)  35.1 us
    pallas_call x10, Pallas kernels, call(): pl.pallas_call(body, out_shape=out_shapes, in_specs=specs, out_specs=out_...  29.6 us
    ppermute x30, waiting for transfers between devices, run(): lax.ppermute(m, names, route)  16.2 us
    unnamed x19, local copies, waits for them, and re-layouts  5.63 us
  transfers between devices with their start and end apart: 31, of which 7 were waited for; matrix products, arithmetic and copies ran while one was open for 0% of the time, Pallas kernels for 5%

profile of v1, /device:TPU:0, one launch (start us, length us, event | category | flops | bytes accessed | tf_op | source)
XLA Modules:
  0.0 89.6 jit_solution(1059649141839692102)
XLA Ops:
  0.6 1.0 %copy-done = f32[1,32,24,128]{3,2,1,0:T(8,128)S(1)} copy-done((f32[1,32,24,128]{3,2,1,0:T(8,128)S(1)}, f32[1,32,24,128]{3,2,1,0:T(8,128)}, u32[]{:S(2)}) %copy-start) | copy-done | bytes 393240
  1.6 1.0 %copy-done.1 = f32[1,32,24,128]{3,2,1,0:T(8,128)S(1)} copy-done((f32[1,32,24,128]{3,2,1,0:T(8,128)S(1)}, f32[1,32,24,128]{3,2,1,0:T(8,128)}, u32[]{:S(2)}) %copy-start.1) | copy-done | bytes 393240
  2.6 1.0 %copy-done.2 = f32[1,32,24,128]{3,2,1,0:T(8,128)S(1)} copy-done((f32[1,32,24,128]{3,2,1,0:T(8,128)S(1)}, f32[1,32,24,128]{3,2,1,0:T(8,128)}, u32[]{:S(2)}) %copy-start.2) | copy-done | bytes 393240
  3.6 1.0 %copy-done.3 = f32[1,32,24,128]{3,2,1,0:T(8,128)S(1)} copy-done((f32[1,32,24,128]{3,2,1,0:T(8,128)S(1)}, f32[1,32,24,128]{3,2,1,0:T(8,128)}, u32[]{:S(2)}) %copy-start.3) | copy-done | bytes 393240
  4.6 1.0 %copy-done.4 = f32[32,24,128]{2,1,0:T(8,128)S(1)} copy-done((f32[32,24,128]{2,1,0:T(8,128)S(1)}, f32[32,24,128]{2,1,0:T(8,128)}, u32[]{:S(2)}) %copy-start.4) | copy-done | bytes 393240
  5.6 1.1 %shard_map.146 = (f32[48,32,128]{2,1,0:T(8,128)S(1)}, f32[48,32,128]{2,1,0:T(8,128)S(1)}, f32[48,32,128]{2,1,0:T(8,128)S(1)}, f32[48,32,128]{2,1,0:T(8,128)S(1)}...) custom-call(f32[1,32,24,128]{3,2,1,0:T(8,128)S(1)} %copy-done, ...), custom_call_target="tpu_custom_call" | custom-call | tf_op jit(solution)/shard_map/pallas_call | solution.py:86
  6.8 0.0 copy-start.8
  6.8 3.0 %collective-permute-start = (f32[112,8,128]{2,1,0:T(8,128)S(1)}, f32[112,8,128]{2,1,0:T(8,128)S(1)}, u32[]{:S(2)}, u32[]{:S(2)}) collective-permute-start(f32[112,8,128]{2,1,0:T(8,128)S(1)} %get-tuple-element.89), channel_id=1, source_target_pairs={{0,2},{1,3},{2,0},{3,1},{4,6},{5,7},{6,4},{7,5},{8,10},{9,11},{10,... | collective-permute-start | bytes 1376264 | tf_op jit(solution)/shard_map/ppermute | solution.py:434
  9.8 1.6 %collective-permute-start.1 = (f32[28,24,128]{2,1,0:T(8,128)S(1)}, f32[28,24,128]{2,1,0:T(8,128)S(1)}, u32[]{:S(2)}, u32[]{:S(2)}) collective-permute-start(f32[28,24,128]{2,1,0:T(8,128)S(1)} %get-tuple-element.90), channel_id=1, source_target_pairs={{0,4},{1,5},{2,6},{3,7},{4,0},{5,1},{6,2},{7,3},{8,12},{9,13},{10,... | collective-permute-start | bytes 1032200 | tf_op jit(solution)/shard_map/ppermute | solution.py:434
  11.4 3.1 %collective-permute-start.3 = (f32[4,8,128]{2,1,0:T(8,128)S(1)}, f32[4,8,128]{2,1,0:T(8,128)S(1)}, u32[]{:S(2)}, u32[]{:S(2)}) collective-permute-start(f32[4,8,128]{2,1,0:T(8,128)S(1)} %get-tuple-element.92), channel_id=1, source_target_pairs={{0,6},{1,7},{2,4},{3,5},{4,2},{5,3},{6,0},{7,1},{8,14},{9,15},{10,... | collective-permute-start | bytes 49160 | tf_op jit(solution)/shard_map/ppermute | solution.py:434
  15.8 0.0 copy-start.5
  15.9 0.0 copy-start.7
  15.9 0.6 copy-done.5
  16.5 0.0 copy-done.6
  16.5 0.0 copy-done.7
  16.5 3.2 %shard_map.147 = (f32[48,32,128]{2,1,0:T(8,128)S(1)}, f32[8,128]{1,0:T(8,128)S(1)}) custom-call(s32[1,64]{1,0:T(1,128)S(1)} %copy-done.5, s32[1,64]{1,0:T(1,128)S(1)} %copy-done.6, f32[1,12,64]{2,1,0:T(8,128)S(1)} %copy.46.traces, f32[1,12]{1,0:T(1,128)S(1)} %copy-done.7), custom_call_target="tpu_custom_call" | custom-call | tf_op jit(solution)/shard_map/pallas_call | solution.py:86
  19.7 0.9 %collective-permute-done.refs_8_ = f32[112,8,128]{2,1,0:T(8,128)S(1)} collective-permute-done((f32[112,8,128]{2,1,0:T(8,128)S(1)}, f32[112,8,128]{2,1,0:T(8,128)S(1)}, u32[]{:S(2)}, u32[]{:S(2)}) %collective-permute-start) | collective-permute-done | bytes 458784 | tf_op jit(solution)/shard_map/ppermute | solution.py:434
  20.7 4.3 %shard_map.148 = (f32[48,32,128]{2,1,0:T(8,128)S(1)}, f32[48,32,128]{2,1,0:T(8,128)S(1)}, f32[48,32,128]{2,1,0:T(8,128)S(1)}, f32[48,32,128]{2,1,0:T(8,128)S(1)}...) custom-call(f32[48,32,128]{2,1,0:T(8,128)S(1)} %get-tuple-element.81, ...), custom_call_target="tpu_custom_call", output_to_operand_aliasing={{0}: (0, {}), {1}: (1, {}), {2}: (2, {}), {3}: (3, {}), {4}... | custom-call | tf_op jit(solution)/shard_map/pallas_call | solution.py:86
  25.0 1.8 %collective-permute-start.5 = (f32[64,8,128]{2,1,0:T(8,128)S(1)}, f32[64,8,128]{2,1,0:T(8,128)S(1)}, u32[]{:S(2)}, u32[]{:S(2)}) collective-permute-start(f32[64,8,128]{2,1,0:T(8,128)S(1)} %get-tuple-element.101), channel_id=1, source_target_pairs={{0,2},{1,3},{2,0},{3,1},{4,6},{5,7},{6,4},{7,5},{8,10},{9,11},{10,... | collective-permute-start | bytes 786440 | tf_op jit(solution)/shard_map/ppermute | solution.py:434
  26.8 2.0 %collective-permute-start.6 = (f32[16,24,128]{2,1,0:T(8,128)S(1)}, f32[16,24,128]{2,1,0:T(8,128)S(1)}, u32[]{:S(2)}, u32[]{:S(2)}) collective-permute-start(f32[16,24,128]{2,1,0:T(8,128)S(1)} %get-tuple-element.102), channel_id=1, source_target_pairs={{0,4},{1,5},{2,6},{3,7},{4,0},{5,1},{6,2},{7,3},{8,12},{9,13},{10,... | collective-permute-start | bytes 589832 | tf_op jit(solution)/shard_map/ppermute | solution.py:434
  28.8 2.7 %collective-permute-start.8 = (f32[4,8,128]{2,1,0:T(8,128)S(1)}, f32[4,8,128]{2,1,0:T(8,128)S(1)}, u32[]{:S(2)}, u32[]{:S(2)}) collective-permute-start(f32[4,8,128]{2,1,0:T(8,128)S(1)} %get-tuple-element.104), channel_id=1, source_target_pairs={{0,6},{1,7},{2,4},{3,5},{4,2},{5,3},{6,0},{7,1},{8,14},{9,15},{10,... | collective-permute-start | bytes 49160 | tf_op jit(solution)/shard_map/ppermute | solution.py:434
  31.5 2.0 %collective-permute-done.8.refs_13_ = f32[4,8,128]{2,1,0:T(8,128)S(1)} collective-permute-done((f32[4,8,128]{2,1,0:T(8,128)S(1)}, f32[4,8,128]{2,1,0:T(8,128)S(1)}, u32[]{:S(2)}, u32[]{:S(2)}) %collective-permute-start.8) | collective-permute-done | bytes 16416 | tf_op jit(solution)/shard_map/ppermute | solution.py:434
  33.5 4.0 %shard_map.149 = (f32[48,32,128]{2,1,0:T(8,128)S(1)}, f32[48,32,128]{2,1,0:T(8,128)S(1)}, f32[48,32,128]{2,1,0:T(8,128)S(1)}, f32[48,32,128]{2,1,0:T(8,128)S(1)}...) custom-call(f32[48,32,128]{2,1,0:T(8,128)S(1)} %get-tuple-element.94, ...), custom_call_target="tpu_custom_call", output_to_operand_aliasing={{0}: (0, {}), {1}: (1, {}), {2}: (2, {}), {3}: (3, {}), {4}... | custom-call | tf_op jit(solution)/shard_map/pallas_call | solution.py:86
  37.5 1.3 %collective-permute-start.10 = (f32[64,8,128]{2,1,0:T(8,128)S(1)}, f32[64,8,128]{2,1,0:T(8,128)S(1)}, u32[]{:S(2)}, u32[]{:S(2)}) collective-permute-start(f32[64,8,128]{2,1,0:T(8,128)S(1)} %get-tuple-element.111), channel_id=1, source_target_pairs={{0,2},{1,3},{2,0},{3,1},{4,6},{5,7},{6,4},{7,5},{8,10},{9,11},{10,... | collective-permute-start | bytes 786440 | tf_op jit(solution)/shard_map/ppermute | solution.py:434
  38.8 2.3 %collective-permute-start.11 = (f32[16,24,128]{2,1,0:T(8,128)S(1)}, f32[16,24,128]{2,1,0:T(8,128)S(1)}, u32[]{:S(2)}, u32[]{:S(2)}) collective-permute-start(f32[16,24,128]{2,1,0:T(8,128)S(1)} %get-tuple-element.112), channel_id=1, source_target_pairs={{0,4},{1,5},{2,6},{3,7},{4,0},{5,1},{6,2},{7,3},{8,12},{9,13},{10,... | collective-permute-start | bytes 589832 | tf_op jit(solution)/shard_map/ppermute | solution.py:434
  41.1 2.0 %collective-permute-start.13 = (f32[4,8,128]{2,1,0:T(8,128)S(1)}, f32[4,8,128]{2,1,0:T(8,128)S(1)}, u32[]{:S(2)}, u32[]{:S(2)}) collective-permute-start(f32[4,8,128]{2,1,0:T(8,128)S(1)} %get-tuple-element.114), channel_id=1, source_target_pairs={{0,6},{1,7},{2,4},{3,5},{4,2},{5,3},{6,0},{7,1},{8,14},{9,15},{10,... | collective-permute-start | bytes 49160 | tf_op jit(solution)/shard_map/ppermute | solution.py:434
  43.1 2.9 %collective-permute-done.13.refs_13_ = f32[4,8,128]{2,1,0:T(8,128)S(1)} collective-permute-done((f32[4,8,128]{2,1,0:T(8,128)S(1)}, f32[4,8,128]{2,1,0:T(8,128)S(1)}, u32[]{:S(2)}, u32[]{:S(2)}) %collective-permute-start.13) | collective-permute-done | bytes 16416 | tf_op jit(solution)/shard_map/ppermute | solution.py:434
  46.0 3.9 %shard_map.150 = (f32[48,32,128]{2,1,0:T(8,128)S(1)}, f32[48,32,128]{2,1,0:T(8,128)S(1)}, f32[48,32,128]{2,1,0:T(8,128)S(1)}, f32[48,32,128]{2,1,0:T(8,128)S(1)}...) custom-call(f32[48,32,128]{2,1,0:T(8,128)S(1)} %get-tuple-element.10, ...), custom_call_target="tpu_custom_call", output_to_operand_aliasing={{0}: (0, {}), {1}: (1, {}), {2}: (2, {}), {3}: (3, {}), {4}... | custom-call | tf_op jit(solution)/shard_map/pallas_call | solution.py:86
  50.0 1.3 %collective-permute-start.15 = (f32[64,8,128]{2,1,0:T(8,128)S(1)}, f32[64,8,128]{2,1,0:T(8,128)S(1)}, u32[]{:S(2)}, u32[]{:S(2)}) collective-permute-start(f32[64,8,128]{2,1,0:T(8,128)S(1)} %get-tuple-element.121), channel_id=1, source_target_pairs={{0,2},{1,3},{2,0},{3,1},{4,6},{5,7},{6,4},{7,5},{8,10},{9,11},{10,... | collective-permute-start | bytes 786440 | tf_op jit(solution)/shard_map/ppermute | solution.py:434
  51.3 2.1 %collective-permute-start.16 = (f32[16,24,128]{2,1,0:T(8,128)S(1)}, f32[16,24,128]{2,1,0:T(8,128)S(1)}, u32[]{:S(2)}, u32[]{:S(2)}) collective-permute-start(f32[16,24,128]{2,1,0:T(8,128)S(1)} %get-tuple-element.122), channel_id=1, source_target_pairs={{0,4},{1,5},{2,6},{3,7},{4,0},{5,1},{6,2},{7,3},{8,12},{9,13},{10,... | collective-permute-start | bytes 589832 | tf_op jit(solution)/shard_map/ppermute | solution.py:434
  53.4 2.0 %collective-permute-start.18 = (f32[4,8,128]{2,1,0:T(8,128)S(1)}, f32[4,8,128]{2,1,0:T(8,128)S(1)}, u32[]{:S(2)}, u32[]{:S(2)}) collective-permute-start(f32[4,8,128]{2,1,0:T(8,128)S(1)} %get-tuple-element.124), channel_id=1, source_target_pairs={{0,6},{1,7},{2,4},{3,5},{4,2},{5,3},{6,0},{7,1},{8,14},{9,15},{10,... | collective-permute-start | bytes 49160 | tf_op jit(solution)/shard_map/ppermute | solution.py:434
  55.4 3.3 %collective-permute-done.18.refs_13_ = f32[4,8,128]{2,1,0:T(8,128)S(1)} collective-permute-done((f32[4,8,128]{2,1,0:T(8,128)S(1)}, f32[4,8,128]{2,1,0:T(8,128)S(1)}, u32[]{:S(2)}, u32[]{:S(2)}) %collective-permute-start.18) | collective-permute-done | bytes 16416 | tf_op jit(solution)/shard_map/ppermute | solution.py:434
  58.7 4.0 %shard_map.151 = (f32[48,32,128]{2,1,0:T(8,128)S(1)}, f32[48,32,128]{2,1,0:T(8,128)S(1)}, f32[48,32,128]{2,1,0:T(8,128)S(1)}, f32[48,32,128]{2,1,0:T(8,128)S(1)}...) custom-call(f32[48,32,128]{2,1,0:T(8,128)S(1)} %get-tuple-element.11, ...), custom_call_target="tpu_custom_call", output_to_operand_aliasing={{0}: (0, {}), {1}: (1, {}), {2}: (2, {}), {3}: (3, {}), {4}... | custom-call | tf_op jit(solution)/shard_map/pallas_call | solution.py:86
  62.7 1.0 %collective-permute-start.20 = (f32[64,8,128]{2,1,0:T(8,128)S(1)}, f32[64,8,128]{2,1,0:T(8,128)S(1)}, u32[]{:S(2)}, u32[]{:S(2)}) collective-permute-start(f32[64,8,128]{2,1,0:T(8,128)S(1)} %get-tuple-element.131), channel_id=1, source_target_pairs={{0,2},{1,3},{2,0},{3,1},{4,6},{5,7},{6,4},{7,5},{8,10},{9,11},{10,... | collective-permute-start | bytes 786440 | tf_op jit(solution)/shard_map/ppermute | solution.py:434
  63.6 2.3 %collective-permute-start.21 = (f32[16,24,128]{2,1,0:T(8,128)S(1)}, f32[16,24,128]{2,1,0:T(8,128)S(1)}, u32[]{:S(2)}, u32[]{:S(2)}) collective-permute-start(f32[16,24,128]{2,1,0:T(8,128)S(1)} %get-tuple-element.132), channel_id=1, source_target_pairs={{0,4},{1,5},{2,6},{3,7},{4,0},{5,1},{6,2},{7,3},{8,12},{9,13},{10,... | collective-permute-start | bytes 589832 | tf_op jit(solution)/shard_map/ppermute | solution.py:434
  65.9 1.7 %collective-permute-start.23 = (f32[4,8,128]{2,1,0:T(8,128)S(1)}, f32[4,8,128]{2,1,0:T(8,128)S(1)}, u32[]{:S(2)}, u32[]{:S(2)}) collective-permute-start(f32[4,8,128]{2,1,0:T(8,128)S(1)} %get-tuple-element.134), channel_id=1, source_target_pairs={{0,6},{1,7},{2,4},{3,5},{4,2},{5,3},{6,0},{7,1},{8,14},{9,15},{10,... | collective-permute-start | bytes 49160 | tf_op jit(solution)/shard_map/ppermute | solution.py:434
  67.6 3.5 %collective-permute-done.23.refs_13_ = f32[4,8,128]{2,1,0:T(8,128)S(1)} collective-permute-done((f32[4,8,128]{2,1,0:T(8,128)S(1)}, f32[4,8,128]{2,1,0:T(8,128)S(1)}, u32[]{:S(2)}, u32[]{:S(2)}) %collective-permute-start.23) | collective-permute-done | bytes 16416 | tf_op jit(solution)/shard_map/ppermute | solution.py:434
  71.1 4.0 %shard_map.152 = (f32[48,32,128]{2,1,0:T(8,128)S(1)}, f32[48,32,128]{2,1,0:T(8,128)S(1)}, f32[48,32,128]{2,1,0:T(8,128)S(1)}, f32[48,32,128]{2,1,0:T(8,128)S(1)}...) custom-call(f32[48,32,128]{2,1,0:T(8,128)S(1)} %get-tuple-element.12, ...), custom_call_target="tpu_custom_call", output_to_operand_aliasing={{0}: (0, {}), {1}: (1, {}), {2}: (2, {}), {3}: (3, {}), {4}... | custom-call | tf_op jit(solution)/shard_map/pallas_call | solution.py:86
  75.1 0.9 %collective-permute-start.25 = (f32[64,8,128]{2,1,0:T(8,128)S(1)}, f32[64,8,128]{2,1,0:T(8,128)S(1)}, u32[]{:S(2)}, u32[]{:S(2)}) collective-permute-start(f32[64,8,128]{2,1,0:T(8,128)S(1)} %get-tuple-element.141), channel_id=1, source_target_pairs={{0,2},{1,3},{2,0},{3,1},{4,6},{5,7},{6,4},{7,5},{8,10},{9,11},{10,... | collective-permute-start | bytes 786440 | tf_op jit(solution)/shard_map/ppermute | solution.py:434
  76.0 2.1 %collective-permute-start.26 = (f32[16,24,128]{2,1,0:T(8,128)S(1)}, f32[16,24,128]{2,1,0:T(8,128)S(1)}, u32[]{:S(2)}, u32[]{:S(2)}) collective-permute-start(f32[16,24,128]{2,1,0:T(8,128)S(1)} %get-tuple-element.142), channel_id=1, source_target_pairs={{0,4},{1,5},{2,6},{3,7},{4,0},{5,1},{6,2},{7,3},{8,12},{9,13},{10,... | collective-permute-start | bytes 589832 | tf_op jit(solution)/shard_map/ppermute | solution.py:434
  78.1 1.8 %collective-permute-start.28 = (f32[4,8,128]{2,1,0:T(8,128)S(1)}, f32[4,8,128]{2,1,0:T(8,128)S(1)}, u32[]{:S(2)}, u32[]{:S(2)}) collective-permute-start(f32[4,8,128]{2,1,0:T(8,128)S(1)} %get-tuple-element.144), channel_id=1, source_target_pairs={{0,6},{1,7},{2,4},{3,5},{4,2},{5,3},{6,0},{7,1},{8,14},{9,15},{10,... | collective-permute-start | bytes 49160 | tf_op jit(solution)/shard_map/ppermute | solution.py:434
  80.0 3.5 %collective-permute-done.28.refs_13_ = f32[4,8,128]{2,1,0:T(8,128)S(1)} collective-permute-done((f32[4,8,128]{2,1,0:T(8,128)S(1)}, f32[4,8,128]{2,1,0:T(8,128)S(1)}, u32[]{:S(2)}, u32[]{:S(2)}) %collective-permute-start.28) | collective-permute-done | bytes 16416 | tf_op jit(solution)/shard_map/ppermute | solution.py:434
  83.5 3.7 %shard_map.153 = (f32[48,32,128]{2,1,0:T(8,128)S(1)}, f32[48,32,128]{2,1,0:T(8,128)S(1)}, f32[48,32,128]{2,1,0:T(8,128)S(1)}, f32[48,32,128]{2,1,0:T(8,128)S(1)}, f32[40,32,128]{2,1,0:T(8,128)S(1)}) custom-call(f32[48,32,128]{2,1,0:T(8,128)S(1)} %get-tuple-element.136.refs_0_, ...), custom_call_target="tpu_custom_call", output_to_operand_aliasing={{0}: (0, {}), {1}: (1, {}), {2}: (2, {}), {3}: (3, {}), {4}... | custom-call | tf_op jit(solution)/shard_map/pallas_call | solution.py:86
  87.2 0.1 shard_map.155
  87.4 0.1 collective-permute-start.30
  87.5 1.2 %shard_map.154 = (f32[1,32,24,128]{3,2,1,0:T(8,128)}, f32[1,32,24,128]{3,2,1,0:T(8,128)}, f32[1,32,24,128]{3,2,1,0:T(8,128)}, f32[1,32,24,128]{3,2,1,0:T(8,128)}) custom-call(f32[48,32,128]{2,1,0:T(8,128)S(1)} %get-tuple-element.146.us, f32[48,32,128]{2,1,0:T(8,128)S(1)} %get-tuple-element.147.ur, f32[48,32,128]{2,1,0:T(8,128)S(1)} %get-tuple-element.148.ps, ...), custom_call_target="tpu_custom_call" | custom-call | tf_op jit(solution)/shard_map/pallas_call | solution.py:86
  88.7 0.2 collective-permute-done.30
  88.9 0.7 add_multiply_fusion
  (44 shorter events, 0.1 us)
Async XLA Ops:
  0.6 1.0 %copy-start = (f32[1,32,24,128]{3,2,1,0:T(8,128)S(1)}, f32[1,32,24,128]{3,2,1,0:T(8,128)}, u32[]{:S(2)}) copy-start(f32[1,32,24,128]{3,2,1,0:T(8,128)} %s0.1) | copy-start | bytes 1179652
  1.6 1.0 %copy-start.1 = (f32[1,32,24,128]{3,2,1,0:T(8,128)S(1)}, f32[1,32,24,128]{3,2,1,0:T(8,128)}, u32[]{:S(2)}) copy-start(f32[1,32,24,128]{3,2,1,0:T(8,128)} %s1_.1) | copy-start | bytes 1179652
  2.6 1.0 %copy-start.2 = (f32[1,32,24,128]{3,2,1,0:T(8,128)S(1)}, f32[1,32,24,128]{3,2,1,0:T(8,128)}, u32[]{:S(2)}) copy-start(f32[1,32,24,128]{3,2,1,0:T(8,128)} %r0.1) | copy-start | bytes 1179652
  3.6 1.0 %copy-start.3 = (f32[1,32,24,128]{3,2,1,0:T(8,128)S(1)}, f32[1,32,24,128]{3,2,1,0:T(8,128)}, u32[]{:S(2)}) copy-start(f32[1,32,24,128]{3,2,1,0:T(8,128)} %r1.1) | copy-start | bytes 1179652
  4.6 1.0 %copy-start.4 = (f32[32,24,128]{2,1,0:T(8,128)S(1)}, f32[32,24,128]{2,1,0:T(8,128)}, u32[]{:S(2)}) copy-start(f32[32,24,128]{2,1,0:T(8,128)} %c0.1) | copy-start | bytes 1179652
  6.8 9.1 %copy-start.8 = (f32[1,12,64]{2,0,1:T(1,128)S(1)}, f32[1,12,64]{2,0,1:T(1,128)}, u32[]{:S(2)}) copy-start(f32[1,12,64]{2,0,1:T(1,128)} %param.17) | copy-start | bytes 9220
  6.8 13.9 %collective-permute-start = (f32[112,8,128]{2,1,0:T(8,128)S(1)}, f32[112,8,128]{2,1,0:T(8,128)S(1)}, u32[]{:S(2)}, u32[]{:S(2)}) collective-permute-start(f32[112,8,128]{2,1,0:T(8,128)S(1)} %get-tuple-element.89), channel_id=1, source_target_pairs={{0,2},{1,3},{2,0},{3,1},{4,6},{5,7},{6,4},{7,5},{8,10},{9,11},{10,... | collective-permute-start | bytes 1376264 | tf_op jit(solution)/shard_map/ppermute | solution.py:434
  9.8 9.9 %collective-permute-start.1 = (f32[28,24,128]{2,1,0:T(8,128)S(1)}, f32[28,24,128]{2,1,0:T(8,128)S(1)}, u32[]{:S(2)}, u32[]{:S(2)}) collective-permute-start(f32[28,24,128]{2,1,0:T(8,128)S(1)} %get-tuple-element.90), channel_id=1, source_target_pairs={{0,4},{1,5},{2,6},{3,7},{4,0},{5,1},{6,2},{7,3},{8,12},{9,13},{10,... | collective-permute-start | bytes 1032200 | tf_op jit(solution)/shard_map/ppermute | solution.py:434
  11.4 8.3 %collective-permute-start.2 = (f32[28,24,128]{2,1,0:T(8,128)S(1)}, f32[28,24,128]{2,1,0:T(8,128)S(1)}, u32[]{:S(2)}, u32[]{:S(2)}) collective-permute-start(f32[28,24,128]{2,1,0:T(8,128)S(1)} %get-tuple-element.91), channel_id=1, source_target_pairs={{0,1},{1,0},{2,3},{3,2},{4,8},{5,9},{6,10},{7,11},{8,4},{9,5},{10,... | collective-permute-start | bytes 1032200 | tf_op jit(solution)/shard_map/ppermute | solution.py:434
  11.4 8.3 %collective-permute-start.3 = (f32[4,8,128]{2,1,0:T(8,128)S(1)}, f32[4,8,128]{2,1,0:T(8,128)S(1)}, u32[]{:S(2)}, u32[]{:S(2)}) collective-permute-start(f32[4,8,128]{2,1,0:T(8,128)S(1)} %get-tuple-element.92), channel_id=1, source_target_pairs={{0,6},{1,7},{2,4},{3,5},{4,2},{5,3},{6,0},{7,1},{8,14},{9,15},{10,... | collective-permute-start | bytes 49160 | tf_op jit(solution)/shard_map/ppermute | solution.py:434
  14.5 5.2 %collective-permute-start.4 = (f32[4,8,128]{2,1,0:T(8,128)S(1)}, f32[4,8,128]{2,1,0:T(8,128)S(1)}, u32[]{:S(2)}, u32[]{:S(2)}) collective-permute-start(f32[4,8,128]{2,1,0:T(8,128)S(1)} %get-tuple-element.93), channel_id=1, source_target_pairs={{0,1},{1,0},{2,3},{3,2},{4,10},{5,11},{6,8},{7,9},{8,6},{9,7},{10,... | collective-permute-start | bytes 49160 | tf_op jit(solution)/shard_map/ppermute | solution.py:434
  15.8 0.7 copy-start.5
  15.8 0.7 copy-start.6
  15.9 0.7 copy-start.7
  25.0 8.5 %collective-permute-start.5 = (f32[64,8,128]{2,1,0:T(8,128)S(1)}, f32[64,8,128]{2,1,0:T(8,128)S(1)}, u32[]{:S(2)}, u32[]{:S(2)}) collective-permute-start(f32[64,8,128]{2,1,0:T(8,128)S(1)} %get-tuple-element.101), channel_id=1, source_target_pairs={{0,2},{1,3},{2,0},{3,1},{4,6},{5,7},{6,4},{7,5},{8,10},{9,11},{10,... | collective-permute-start | bytes 786440 | tf_op jit(solution)/shard_map/ppermute | solution.py:434
  26.8 6.7 %collective-permute-start.6 = (f32[16,24,128]{2,1,0:T(8,128)S(1)}, f32[16,24,128]{2,1,0:T(8,128)S(1)}, u32[]{:S(2)}, u32[]{:S(2)}) collective-permute-start(f32[16,24,128]{2,1,0:T(8,128)S(1)} %get-tuple-element.102), channel_id=1, source_target_pairs={{0,4},{1,5},{2,6},{3,7},{4,0},{5,1},{6,2},{7,3},{8,12},{9,13},{10,... | collective-permute-start | bytes 589832 | tf_op jit(solution)/shard_map/ppermute | solution.py:434
  28.8 4.7 %collective-permute-start.7 = (f32[16,24,128]{2,1,0:T(8,128)S(1)}, f32[16,24,128]{2,1,0:T(8,128)S(1)}, u32[]{:S(2)}, u32[]{:S(2)}) collective-permute-start(f32[16,24,128]{2,1,0:T(8,128)S(1)} %get-tuple-element.103), channel_id=1, source_target_pairs={{0,1},{1,0},{2,3},{3,2},{4,8},{5,9},{6,10},{7,11},{8,4},{9,5},{10,... | collective-permute-start | bytes 589832 | tf_op jit(solution)/shard_map/ppermute | solution.py:434
  28.8 4.6 %collective-permute-start.8 = (f32[4,8,128]{2,1,0:T(8,128)S(1)}, f32[4,8,128]{2,1,0:T(8,128)S(1)}, u32[]{:S(2)}, u32[]{:S(2)}) collective-permute-start(f32[4,8,128]{2,1,0:T(8,128)S(1)} %get-tuple-element.104), channel_id=1, source_target_pairs={{0,6},{1,7},{2,4},{3,5},{4,2},{5,3},{6,0},{7,1},{8,14},{9,15},{10,... | collective-permute-start | bytes 49160 | tf_op jit(solution)/shard_map/ppermute | solution.py:434
  31.5 2.0 %collective-permute-start.9 = (f32[4,8,128]{2,1,0:T(8,128)S(1)}, f32[4,8,128]{2,1,0:T(8,128)S(1)}, u32[]{:S(2)}, u32[]{:S(2)}) collective-permute-start(f32[4,8,128]{2,1,0:T(8,128)S(1)} %get-tuple-element.105), channel_id=1, source_target_pairs={{0,1},{1,0},{2,3},{3,2},{4,10},{5,11},{6,8},{7,9},{8,6},{9,7},{10,... | collective-permute-start | bytes 49160 | tf_op jit(solution)/shard_map/ppermute | solution.py:434
  37.5 8.5 %collective-permute-start.10 = (f32[64,8,128]{2,1,0:T(8,128)S(1)}, f32[64,8,128]{2,1,0:T(8,128)S(1)}, u32[]{:S(2)}, u32[]{:S(2)}) collective-permute-start(f32[64,8,128]{2,1,0:T(8,128)S(1)} %get-tuple-element.111), channel_id=1, source_target_pairs={{0,2},{1,3},{2,0},{3,1},{4,6},{5,7},{6,4},{7,5},{8,10},{9,11},{10,... | collective-permute-start | bytes 786440 | tf_op jit(solution)/shard_map/ppermute | solution.py:434
  38.8 7.2 %collective-permute-start.11 = (f32[16,24,128]{2,1,0:T(8,128)S(1)}, f32[16,24,128]{2,1,0:T(8,128)S(1)}, u32[]{:S(2)}, u32[]{:S(2)}) collective-permute-start(f32[16,24,128]{2,1,0:T(8,128)S(1)} %get-tuple-element.112), channel_id=1, source_target_pairs={{0,4},{1,5},{2,6},{3,7},{4,0},{5,1},{6,2},{7,3},{8,12},{9,13},{10,... | collective-permute-start | bytes 589832 | tf_op jit(solution)/shard_map/ppermute | solution.py:434
  41.1 4.9 %collective-permute-start.12 = (f32[16,24,128]{2,1,0:T(8,128)S(1)}, f32[16,24,128]{2,1,0:T(8,128)S(1)}, u32[]{:S(2)}, u32[]{:S(2)}) collective-permute-start(f32[16,24,128]{2,1,0:T(8,128)S(1)} %get-tuple-element.113), channel_id=1, source_target_pairs={{0,1},{1,0},{2,3},{3,2},{4,8},{5,9},{6,10},{7,11},{8,4},{9,5},{10,... | collective-permute-start | bytes 589832 | tf_op jit(solution)/shard_map/ppermute | solution.py:434
  41.1 4.9 %collective-permute-start.13 = (f32[4,8,128]{2,1,0:T(8,128)S(1)}, f32[4,8,128]{2,1,0:T(8,128)S(1)}, u32[]{:S(2)}, u32[]{:S(2)}) collective-permute-start(f32[4,8,128]{2,1,0:T(8,128)S(1)} %get-tuple-element.114), channel_id=1, source_target_pairs={{0,6},{1,7},{2,4},{3,5},{4,2},{5,3},{6,0},{7,1},{8,14},{9,15},{10,... | collective-permute-start | bytes 49160 | tf_op jit(solution)/shard_map/ppermute | solution.py:434
  43.1 2.9 %collective-permute-start.14 = (f32[4,8,128]{2,1,0:T(8,128)S(1)}, f32[4,8,128]{2,1,0:T(8,128)S(1)}, u32[]{:S(2)}, u32[]{:S(2)}) collective-permute-start(f32[4,8,128]{2,1,0:T(8,128)S(1)} %get-tuple-element.115), channel_id=1, source_target_pairs={{0,1},{1,0},{2,3},{3,2},{4,10},{5,11},{6,8},{7,9},{8,6},{9,7},{10,... | collective-permute-start | bytes 49160 | tf_op jit(solution)/shard_map/ppermute | solution.py:434
  50.0 8.7 %collective-permute-start.15 = (f32[64,8,128]{2,1,0:T(8,128)S(1)}, f32[64,8,128]{2,1,0:T(8,128)S(1)}, u32[]{:S(2)}, u32[]{:S(2)}) collective-permute-start(f32[64,8,128]{2,1,0:T(8,128)S(1)} %get-tuple-element.121), channel_id=1, source_target_pairs={{0,2},{1,3},{2,0},{3,1},{4,6},{5,7},{6,4},{7,5},{8,10},{9,11},{10,... | collective-permute-start | bytes 786440 | tf_op jit(solution)/shard_map/ppermute | solution.py:434
  51.3 7.4 %collective-permute-start.16 = (f32[16,24,128]{2,1,0:T(8,128)S(1)}, f32[16,24,128]{2,1,0:T(8,128)S(1)}, u32[]{:S(2)}, u32[]{:S(2)}) collective-permute-start(f32[16,24,128]{2,1,0:T(8,128)S(1)} %get-tuple-element.122), channel_id=1, source_target_pairs={{0,4},{1,5},{2,6},{3,7},{4,0},{5,1},{6,2},{7,3},{8,12},{9,13},{10,... | collective-permute-start | bytes 589832 | tf_op jit(solution)/shard_map/ppermute | solution.py:434
  53.4 5.3 %collective-permute-start.17 = (f32[16,24,128]{2,1,0:T(8,128)S(1)}, f32[16,24,128]{2,1,0:T(8,128)S(1)}, u32[]{:S(2)}, u32[]{:S(2)}) collective-permute-start(f32[16,24,128]{2,1,0:T(8,128)S(1)} %get-tuple-element.123), channel_id=1, source_target_pairs={{0,1},{1,0},{2,3},{3,2},{4,8},{5,9},{6,10},{7,11},{8,4},{9,5},{10,... | collective-permute-start | bytes 589832 | tf_op jit(solution)/shard_map/ppermute | solution.py:434
  53.4 5.3 %collective-permute-start.18 = (f32[4,8,128]{2,1,0:T(8,128)S(1)}, f32[4,8,128]{2,1,0:T(8,128)S(1)}, u32[]{:S(2)}, u32[]{:S(2)}) collective-permute-start(f32[4,8,128]{2,1,0:T(8,128)S(1)} %get-tuple-element.124), channel_id=1, source_target_pairs={{0,6},{1,7},{2,4},{3,5},{4,2},{5,3},{6,0},{7,1},{8,14},{9,15},{10,... | collective-permute-start | bytes 49160 | tf_op jit(solution)/shard_map/ppermute | solution.py:434
  55.4 3.3 %collective-permute-start.19 = (f32[4,8,128]{2,1,0:T(8,128)S(1)}, f32[4,8,128]{2,1,0:T(8,128)S(1)}, u32[]{:S(2)}, u32[]{:S(2)}) collective-permute-start(f32[4,8,128]{2,1,0:T(8,128)S(1)} %get-tuple-element.125), channel_id=1, source_target_pairs={{0,1},{1,0},{2,3},{3,2},{4,10},{5,11},{6,8},{7,9},{8,6},{9,7},{10,... | collective-permute-start | bytes 49160 | tf_op jit(solution)/shard_map/ppermute | solution.py:434
  62.7 8.5 %collective-permute-start.20 = (f32[64,8,128]{2,1,0:T(8,128)S(1)}, f32[64,8,128]{2,1,0:T(8,128)S(1)}, u32[]{:S(2)}, u32[]{:S(2)}) collective-permute-start(f32[64,8,128]{2,1,0:T(8,128)S(1)} %get-tuple-element.131), channel_id=1, source_target_pairs={{0,2},{1,3},{2,0},{3,1},{4,6},{5,7},{6,4},{7,5},{8,10},{9,11},{10,... | collective-permute-start | bytes 786440 | tf_op jit(solution)/shard_map/ppermute | solution.py:434
  63.6 7.5 %collective-permute-start.21 = (f32[16,24,128]{2,1,0:T(8,128)S(1)}, f32[16,24,128]{2,1,0:T(8,128)S(1)}, u32[]{:S(2)}, u32[]{:S(2)}) collective-permute-start(f32[16,24,128]{2,1,0:T(8,128)S(1)} %get-tuple-element.132), channel_id=1, source_target_pairs={{0,4},{1,5},{2,6},{3,7},{4,0},{5,1},{6,2},{7,3},{8,12},{9,13},{10,... | collective-permute-start | bytes 589832 | tf_op jit(solution)/shard_map/ppermute | solution.py:434
  65.9 5.2 %collective-permute-start.22 = (f32[16,24,128]{2,1,0:T(8,128)S(1)}, f32[16,24,128]{2,1,0:T(8,128)S(1)}, u32[]{:S(2)}, u32[]{:S(2)}) collective-permute-start(f32[16,24,128]{2,1,0:T(8,128)S(1)} %get-tuple-element.133), channel_id=1, source_target_pairs={{0,1},{1,0},{2,3},{3,2},{4,8},{5,9},{6,10},{7,11},{8,4},{9,5},{10,... | collective-permute-start | bytes 589832 | tf_op jit(solution)/shard_map/ppermute | solution.py:434
  65.9 5.2 %collective-permute-start.23 = (f32[4,8,128]{2,1,0:T(8,128)S(1)}, f32[4,8,128]{2,1,0:T(8,128)S(1)}, u32[]{:S(2)}, u32[]{:S(2)}) collective-permute-start(f32[4,8,128]{2,1,0:T(8,128)S(1)} %get-tuple-element.134), channel_id=1, source_target_pairs={{0,6},{1,7},{2,4},{3,5},{4,2},{5,3},{6,0},{7,1},{8,14},{9,15},{10,... | collective-permute-start | bytes 49160 | tf_op jit(solution)/shard_map/ppermute | solution.py:434
  67.6 3.5 %collective-permute-start.24 = (f32[4,8,128]{2,1,0:T(8,128)S(1)}, f32[4,8,128]{2,1,0:T(8,128)S(1)}, u32[]{:S(2)}, u32[]{:S(2)}) collective-permute-start(f32[4,8,128]{2,1,0:T(8,128)S(1)} %get-tuple-element.135), channel_id=1, source_target_pairs={{0,1},{1,0},{2,3},{3,2},{4,10},{5,11},{6,8},{7,9},{8,6},{9,7},{10,... | collective-permute-start | bytes 49160 | tf_op jit(solution)/shard_map/ppermute | solution.py:434
  75.1 8.4 %collective-permute-start.25 = (f32[64,8,128]{2,1,0:T(8,128)S(1)}, f32[64,8,128]{2,1,0:T(8,128)S(1)}, u32[]{:S(2)}, u32[]{:S(2)}) collective-permute-start(f32[64,8,128]{2,1,0:T(8,128)S(1)} %get-tuple-element.141), channel_id=1, source_target_pairs={{0,2},{1,3},{2,0},{3,1},{4,6},{5,7},{6,4},{7,5},{8,10},{9,11},{10,... | collective-permute-start | bytes 786440 | tf_op jit(solution)/shard_map/ppermute | solution.py:434
  76.0 7.5 %collective-permute-start.26 = (f32[16,24,128]{2,1,0:T(8,128)S(1)}, f32[16,24,128]{2,1,0:T(8,128)S(1)}, u32[]{:S(2)}, u32[]{:S(2)}) collective-permute-start(f32[16,24,128]{2,1,0:T(8,128)S(1)} %get-tuple-element.142), channel_id=1, source_target_pairs={{0,4},{1,5},{2,6},{3,7},{4,0},{5,1},{6,2},{7,3},{8,12},{9,13},{10,... | collective-permute-start | bytes 589832 | tf_op jit(solution)/shard_map/ppermute | solution.py:434
  78.1 5.4 %collective-permute-start.27 = (f32[16,24,128]{2,1,0:T(8,128)S(1)}, f32[16,24,128]{2,1,0:T(8,128)S(1)}, u32[]{:S(2)}, u32[]{:S(2)}) collective-permute-start(f32[16,24,128]{2,1,0:T(8,128)S(1)} %get-tuple-element.143), channel_id=1, source_target_pairs={{0,1},{1,0},{2,3},{3,2},{4,8},{5,9},{6,10},{7,11},{8,4},{9,5},{10,... | collective-permute-start | bytes 589832 | tf_op jit(solution)/shard_map/ppermute | solution.py:434
  78.1 5.4 %collective-permute-start.28 = (f32[4,8,128]{2,1,0:T(8,128)S(1)}, f32[4,8,128]{2,1,0:T(8,128)S(1)}, u32[]{:S(2)}, u32[]{:S(2)}) collective-permute-start(f32[4,8,128]{2,1,0:T(8,128)S(1)} %get-tuple-element.144), channel_id=1, source_target_pairs={{0,6},{1,7},{2,4},{3,5},{4,2},{5,3},{6,0},{7,1},{8,14},{9,15},{10,... | collective-permute-start | bytes 49160 | tf_op jit(solution)/shard_map/ppermute | solution.py:434
  80.0 3.5 %collective-permute-start.29 = (f32[4,8,128]{2,1,0:T(8,128)S(1)}, f32[4,8,128]{2,1,0:T(8,128)S(1)}, u32[]{:S(2)}, u32[]{:S(2)}) collective-permute-start(f32[4,8,128]{2,1,0:T(8,128)S(1)} %get-tuple-element.145), channel_id=1, source_target_pairs={{0,1},{1,0},{2,3},{3,2},{4,10},{5,11},{6,8},{7,9},{8,6},{9,7},{10,... | collective-permute-start | bytes 49160 | tf_op jit(solution)/shard_map/ppermute | solution.py:434
  87.4 1.5 %collective-permute-start.30 = (f32[16,24,128]{2,1,0:T(8,128)S(1)}, f32[16,24,128]{2,1,0:T(8,128)S(1)}, u32[]{:S(2)}, u32[]{:S(2)}) collective-permute-start(f32[16,24,128]{2,1,0:T(8,128)S(1)} %get-tuple-element.156), channel_id=1, source_target_pairs={{0,1},{1,0},{2,3},{3,2},{4,5},{5,4},{6,7},{7,6},{8,9},{9,8},{10,11... | collective-permute-start | bytes 589832 | tf_op jit(solution)/shard_map/ppermute | solution.py:488

commit v2 on v1

--- a/solution.py
+++ b/solution.py
@@ -117,7 +117,7 @@
                 my[f * nx + x, 4 * i : 4 * i + 4, :] = u[x + HALO, pl.ds(4 + i - 2 * p, 4, stride=SUB), :]
         return carry
 
-    lax.fori_loop(0, nx, ybody, 0, unroll=4)
+    lax.fori_loop(0, nx, ybody, 0, unroll=16)
     if extras:
 
         def yextra(h, carry):
@@ -138,7 +138,7 @@
                     mx[f * HALO + i, 4 * q : 4 * q + 4, :] = u[wide + i, pl.ds(2 * p + q, 4, stride=SUB), :]
             return carry
 
-        lax.fori_loop(0, HALO, xbody, 0, unroll=2)
+        lax.fori_loop(0, HALO, xbody, 0, unroll=8)
         for i in range(RADIUS):
             for f, u in enumerate(extras):
                 for q in range(geo.srows):
@@ -159,7 +159,7 @@
                 u[x + HALO, pl.ds(6 + i - 6 * p, 4, stride=SUB), :] = my[f * nx + x, 4 * i : 4 * i + 4, :]
         return carry
 
-    lax.fori_loop(0, nx, ybody, 0, unroll=4)
+    lax.fori_loop(0, nx, ybody, 0, unroll=16)
     if extras:
 
         def yextra(h, carry):
@@ -183,7 +183,7 @@
                         u[wide + i, pl.ds(2 * p + q, 4, stride=SUB), :] = mx[f * HALO + i, 4 * q : 4 * q + 4, :]
                 return carry
 
-            lax.fori_loop(0, HALO, xbody, 0, unroll=2)
+            lax.fori_loop(0, HALO, xbody, 0, unroll=8)
             for i in range(RADIUS):
                 for f, u in enumerate(extras):
                     for q in range(geo.srows):
@@ -239,7 +239,7 @@
 
 def receiver_kernel(geo, nrec):
     rows_all = geo.xe * geo.win
-    block = 128
+    block = 256
 
     def body(ri, rc, traces, wavelet, out, wav, table):
         p, g, _ = geo.place()
@@ -253,14 +253,17 @@
         table[0:STEPS, :] = traces[0] * (1.0 / COEFFS[1])
         wav[...] = jnp.zeros_like(wav)
         wav[0:1, 0:STEPS] = wavelet[...] * (1.0 / COEFFS[1])
-        tab = table[...]
+        part, left = [], table[...]
+        for _ in range(3):
+            part.append(left.astype(jnp.bfloat16))
+            left = left - part[-1].astype(F32)
+        parts = jnp.concatenate(part, axis=1)
 
         def chunk(i, carry):
             at = i * block + lax.broadcasted_iota(jnp.int32, (block, nrec), 0)
-            hot = jnp.where(at == row, 1.0, 0.0).astype(F32)
-            plane = lax.dot_general(
-                hot, tab, (((1,), (1,)), ((), ())), precision=lax.Precision.HIGHEST, preferred_element_type=F32
-            )
+            hot = jnp.where(at == row, 1.0, 0.0).astype(jnp.bfloat16)
+            hots = jnp.concatenate([hot, hot, hot], axis=1)
+            plane = lax.dot_general(hots, parts, (((1,), (1,)), ((), ())), preferred_element_type=F32)
             planes = block // geo.win
             out[pl.ds(i * planes, planes)] = plane.reshape(planes, geo.win, LANES)
             return carry
@@ -438,7 +441,7 @@
             + [jax.ShapeDtypeStruct((2 * LANES, LANES), jnp.bfloat16)]
             + message_shapes(geo, True),
             [HBM] * 5,
-            (sn, sl, rn, rl, courant),
+            tuple(pltpu.with_memory_space_constraint(v, pltpu.HBM) for v in (sn, sl, rn, rl, courant)),
             scratch=[pltpu.VMEM((5, nx, geo.win, nz), F32), pltpu.SemaphoreType.DMA((5,))],
         )
         us, ur, ps, pr, cc, dw = loaded[:6]

time: 90 us -> 84.7 us (0.941)
  local copies, waits for them, and re-layouts: 5.63 us -> 0.66 us
  Pallas kernels: 29.6 us -> 28.2 us
  starting transfers between devices: 35.1 us -> 36.1 us
    unnamed x19 -> x9, local copies, waits for them, and re-layouts: 5.63 us -> 0.66 us
    pallas_call x10, Pallas kernels: 29.6 us -> 28.2 us  [call(): pl.pallas_call(body, out_shape=out_shapes, in_specs=specs, out_specs=out_...]
    ppermute x30, starting transfers between devices: 35.1 us -> 36 us  [run(): lax.ppermute(m, names, route)]
  transfers between devices with their start and end apart: 31 -> 31, of which waited for: 7 -> 8; matrix products, arithmetic and copies ran while one was open for 0% -> 0% of each run, Pallas kernels for 5% -> 3%
where the time goes in v2:
time: 84.7 us; the launch traced here: 84.4 us
  starting transfers between devices  36.1 us (43%)
  Pallas kernels  28.2 us (33%)
  waiting for transfers between devices  16.7 us (20%)
  between operations  2.16 us (3%)
    ppermute x30, starting transfers between devices, run(): lax.ppermute(m, names, route)  36 us
    pallas_call x10, Pallas kernels, call(): pl.pallas_call(body, out_shape=out_shapes, in_specs=specs, out_specs=out_...  28.2 us
    ppermute x30, waiting for transfers between devices, run(): lax.ppermute(m, names, route)  16.5 us
  transfers between devices with their start and end apart: 31, of which 8 were waited for; matrix products, arithmetic and copies ran while one was open for 0% of the time, Pallas kernels for 3%

profile of v2, /device:TPU:0, one launch (start us, length us, event | category | flops | bytes accessed | tf_op | source)
XLA Modules:
  0.0 84.4 jit_solution(7000878871528004721)
XLA Ops:
  0.6 2.0 %shard_map.146 = (f32[48,32,128]{2,1,0:T(8,128)S(1)}, f32[48,32,128]{2,1,0:T(8,128)S(1)}, f32[48,32,128]{2,1,0:T(8,128)S(1)}, f32[48,32,128]{2,1,0:T(8,128)S(1)}...) custom-call(f32[1,32,24,128]{3,2,1,0:T(8,128)} %s0.1, ...), custom_call_target="tpu_custom_call" | custom-call | tf_op jit(solution)/shard_map/pallas_call | solution.py:86
  2.7 0.0 copy-start.3
  2.7 3.0 %collective-permute-start = (f32[112,8,128]{2,1,0:T(8,128)S(1)}, f32[112,8,128]{2,1,0:T(8,128)S(1)}, u32[]{:S(2)}, u32[]{:S(2)}) collective-permute-start(f32[112,8,128]{2,1,0:T(8,128)S(1)} %get-tuple-element.89), channel_id=1, source_target_pairs={{0,2},{1,3},{2,0},{3,1},{4,6},{5,7},{6,4},{7,5},{8,10},{9,11},{10,... | collective-permute-start | bytes 1376264 | tf_op jit(solution)/shard_map/ppermute | solution.py:437
  5.7 1.6 %collective-permute-start.1 = (f32[28,24,128]{2,1,0:T(8,128)S(1)}, f32[28,24,128]{2,1,0:T(8,128)S(1)}, u32[]{:S(2)}, u32[]{:S(2)}) collective-permute-start(f32[28,24,128]{2,1,0:T(8,128)S(1)} %get-tuple-element.90), channel_id=1, source_target_pairs={{0,4},{1,5},{2,6},{3,7},{4,0},{5,1},{6,2},{7,3},{8,12},{9,13},{10,... | collective-permute-start | bytes 1032200 | tf_op jit(solution)/shard_map/ppermute | solution.py:437
  7.3 0.0 collective-permute-start.2
  7.3 3.1 %collective-permute-start.3 = (f32[4,8,128]{2,1,0:T(8,128)S(1)}, f32[4,8,128]{2,1,0:T(8,128)S(1)}, u32[]{:S(2)}, u32[]{:S(2)}) collective-permute-start(f32[4,8,128]{2,1,0:T(8,128)S(1)} %get-tuple-element.92), channel_id=1, source_target_pairs={{0,6},{1,7},{2,4},{3,5},{4,2},{5,3},{6,0},{7,1},{8,14},{9,15},{10,... | collective-permute-start | bytes 49160 | tf_op jit(solution)/shard_map/ppermute | solution.py:437
  10.4 0.0 collective-permute-start.4
  11.7 0.0 copy-start
  11.7 0.0 copy-start.1
  11.7 0.0 copy-start.2
  11.8 0.6 copy-done
  12.4 0.0 copy-done.1
  12.4 0.0 copy-done.2
  12.4 1.5 %shard_map.147 = (f32[48,32,128]{2,1,0:T(8,128)S(1)}, f32[8,128]{1,0:T(8,128)S(1)}) custom-call(s32[1,64]{1,0:T(1,128)S(1)} %copy-done, s32[1,64]{1,0:T(1,128)S(1)} %copy-done.1, f32[1,12,64]{2,1,0:T(8,128)S(1)} %copy.46.traces, f32[1,12]{1,0:T(1,128)S(1)} %copy-done.2), custom_call_target="tpu_custom_call" | custom-call | tf_op jit(solution)/shard_map/pallas_call | solution.py:86
  13.9 1.6 %collective-permute-done.3.refs_11_ = f32[4,8,128]{2,1,0:T(8,128)S(1)} collective-permute-done((f32[4,8,128]{2,1,0:T(8,128)S(1)}, f32[4,8,128]{2,1,0:T(8,128)S(1)}, u32[]{:S(2)}, u32[]{:S(2)}) %collective-permute-start.3) | collective-permute-done | bytes 16416 | tf_op jit(solution)/shard_map/ppermute | solution.py:437
  15.5 0.0 collective-permute-done.4.refs_12_
  15.5 1.1 %collective-permute-done.refs_8_ = f32[112,8,128]{2,1,0:T(8,128)S(1)} collective-permute-done((f32[112,8,128]{2,1,0:T(8,128)S(1)}, f32[112,8,128]{2,1,0:T(8,128)S(1)}, u32[]{:S(2)}, u32[]{:S(2)}) %collective-permute-start) | collective-permute-done | bytes 458784 | tf_op jit(solution)/shard_map/ppermute | solution.py:437
  16.6 4.2 %shard_map.148 = (f32[48,32,128]{2,1,0:T(8,128)S(1)}, f32[48,32,128]{2,1,0:T(8,128)S(1)}, f32[48,32,128]{2,1,0:T(8,128)S(1)}, f32[48,32,128]{2,1,0:T(8,128)S(1)}...) custom-call(f32[48,32,128]{2,1,0:T(8,128)S(1)} %get-tuple-element.81, ...), custom_call_target="tpu_custom_call", output_to_operand_aliasing={{0}: (0, {}), {1}: (1, {}), {2}: (2, {}), {3}: (3, {}), {4}... | custom-call | tf_op jit(solution)/shard_map/pallas_call | solution.py:86
  20.8 1.8 %collective-permute-start.5 = (f32[64,8,128]{2,1,0:T(8,128)S(1)}, f32[64,8,128]{2,1,0:T(8,128)S(1)}, u32[]{:S(2)}, u32[]{:S(2)}) collective-permute-start(f32[64,8,128]{2,1,0:T(8,128)S(1)} %get-tuple-element.101), channel_id=1, source_target_pairs={{0,2},{1,3},{2,0},{3,1},{4,6},{5,7},{6,4},{7,5},{8,10},{9,11},{10,... | collective-permute-start | bytes 786440 | tf_op jit(solution)/shard_map/ppermute | solution.py:437
  22.6 2.0 %collective-permute-start.6 = (f32[16,24,128]{2,1,0:T(8,128)S(1)}, f32[16,24,128]{2,1,0:T(8,128)S(1)}, u32[]{:S(2)}, u32[]{:S(2)}) collective-permute-start(f32[16,24,128]{2,1,0:T(8,128)S(1)} %get-tuple-element.102), channel_id=1, source_target_pairs={{0,4},{1,5},{2,6},{3,7},{4,0},{5,1},{6,2},{7,3},{8,12},{9,13},{10,... | collective-permute-start | bytes 589832 | tf_op jit(solution)/shard_map/ppermute | solution.py:437
  24.6 2.8 %collective-permute-start.8 = (f32[4,8,128]{2,1,0:T(8,128)S(1)}, f32[4,8,128]{2,1,0:T(8,128)S(1)}, u32[]{:S(2)}, u32[]{:S(2)}) collective-permute-start(f32[4,8,128]{2,1,0:T(8,128)S(1)} %get-tuple-element.104), channel_id=1, source_target_pairs={{0,6},{1,7},{2,4},{3,5},{4,2},{5,3},{6,0},{7,1},{8,14},{9,15},{10,... | collective-permute-start | bytes 49160 | tf_op jit(solution)/shard_map/ppermute | solution.py:437
  27.4 1.8 %collective-permute-done.8.refs_13_ = f32[4,8,128]{2,1,0:T(8,128)S(1)} collective-permute-done((f32[4,8,128]{2,1,0:T(8,128)S(1)}, f32[4,8,128]{2,1,0:T(8,128)S(1)}, u32[]{:S(2)}, u32[]{:S(2)}) %collective-permute-start.8) | collective-permute-done | bytes 16416 | tf_op jit(solution)/shard_map/ppermute | solution.py:437
  29.2 3.9 %shard_map.149 = (f32[48,32,128]{2,1,0:T(8,128)S(1)}, f32[48,32,128]{2,1,0:T(8,128)S(1)}, f32[48,32,128]{2,1,0:T(8,128)S(1)}, f32[48,32,128]{2,1,0:T(8,128)S(1)}...) custom-call(f32[48,32,128]{2,1,0:T(8,128)S(1)} %get-tuple-element.94, ...), custom_call_target="tpu_custom_call", output_to_operand_aliasing={{0}: (0, {}), {1}: (1, {}), {2}: (2, {}), {3}: (3, {}), {4}... | custom-call | tf_op jit(solution)/shard_map/pallas_call | solution.py:86
  33.1 1.3 %collective-permute-start.10 = (f32[64,8,128]{2,1,0:T(8,128)S(1)}, f32[64,8,128]{2,1,0:T(8,128)S(1)}, u32[]{:S(2)}, u32[]{:S(2)}) collective-permute-start(f32[64,8,128]{2,1,0:T(8,128)S(1)} %get-tuple-element.111), channel_id=1, source_target_pairs={{0,2},{1,3},{2,0},{3,1},{4,6},{5,7},{6,4},{7,5},{8,10},{9,11},{10,... | collective-permute-start | bytes 786440 | tf_op jit(solution)/shard_map/ppermute | solution.py:437
  34.5 2.4 %collective-permute-start.11 = (f32[16,24,128]{2,1,0:T(8,128)S(1)}, f32[16,24,128]{2,1,0:T(8,128)S(1)}, u32[]{:S(2)}, u32[]{:S(2)}) collective-permute-start(f32[16,24,128]{2,1,0:T(8,128)S(1)} %get-tuple-element.112), channel_id=1, source_target_pairs={{0,4},{1,5},{2,6},{3,7},{4,0},{5,1},{6,2},{7,3},{8,12},{9,13},{10,... | collective-permute-start | bytes 589832 | tf_op jit(solution)/shard_map/ppermute | solution.py:437
  36.8 2.1 %collective-permute-start.13 = (f32[4,8,128]{2,1,0:T(8,128)S(1)}, f32[4,8,128]{2,1,0:T(8,128)S(1)}, u32[]{:S(2)}, u32[]{:S(2)}) collective-permute-start(f32[4,8,128]{2,1,0:T(8,128)S(1)} %get-tuple-element.114), channel_id=1, source_target_pairs={{0,6},{1,7},{2,4},{3,5},{4,2},{5,3},{6,0},{7,1},{8,14},{9,15},{10,... | collective-permute-start | bytes 49160 | tf_op jit(solution)/shard_map/ppermute | solution.py:437
  39.0 2.6 %collective-permute-done.13.refs_13_ = f32[4,8,128]{2,1,0:T(8,128)S(1)} collective-permute-done((f32[4,8,128]{2,1,0:T(8,128)S(1)}, f32[4,8,128]{2,1,0:T(8,128)S(1)}, u32[]{:S(2)}, u32[]{:S(2)}) %collective-permute-start.13) | collective-permute-done | bytes 16416 | tf_op jit(solution)/shard_map/ppermute | solution.py:437
  41.6 3.9 %shard_map.150 = (f32[48,32,128]{2,1,0:T(8,128)S(1)}, f32[48,32,128]{2,1,0:T(8,128)S(1)}, f32[48,32,128]{2,1,0:T(8,128)S(1)}, f32[48,32,128]{2,1,0:T(8,128)S(1)}...) custom-call(f32[48,32,128]{2,1,0:T(8,128)S(1)} %get-tuple-element.10, ...), custom_call_target="tpu_custom_call", output_to_operand_aliasing={{0}: (0, {}), {1}: (1, {}), {2}: (2, {}), {3}: (3, {}), {4}... | custom-call | tf_op jit(solution)/shard_map/pallas_call | solution.py:86
  45.5 1.3 %collective-permute-start.15 = (f32[64,8,128]{2,1,0:T(8,128)S(1)}, f32[64,8,128]{2,1,0:T(8,128)S(1)}, u32[]{:S(2)}, u32[]{:S(2)}) collective-permute-start(f32[64,8,128]{2,1,0:T(8,128)S(1)} %get-tuple-element.121), channel_id=1, source_target_pairs={{0,2},{1,3},{2,0},{3,1},{4,6},{5,7},{6,4},{7,5},{8,10},{9,11},{10,... | collective-permute-start | bytes 786440 | tf_op jit(solution)/shard_map/ppermute | solution.py:437
  46.8 2.2 %collective-permute-start.16 = (f32[16,24,128]{2,1,0:T(8,128)S(1)}, f32[16,24,128]{2,1,0:T(8,128)S(1)}, u32[]{:S(2)}, u32[]{:S(2)}) collective-permute-start(f32[16,24,128]{2,1,0:T(8,128)S(1)} %get-tuple-element.122), channel_id=1, source_target_pairs={{0,4},{1,5},{2,6},{3,7},{4,0},{5,1},{6,2},{7,3},{8,12},{9,13},{10,... | collective-permute-start | bytes 589832 | tf_op jit(solution)/shard_map/ppermute | solution.py:437
  48.9 2.1 %collective-permute-start.18 = (f32[4,8,128]{2,1,0:T(8,128)S(1)}, f32[4,8,128]{2,1,0:T(8,128)S(1)}, u32[]{:S(2)}, u32[]{:S(2)}) collective-permute-start(f32[4,8,128]{2,1,0:T(8,128)S(1)} %get-tuple-element.124), channel_id=1, source_target_pairs={{0,6},{1,7},{2,4},{3,5},{4,2},{5,3},{6,0},{7,1},{8,14},{9,15},{10,... | collective-permute-start | bytes 49160 | tf_op jit(solution)/shard_map/ppermute | solution.py:437
  51.0 3.1 %collective-permute-done.18.refs_13_ = f32[4,8,128]{2,1,0:T(8,128)S(1)} collective-permute-done((f32[4,8,128]{2,1,0:T(8,128)S(1)}, f32[4,8,128]{2,1,0:T(8,128)S(1)}, u32[]{:S(2)}, u32[]{:S(2)}) %collective-permute-start.18) | collective-permute-done | bytes 16416 | tf_op jit(solution)/shard_map/ppermute | solution.py:437
  54.2 3.9 %shard_map.151 = (f32[48,32,128]{2,1,0:T(8,128)S(1)}, f32[48,32,128]{2,1,0:T(8,128)S(1)}, f32[48,32,128]{2,1,0:T(8,128)S(1)}, f32[48,32,128]{2,1,0:T(8,128)S(1)}...) custom-call(f32[48,32,128]{2,1,0:T(8,128)S(1)} %get-tuple-element.11, ...), custom_call_target="tpu_custom_call", output_to_operand_aliasing={{0}: (0, {}), {1}: (1, {}), {2}: (2, {}), {3}: (3, {}), {4}... | custom-call | tf_op jit(solution)/shard_map/pallas_call | solution.py:86
  58.0 0.9 %collective-permute-start.20 = (f32[64,8,128]{2,1,0:T(8,128)S(1)}, f32[64,8,128]{2,1,0:T(8,128)S(1)}, u32[]{:S(2)}, u32[]{:S(2)}) collective-permute-start(f32[64,8,128]{2,1,0:T(8,128)S(1)} %get-tuple-element.131), channel_id=1, source_target_pairs={{0,2},{1,3},{2,0},{3,1},{4,6},{5,7},{6,4},{7,5},{8,10},{9,11},{10,... | collective-permute-start | bytes 786440 | tf_op jit(solution)/shard_map/ppermute | solution.py:437
  58.9 2.2 %collective-permute-start.21 = (f32[16,24,128]{2,1,0:T(8,128)S(1)}, f32[16,24,128]{2,1,0:T(8,128)S(1)}, u32[]{:S(2)}, u32[]{:S(2)}) collective-permute-start(f32[16,24,128]{2,1,0:T(8,128)S(1)} %get-tuple-element.132), channel_id=1, source_target_pairs={{0,4},{1,5},{2,6},{3,7},{4,0},{5,1},{6,2},{7,3},{8,12},{9,13},{10,... | collective-permute-start | bytes 589832 | tf_op jit(solution)/shard_map/ppermute | solution.py:437
  61.2 2.0 %collective-permute-start.23 = (f32[4,8,128]{2,1,0:T(8,128)S(1)}, f32[4,8,128]{2,1,0:T(8,128)S(1)}, u32[]{:S(2)}, u32[]{:S(2)}) collective-permute-start(f32[4,8,128]{2,1,0:T(8,128)S(1)} %get-tuple-element.134), channel_id=1, source_target_pairs={{0,6},{1,7},{2,4},{3,5},{4,2},{5,3},{6,0},{7,1},{8,14},{9,15},{10,... | collective-permute-start | bytes 49160 | tf_op jit(solution)/shard_map/ppermute | solution.py:437
  63.2 3.3 %collective-permute-done.23.refs_13_ = f32[4,8,128]{2,1,0:T(8,128)S(1)} collective-permute-done((f32[4,8,128]{2,1,0:T(8,128)S(1)}, f32[4,8,128]{2,1,0:T(8,128)S(1)}, u32[]{:S(2)}, u32[]{:S(2)}) %collective-permute-start.23) | collective-permute-done | bytes 16416 | tf_op jit(solution)/shard_map/ppermute | solution.py:437
  66.5 3.9 %shard_map.152 = (f32[48,32,128]{2,1,0:T(8,128)S(1)}, f32[48,32,128]{2,1,0:T(8,128)S(1)}, f32[48,32,128]{2,1,0:T(8,128)S(1)}, f32[48,32,128]{2,1,0:T(8,128)S(1)}...) custom-call(f32[48,32,128]{2,1,0:T(8,128)S(1)} %get-tuple-element.12, ...), custom_call_target="tpu_custom_call", output_to_operand_aliasing={{0}: (0, {}), {1}: (1, {}), {2}: (2, {}), {3}: (3, {}), {4}... | custom-call | tf_op jit(solution)/shard_map/pallas_call | solution.py:86
  70.3 0.8 collective-permute-start.25
  71.1 2.3 %collective-permute-start.26 = (f32[16,24,128]{2,1,0:T(8,128)S(1)}, f32[16,24,128]{2,1,0:T(8,128)S(1)}, u32[]{:S(2)}, u32[]{:S(2)}) collective-permute-start(f32[16,24,128]{2,1,0:T(8,128)S(1)} %get-tuple-element.142), channel_id=1, source_target_pairs={{0,4},{1,5},{2,6},{3,7},{4,0},{5,1},{6,2},{7,3},{8,12},{9,13},{10,... | collective-permute-start | bytes 589832 | tf_op jit(solution)/shard_map/ppermute | solution.py:437
  73.4 2.0 %collective-permute-start.28 = (f32[4,8,128]{2,1,0:T(8,128)S(1)}, f32[4,8,128]{2,1,0:T(8,128)S(1)}, u32[]{:S(2)}, u32[]{:S(2)}) collective-permute-start(f32[4,8,128]{2,1,0:T(8,128)S(1)} %get-tuple-element.144), channel_id=1, source_target_pairs={{0,6},{1,7},{2,4},{3,5},{4,2},{5,3},{6,0},{7,1},{8,14},{9,15},{10,... | collective-permute-start | bytes 49160 | tf_op jit(solution)/shard_map/ppermute | solution.py:437
  75.4 2.9 %collective-permute-done.28.refs_13_ = f32[4,8,128]{2,1,0:T(8,128)S(1)} collective-permute-done((f32[4,8,128]{2,1,0:T(8,128)S(1)}, f32[4,8,128]{2,1,0:T(8,128)S(1)}, u32[]{:S(2)}, u32[]{:S(2)}) %collective-permute-start.28) | collective-permute-done | bytes 16416 | tf_op jit(solution)/shard_map/ppermute | solution.py:437
  78.4 3.7 %shard_map.153 = (f32[48,32,128]{2,1,0:T(8,128)S(1)}, f32[48,32,128]{2,1,0:T(8,128)S(1)}, f32[48,32,128]{2,1,0:T(8,128)S(1)}, f32[48,32,128]{2,1,0:T(8,128)S(1)}, f32[40,32,128]{2,1,0:T(8,128)S(1)}) custom-call(f32[48,32,128]{2,1,0:T(8,128)S(1)} %get-tuple-element.136.refs_0_, ...), custom_call_target="tpu_custom_call", output_to_operand_aliasing={{0}: (0, {}), {1}: (1, {}), {2}: (2, {}), {3}: (3, {}), {4}... | custom-call | tf_op jit(solution)/shard_map/pallas_call | solution.py:86
  82.1 0.1 shard_map.155
  82.2 0.1 collective-permute-start.30
  82.3 1.2 %shard_map.154 = (f32[1,32,24,128]{3,2,1,0:T(8,128)}, f32[1,32,24,128]{3,2,1,0:T(8,128)}, f32[1,32,24,128]{3,2,1,0:T(8,128)}, f32[1,32,24,128]{3,2,1,0:T(8,128)}) custom-call(f32[48,32,128]{2,1,0:T(8,128)S(1)} %get-tuple-element.146.us, f32[48,32,128]{2,1,0:T(8,128)S(1)} %get-tuple-element.147.ur, f32[48,32,128]{2,1,0:T(8,128)S(1)} %get-tuple-element.148.ps, ...), custom_call_target="tpu_custom_call" | custom-call | tf_op jit(solution)/shard_map/pallas_call | solution.py:86
  83.6 0.2 collective-permute-done.30
  83.7 0.7 add_multiply_fusion
  (34 shorter events, 0.1 us)
Async XLA Ops:
  2.7 9.1 %copy-start.3 = (f32[1,12,64]{2,0,1:T(1,128)S(1)}, f32[1,12,64]{2,0,1:T(1,128)}, u32[]{:S(2)}) copy-start(f32[1,12,64]{2,0,1:T(1,128)} %param.17) | copy-start | bytes 9220
  2.7 13.9 %collective-permute-start = (f32[112,8,128]{2,1,0:T(8,128)S(1)}, f32[112,8,128]{2,1,0:T(8,128)S(1)}, u32[]{:S(2)}, u32[]{:S(2)}) collective-permute-start(f32[112,8,128]{2,1,0:T(8,128)S(1)} %get-tuple-element.89), channel_id=1, source_target_pairs={{0,2},{1,3},{2,0},{3,1},{4,6},{5,7},{6,4},{7,5},{8,10},{9,11},{10,... | collective-permute-start | bytes 1376264 | tf_op jit(solution)/shard_map/ppermute | solution.py:437
  5.7 9.8 %collective-permute-start.1 = (f32[28,24,128]{2,1,0:T(8,128)S(1)}, f32[28,24,128]{2,1,0:T(8,128)S(1)}, u32[]{:S(2)}, u32[]{:S(2)}) collective-permute-start(f32[28,24,128]{2,1,0:T(8,128)S(1)} %get-tuple-element.90), channel_id=1, source_target_pairs={{0,4},{1,5},{2,6},{3,7},{4,0},{5,1},{6,2},{7,3},{8,12},{9,13},{10,... | collective-permute-start | bytes 1032200 | tf_op jit(solution)/shard_map/ppermute | solution.py:437
  7.3 8.2 %collective-permute-start.2 = (f32[28,24,128]{2,1,0:T(8,128)S(1)}, f32[28,24,128]{2,1,0:T(8,128)S(1)}, u32[]{:S(2)}, u32[]{:S(2)}) collective-permute-start(f32[28,24,128]{2,1,0:T(8,128)S(1)} %get-tuple-element.91), channel_id=1, source_target_pairs={{0,1},{1,0},{2,3},{3,2},{4,8},{5,9},{6,10},{7,11},{8,4},{9,5},{10,... | collective-permute-start | bytes 1032200 | tf_op jit(solution)/shard_map/ppermute | solution.py:437
  7.3 8.2 %collective-permute-start.3 = (f32[4,8,128]{2,1,0:T(8,128)S(1)}, f32[4,8,128]{2,1,0:T(8,128)S(1)}, u32[]{:S(2)}, u32[]{:S(2)}) collective-permute-start(f32[4,8,128]{2,1,0:T(8,128)S(1)} %get-tuple-element.92), channel_id=1, source_target_pairs={{0,6},{1,7},{2,4},{3,5},{4,2},{5,3},{6,0},{7,1},{8,14},{9,15},{10,... | collective-permute-start | bytes 49160 | tf_op jit(solution)/shard_map/ppermute | solution.py:437
  10.4 5.1 %collective-permute-start.4 = (f32[4,8,128]{2,1,0:T(8,128)S(1)}, f32[4,8,128]{2,1,0:T(8,128)S(1)}, u32[]{:S(2)}, u32[]{:S(2)}) collective-permute-start(f32[4,8,128]{2,1,0:T(8,128)S(1)} %get-tuple-element.93), channel_id=1, source_target_pairs={{0,1},{1,0},{2,3},{3,2},{4,10},{5,11},{6,8},{7,9},{8,6},{9,7},{10,... | collective-permute-start | bytes 49160 | tf_op jit(solution)/shard_map/ppermute | solution.py:437
  11.7 0.7 copy-start
  11.7 0.7 copy-start.1
  11.7 0.7 copy-start.2
  20.8 8.5 %collective-permute-start.5 = (f32[64,8,128]{2,1,0:T(8,128)S(1)}, f32[64,8,128]{2,1,0:T(8,128)S(1)}, u32[]{:S(2)}, u32[]{:S(2)}) collective-permute-start(f32[64,8,128]{2,1,0:T(8,128)S(1)} %get-tuple-element.101), channel_id=1, source_target_pairs={{0,2},{1,3},{2,0},{3,1},{4,6},{5,7},{6,4},{7,5},{8,10},{9,11},{10,... | collective-permute-start | bytes 786440 | tf_op jit(solution)/shard_map/ppermute | solution.py:437
  22.6 6.7 %collective-permute-start.6 = (f32[16,24,128]{2,1,0:T(8,128)S(1)}, f32[16,24,128]{2,1,0:T(8,128)S(1)}, u32[]{:S(2)}, u32[]{:S(2)}) collective-permute-start(f32[16,24,128]{2,1,0:T(8,128)S(1)} %get-tuple-element.102), channel_id=1, source_target_pairs={{0,4},{1,5},{2,6},{3,7},{4,0},{5,1},{6,2},{7,3},{8,12},{9,13},{10,... | collective-permute-start | bytes 589832 | tf_op jit(solution)/shard_map/ppermute | solution.py:437
  24.6 4.7 %collective-permute-start.7 = (f32[16,24,128]{2,1,0:T(8,128)S(1)}, f32[16,24,128]{2,1,0:T(8,128)S(1)}, u32[]{:S(2)}, u32[]{:S(2)}) collective-permute-start(f32[16,24,128]{2,1,0:T(8,128)S(1)} %get-tuple-element.103), channel_id=1, source_target_pairs={{0,1},{1,0},{2,3},{3,2},{4,8},{5,9},{6,10},{7,11},{8,4},{9,5},{10,... | collective-permute-start | bytes 589832 | tf_op jit(solution)/shard_map/ppermute | solution.py:437
  24.6 4.6 %collective-permute-start.8 = (f32[4,8,128]{2,1,0:T(8,128)S(1)}, f32[4,8,128]{2,1,0:T(8,128)S(1)}, u32[]{:S(2)}, u32[]{:S(2)}) collective-permute-start(f32[4,8,128]{2,1,0:T(8,128)S(1)} %get-tuple-element.104), channel_id=1, source_target_pairs={{0,6},{1,7},{2,4},{3,5},{4,2},{5,3},{6,0},{7,1},{8,14},{9,15},{10,... | collective-permute-start | bytes 49160 | tf_op jit(solution)/shard_map/ppermute | solution.py:437
  27.4 1.8 %collective-permute-start.9 = (f32[4,8,128]{2,1,0:T(8,128)S(1)}, f32[4,8,128]{2,1,0:T(8,128)S(1)}, u32[]{:S(2)}, u32[]{:S(2)}) collective-permute-start(f32[4,8,128]{2,1,0:T(8,128)S(1)} %get-tuple-element.105), channel_id=1, source_target_pairs={{0,1},{1,0},{2,3},{3,2},{4,10},{5,11},{6,8},{7,9},{8,6},{9,7},{10,... | collective-permute-start | bytes 49160 | tf_op jit(solution)/shard_map/ppermute | solution.py:437
  33.1 8.5 %collective-permute-start.10 = (f32[64,8,128]{2,1,0:T(8,128)S(1)}, f32[64,8,128]{2,1,0:T(8,128)S(1)}, u32[]{:S(2)}, u32[]{:S(2)}) collective-permute-start(f32[64,8,128]{2,1,0:T(8,128)S(1)} %get-tuple-element.111), channel_id=1, source_target_pairs={{0,2},{1,3},{2,0},{3,1},{4,6},{5,7},{6,4},{7,5},{8,10},{9,11},{10,... | collective-permute-start | bytes 786440 | tf_op jit(solution)/shard_map/ppermute | solution.py:437
  34.5 7.1 %collective-permute-start.11 = (f32[16,24,128]{2,1,0:T(8,128)S(1)}, f32[16,24,128]{2,1,0:T(8,128)S(1)}, u32[]{:S(2)}, u32[]{:S(2)}) collective-permute-start(f32[16,24,128]{2,1,0:T(8,128)S(1)} %get-tuple-element.112), channel_id=1, source_target_pairs={{0,4},{1,5},{2,6},{3,7},{4,0},{5,1},{6,2},{7,3},{8,12},{9,13},{10,... | collective-permute-start | bytes 589832 | tf_op jit(solution)/shard_map/ppermute | solution.py:437
  36.8 4.8 %collective-permute-start.12 = (f32[16,24,128]{2,1,0:T(8,128)S(1)}, f32[16,24,128]{2,1,0:T(8,128)S(1)}, u32[]{:S(2)}, u32[]{:S(2)}) collective-permute-start(f32[16,24,128]{2,1,0:T(8,128)S(1)} %get-tuple-element.113), channel_id=1, source_target_pairs={{0,1},{1,0},{2,3},{3,2},{4,8},{5,9},{6,10},{7,11},{8,4},{9,5},{10,... | collective-permute-start | bytes 589832 | tf_op jit(solution)/shard_map/ppermute | solution.py:437
  36.8 4.8 %collective-permute-start.13 = (f32[4,8,128]{2,1,0:T(8,128)S(1)}, f32[4,8,128]{2,1,0:T(8,128)S(1)}, u32[]{:S(2)}, u32[]{:S(2)}) collective-permute-start(f32[4,8,128]{2,1,0:T(8,128)S(1)} %get-tuple-element.114), channel_id=1, source_target_pairs={{0,6},{1,7},{2,4},{3,5},{4,2},{5,3},{6,0},{7,1},{8,14},{9,15},{10,... | collective-permute-start | bytes 49160 | tf_op jit(solution)/shard_map/ppermute | solution.py:437
  39.0 2.6 %collective-permute-start.14 = (f32[4,8,128]{2,1,0:T(8,128)S(1)}, f32[4,8,128]{2,1,0:T(8,128)S(1)}, u32[]{:S(2)}, u32[]{:S(2)}) collective-permute-start(f32[4,8,128]{2,1,0:T(8,128)S(1)} %get-tuple-element.115), channel_id=1, source_target_pairs={{0,1},{1,0},{2,3},{3,2},{4,10},{5,11},{6,8},{7,9},{8,6},{9,7},{10,... | collective-permute-start | bytes 49160 | tf_op jit(solution)/shard_map/ppermute | solution.py:437
  45.5 8.7 %collective-permute-start.15 = (f32[64,8,128]{2,1,0:T(8,128)S(1)}, f32[64,8,128]{2,1,0:T(8,128)S(1)}, u32[]{:S(2)}, u32[]{:S(2)}) collective-permute-start(f32[64,8,128]{2,1,0:T(8,128)S(1)} %get-tuple-element.121), channel_id=1, source_target_pairs={{0,2},{1,3},{2,0},{3,1},{4,6},{5,7},{6,4},{7,5},{8,10},{9,11},{10,... | collective-permute-start | bytes 786440 | tf_op jit(solution)/shard_map/ppermute | solution.py:437
  46.8 7.4 %collective-permute-start.16 = (f32[16,24,128]{2,1,0:T(8,128)S(1)}, f32[16,24,128]{2,1,0:T(8,128)S(1)}, u32[]{:S(2)}, u32[]{:S(2)}) collective-permute-start(f32[16,24,128]{2,1,0:T(8,128)S(1)} %get-tuple-element.122), channel_id=1, source_target_pairs={{0,4},{1,5},{2,6},{3,7},{4,0},{5,1},{6,2},{7,3},{8,12},{9,13},{10,... | collective-permute-start | bytes 589832 | tf_op jit(solution)/shard_map/ppermute | solution.py:437
  48.9 5.2 %collective-permute-start.17 = (f32[16,24,128]{2,1,0:T(8,128)S(1)}, f32[16,24,128]{2,1,0:T(8,128)S(1)}, u32[]{:S(2)}, u32[]{:S(2)}) collective-permute-start(f32[16,24,128]{2,1,0:T(8,128)S(1)} %get-tuple-element.123), channel_id=1, source_target_pairs={{0,1},{1,0},{2,3},{3,2},{4,8},{5,9},{6,10},{7,11},{8,4},{9,5},{10,... | collective-permute-start | bytes 589832 | tf_op jit(solution)/shard_map/ppermute | solution.py:437
  48.9 5.2 %collective-permute-start.18 = (f32[4,8,128]{2,1,0:T(8,128)S(1)}, f32[4,8,128]{2,1,0:T(8,128)S(1)}, u32[]{:S(2)}, u32[]{:S(2)}) collective-permute-start(f32[4,8,128]{2,1,0:T(8,128)S(1)} %get-tuple-element.124), channel_id=1, source_target_pairs={{0,6},{1,7},{2,4},{3,5},{4,2},{5,3},{6,0},{7,1},{8,14},{9,15},{10,... | collective-permute-start | bytes 49160 | tf_op jit(solution)/shard_map/ppermute | solution.py:437
  51.0 3.1 %collective-permute-start.19 = (f32[4,8,128]{2,1,0:T(8,128)S(1)}, f32[4,8,128]{2,1,0:T(8,128)S(1)}, u32[]{:S(2)}, u32[]{:S(2)}) collective-permute-start(f32[4,8,128]{2,1,0:T(8,128)S(1)} %get-tuple-element.125), channel_id=1, source_target_pairs={{0,1},{1,0},{2,3},{3,2},{4,10},{5,11},{6,8},{7,9},{8,6},{9,7},{10,... | collective-permute-start | bytes 49160 | tf_op jit(solution)/shard_map/ppermute | solution.py:437
  58.0 8.4 %collective-permute-start.20 = (f32[64,8,128]{2,1,0:T(8,128)S(1)}, f32[64,8,128]{2,1,0:T(8,128)S(1)}, u32[]{:S(2)}, u32[]{:S(2)}) collective-permute-start(f32[64,8,128]{2,1,0:T(8,128)S(1)} %get-tuple-element.131), channel_id=1, source_target_pairs={{0,2},{1,3},{2,0},{3,1},{4,6},{5,7},{6,4},{7,5},{8,10},{9,11},{10,... | collective-permute-start | bytes 786440 | tf_op jit(solution)/shard_map/ppermute | solution.py:437
  58.9 7.5 %collective-permute-start.21 = (f32[16,24,128]{2,1,0:T(8,128)S(1)}, f32[16,24,128]{2,1,0:T(8,128)S(1)}, u32[]{:S(2)}, u32[]{:S(2)}) collective-permute-start(f32[16,24,128]{2,1,0:T(8,128)S(1)} %get-tuple-element.132), channel_id=1, source_target_pairs={{0,4},{1,5},{2,6},{3,7},{4,0},{5,1},{6,2},{7,3},{8,12},{9,13},{10,... | collective-permute-start | bytes 589832 | tf_op jit(solution)/shard_map/ppermute | solution.py:437
  61.1 5.3 %collective-permute-start.22 = (f32[16,24,128]{2,1,0:T(8,128)S(1)}, f32[16,24,128]{2,1,0:T(8,128)S(1)}, u32[]{:S(2)}, u32[]{:S(2)}) collective-permute-start(f32[16,24,128]{2,1,0:T(8,128)S(1)} %get-tuple-element.133), channel_id=1, source_target_pairs={{0,1},{1,0},{2,3},{3,2},{4,8},{5,9},{6,10},{7,11},{8,4},{9,5},{10,... | collective-permute-start | bytes 589832 | tf_op jit(solution)/shard_map/ppermute | solution.py:437
  61.2 5.3 %collective-permute-start.23 = (f32[4,8,128]{2,1,0:T(8,128)S(1)}, f32[4,8,128]{2,1,0:T(8,128)S(1)}, u32[]{:S(2)}, u32[]{:S(2)}) collective-permute-start(f32[4,8,128]{2,1,0:T(8,128)S(1)} %get-tuple-element.134), channel_id=1, source_target_pairs={{0,6},{1,7},{2,4},{3,5},{4,2},{5,3},{6,0},{7,1},{8,14},{9,15},{10,... | collective-permute-start | bytes 49160 | tf_op jit(solution)/shard_map/ppermute | solution.py:437
  63.2 3.3 %collective-permute-start.24 = (f32[4,8,128]{2,1,0:T(8,128)S(1)}, f32[4,8,128]{2,1,0:T(8,128)S(1)}, u32[]{:S(2)}, u32[]{:S(2)}) collective-permute-start(f32[4,8,128]{2,1,0:T(8,128)S(1)} %get-tuple-element.135), channel_id=1, source_target_pairs={{0,1},{1,0},{2,3},{3,2},{4,10},{5,11},{6,8},{7,9},{8,6},{9,7},{10,... | collective-permute-start | bytes 49160 | tf_op jit(solution)/shard_map/ppermute | solution.py:437
  70.3 8.1 %collective-permute-start.25 = (f32[64,8,128]{2,1,0:T(8,128)S(1)}, f32[64,8,128]{2,1,0:T(8,128)S(1)}, u32[]{:S(2)}, u32[]{:S(2)}) collective-permute-start(f32[64,8,128]{2,1,0:T(8,128)S(1)} %get-tuple-element.141), channel_id=1, source_target_pairs={{0,2},{1,3},{2,0},{3,1},{4,6},{5,7},{6,4},{7,5},{8,10},{9,11},{10,... | collective-permute-start | bytes 786440 | tf_op jit(solution)/shard_map/ppermute | solution.py:437
  71.1 7.2 %collective-permute-start.26 = (f32[16,24,128]{2,1,0:T(8,128)S(1)}, f32[16,24,128]{2,1,0:T(8,128)S(1)}, u32[]{:S(2)}, u32[]{:S(2)}) collective-permute-start(f32[16,24,128]{2,1,0:T(8,128)S(1)} %get-tuple-element.142), channel_id=1, source_target_pairs={{0,4},{1,5},{2,6},{3,7},{4,0},{5,1},{6,2},{7,3},{8,12},{9,13},{10,... | collective-permute-start | bytes 589832 | tf_op jit(solution)/shard_map/ppermute | solution.py:437
  73.4 4.9 %collective-permute-start.27 = (f32[16,24,128]{2,1,0:T(8,128)S(1)}, f32[16,24,128]{2,1,0:T(8,128)S(1)}, u32[]{:S(2)}, u32[]{:S(2)}) collective-permute-start(f32[16,24,128]{2,1,0:T(8,128)S(1)} %get-tuple-element.143), channel_id=1, source_target_pairs={{0,1},{1,0},{2,3},{3,2},{4,8},{5,9},{6,10},{7,11},{8,4},{9,5},{10,... | collective-permute-start | bytes 589832 | tf_op jit(solution)/shard_map/ppermute | solution.py:437
  73.4 4.9 %collective-permute-start.28 = (f32[4,8,128]{2,1,0:T(8,128)S(1)}, f32[4,8,128]{2,1,0:T(8,128)S(1)}, u32[]{:S(2)}, u32[]{:S(2)}) collective-permute-start(f32[4,8,128]{2,1,0:T(8,128)S(1)} %get-tuple-element.144), channel_id=1, source_target_pairs={{0,6},{1,7},{2,4},{3,5},{4,2},{5,3},{6,0},{7,1},{8,14},{9,15},{10,... | collective-permute-start | bytes 49160 | tf_op jit(solution)/shard_map/ppermute | solution.py:437
  75.4 2.9 %collective-permute-start.29 = (f32[4,8,128]{2,1,0:T(8,128)S(1)}, f32[4,8,128]{2,1,0:T(8,128)S(1)}, u32[]{:S(2)}, u32[]{:S(2)}) collective-permute-start(f32[4,8,128]{2,1,0:T(8,128)S(1)} %get-tuple-element.145), channel_id=1, source_target_pairs={{0,1},{1,0},{2,3},{3,2},{4,10},{5,11},{6,8},{7,9},{8,6},{9,7},{10,... | collective-permute-start | bytes 49160 | tf_op jit(solution)/shard_map/ppermute | solution.py:437
  82.2 1.5 %collective-permute-start.30 = (f32[16,24,128]{2,1,0:T(8,128)S(1)}, f32[16,24,128]{2,1,0:T(8,128)S(1)}, u32[]{:S(2)}, u32[]{:S(2)}) collective-permute-start(f32[16,24,128]{2,1,0:T(8,128)S(1)} %get-tuple-element.156), channel_id=1, source_target_pairs={{0,1},{1,0},{2,3},{3,2},{4,5},{5,4},{6,7},{7,6},{8,9},{9,8},{10,11... | collective-permute-start | bytes 589832 | tf_op jit(solution)/shard_map/ppermute | solution.py:491

commit v3 on v2

--- a/solution.py
+++ b/solution.py
@@ -16,7 +16,8 @@
 SUB = 8
 DEEP = 2
 HALO = RADIUS * DEEP
-GROUP = 8
+TRIPS = 1
+FAR = (3, 4)
 RATIOS = [c / COEFFS[1] for c in COEFFS]
 GENERAL_BLOCK = 4
 GENERAL_BLOCKS = 3
@@ -106,9 +107,8 @@
     return [y, x, x, d, d]
 
 
-def pack(geo, fields, extras, messages):
-    p, _, sides = geo.place()
-    my, me, mo, de, do = messages
+def pack_y(geo, fields, my):
+    p, _, _ = geo.place()
     nx = geo.nx
 
     def ybody(x, carry):
@@ -118,16 +118,11 @@
         return carry
 
     lax.fori_loop(0, nx, ybody, 0, unroll=16)
-    if extras:
-
-        def yextra(h, carry):
-            for f, u in enumerate(extras):
-                for i in range(2):
-                    rows = u[2 * h + i + HALO, pl.ds(5 - 3 * p, 4, stride=SUB), :]
-                    my[2 * nx + f * (nx // 2) + h, 4 * i : 4 * i + 4, :] = rows
-            return carry
-
-        lax.fori_loop(0, nx // 2, yextra, 0, unroll=2)
+
+def pack_x(geo, fields, messages):
+    p, _, sides = geo.place()
+    me, mo, de, do = messages
+    nx = geo.nx
     for (right, _), mx, md in zip(sides, (me, mo), (de, do)):
         wide = jnp.where(right, nx, HALO)
         thin = jnp.where(right, nx + HALO - RADIUS, HALO)
@@ -140,9 +135,6 @@
 
         lax.fori_loop(0, HALO, xbody, 0, unroll=8)
         for i in range(RADIUS):
-            for f, u in enumerate(extras):
-                for q in range(geo.srows):
-                    mx[2 * HALO + f * RADIUS + i, 4 * q : 4 * q + 4, :] = u[thin + i, pl.ds(2 * p + q, 4, stride=SUB), :]
             for f, u in enumerate(fields):
                 rows = u[thin + i, pl.ds(5 - 3 * p, 4, stride=SUB), :]
                 md[2 * f + i // 2, 4 * (i % 2) : 4 * (i % 2) + 4, :] = rows
@@ -194,10 +186,49 @@
                     u[thin + i, pl.ds(6 - 5 * p, 4, stride=SUB), :] = rows
 
 
+def edge_kernel(geo):
+    nx = geo.nx
+
+    def body(s0, s1, r0, r1, c0, my, me, mo, de, do, pad, sem):
+        p, _, sides = geo.place()
+        edge = pl.ds(pl.multiple_of((geo.ny - HALO) * (1 - p), SUB), HALO)
+        sources = (s0.at[0], r0.at[0], s1.at[0], r1.at[0], c0)
+        copies, along_x = [], []
+        for f, src in enumerate(sources):
+            to = my.at[f * nx : f * nx + nx] if f < 2 else pad.at[f - 2]
+            copies.append(pltpu.make_async_copy(src.at[:, edge, :], to, sem.at[f]))
+        for n, ((right, _), mx) in enumerate(zip(sides, (me, mo))):
+            for f, src in enumerate(sources):
+                planes = HALO if f < 2 else RADIUS
+                at = f * HALO if f < 2 else 2 * HALO + (f - 2) * RADIUS
+                begin = jnp.where(right, nx - planes, 0)
+                along_x.append(
+                    pltpu.make_async_copy(src.at[pl.ds(begin, planes)], mx.at[at : at + planes], sem.at[5 * n + 5 + f])
+                )
+        for copy in copies + along_x:
+            copy.start()
+        near = pl.ds(4 - 4 * p, 4)
+        for f, copy in enumerate(copies):
+            copy.wait()
+            if f < 2:
+                for (right, _), md in zip(sides, (de, do)):
+                    begin = f * nx + jnp.where(right, nx - RADIUS, 0)
+                    for i in range(RADIUS):
+                        md[2 * f + i // 2, 4 * (i % 2) : 4 * (i % 2) + 4, :] = my[begin + i, near, :]
+            else:
+                for x in range(nx):
+                    half = 4 * (x % 2)
+                    my[2 * nx + (f - 2) * (nx // 2) + x // 2, half : half + 4, :] = pad[f - 2, x, near, :]
+        for copy in along_x:
+            copy.wait()
+
+    return body
+
+
 def load_kernel(geo):
     nx, ny, xe = geo.nx, geo.ny, geo.xe
 
-    def body(s0, s1, r0, r1, c0, us, ur, ps, pr, cc, dw, my, me, mo, de, do, pad, sem):
+    def body(s0, s1, r0, r1, c0, us, ur, ps, pr, cc, dw, pad, sem):
         p, _, _ = geo.place()
         inside = pl.ds(pl.multiple_of(SUB * p, SUB), ny)
         sources = (s0.at[0], r0.at[0], s1.at[0], r1.at[0], c0)
@@ -216,6 +247,9 @@
             d = jnp.where(gap == k, RATIOS[k], d)
         dw[0:LANES, :] = d.astype(jnp.bfloat16)
         dw[LANES : 2 * LANES, :] = d.astype(jnp.bfloat16)
+        for i, k in enumerate(FAR):
+            at = (2 + i) * LANES
+            dw[at : at + LANES, :] = jnp.where(gap == 0, RATIOS[k], 0.0).astype(jnp.bfloat16)
         zero = jnp.zeros((geo.win, LANES), F32)
         for f, u in enumerate(targets):
             for x in range(nx):
@@ -232,7 +266,6 @@
                 return carry
 
             lax.fori_loop(0, nx, turn, 0, unroll=4)
-        pack(geo, (us, ur), (ps, pr, cc), (my, me, mo, de, do))
 
     return body
 
@@ -273,16 +306,21 @@
     return body
 
 
-def update_planes(geo, pairs, cc, ee, dw, x, moment, gg, corr, fresh):
-    jn, span = geo.jn, GROUP * geo.win
+def update_planes(geo, count, pairs, cc, ee, dw, x, moment, gg, corr, fresh):
+    jn, span = geo.jn, count * geo.win
     sub = lax.broadcasted_iota(jnp.int32, (SUB, LANES), 0)
     at_depth = lax.broadcasted_iota(jnp.int32, (SUB, LANES), 1) == REC_DEPTH
     first, last = sub == 0, sub == SUB - 1
-    rows = jnp.concatenate([u[pl.ds(x, GROUP)].reshape(span, LANES) for u, _ in pairs], axis=0)
-    hi = rows.astype(jnp.bfloat16)
-    lo = (rows - hi.astype(F32)).astype(jnp.bfloat16)
-    deep = jnp.dot(jnp.concatenate([hi, lo], axis=1), dw[...], preferred_element_type=F32)
-    for i in range(GROUP):
+    parts = []
+    for u, _ in pairs:
+        rows = u[pl.ds(x - RADIUS, count + 2 * RADIUS)].reshape(span + 2 * RADIUS * geo.win, LANES)
+        near_hi = rows.astype(jnp.bfloat16)
+        shifted = lambda k: near_hi[(RADIUS + k) * geo.win : (RADIUS + k) * geo.win + span]
+        hi = shifted(0)
+        lo = (rows[RADIUS * geo.win : RADIUS * geo.win + span] - hi.astype(F32)).astype(jnp.bfloat16)
+        parts.append(jnp.concatenate([hi, lo] + [shifted(k) + shifted(-k) for k in FAR], axis=1))
+    deep = jnp.dot(jnp.concatenate(parts, axis=0), dw[...], preferred_element_type=F32)
+    for i in range(count):
         news = []
         for f, (u, prior) in enumerate(pairs):
             mid = [u[x + i, SUB * j : SUB * j + SUB, :] for j in range(jn)]
@@ -297,7 +335,9 @@
                     fed = pltpu.roll(gg[x + i, tile, :], (REC_DEPTH - moment) % LANES, 1)
                     acc = acc + jnp.where(at_depth, fed, 0.0)
                 for k in range(1, RADIUS + 1):
-                    near = (u[x + i + k, tile, :] + u[x + i - k, tile, :]) + (line[jn + j + k] + line[jn + j - k])
+                    near = line[jn + j + k] + line[jn + j - k]
+                    if k not in FAR:
+                        near = (u[x + i + k, tile, :] + u[x + i - k, tile, :]) + near
                     acc = acc + (near if k == 1 else RATIOS[k] * near)
                 new = (ee[x + i, tile, :] * mid[j] - prior[x + i, tile, :]) + cc[x + i, tile, :] * acc
                 prior[x + i, tile, :] = new
@@ -311,12 +351,14 @@
 
 
 def one_step(geo, moment, us, ur, ps, pr, cc, ee, gg, corr, dw, wav, src, first, count, fresh):
+    group_planes = count // TRIPS
+
     def group(i, carry):
-        x = first + i * GROUP
-        update_planes(geo, ((us, ps), (ur, pr)), cc, ee, dw, x, moment, gg, corr, fresh)
+        x = first + i * group_planes
+        update_planes(geo, group_planes, ((us, ps), (ur, pr)), cc, ee, dw, x, moment, gg, corr, fresh)
         return carry
 
-    lax.fori_loop(0, count // GROUP, group, 0)
+    lax.fori_loop(0, TRIPS, group, 0)
     xs, row, ok = src
 
     @pl.when(ok & (xs >= first) & (xs < first + count))
@@ -369,7 +411,8 @@
         one_step(geo, DEEP * block, us, ur, ps, pr, *common, HALO - RADIUS, geo.nx + 2 * RADIUS, first_round)
         one_step(geo, DEEP * block + 1, ps, pr, us, ur, *common, HALO, geo.nx, False)
         if not last:
-            pack(geo, (us, ur), (), outs)
+            pack_y(geo, (us, ur), outs[0])
+            pack_x(geo, (us, ur), outs[1:])
 
     return body
 
@@ -435,17 +478,24 @@
             neighbour(mesh, 1, True, True),
         ]
         send = lambda ms: [lax.ppermute(m, names, route) for m, route in zip(ms, routes)]
-        loaded = call(
+        given = tuple(pltpu.with_memory_space_constraint(v, pltpu.HBM) for v in (sn, sl, rn, rl, courant))
+        first = message_shapes(geo, True)
+        messages = send(
+            call(
+                edge_kernel(geo),
+                first,
+                [HBM] * 5,
+                given,
+                scratch=[pltpu.VMEM((3, nx, SUB, nz), F32), pltpu.SemaphoreType.DMA((15,))],
+            )
+        )
+        us, ur, ps, pr, cc, dw = call(
             load_kernel(geo),
-            [state] * 5
-            + [jax.ShapeDtypeStruct((2 * LANES, LANES), jnp.bfloat16)]
-            + message_shapes(geo, True),
+            [state] * 5 + [jax.ShapeDtypeStruct(((2 + len(FAR)) * LANES, LANES), jnp.bfloat16)],
             [HBM] * 5,
-            tuple(pltpu.with_memory_space_constraint(v, pltpu.HBM) for v in (sn, sl, rn, rl, courant)),
+            given,
             scratch=[pltpu.VMEM((5, nx, geo.win, nz), F32), pltpu.SemaphoreType.DMA((5,))],
         )
-        us, ur, ps, pr, cc, dw = loaded[:6]
-        messages = send(loaded[6:])
         nrec = traces.shape[2]
         gg, wav = call(
             receiver_kernel(geo, nrec),

time: 84.7 us -> 80 us (0.945)
  Pallas kernels: 28.2 us -> 25.7 us
  starting transfers between devices: 36.1 us -> 34.9 us
  waiting for transfers between devices: 16.7 us -> 15.6 us
    pallas_call x10 -> x11, Pallas kernels: 28.2 us -> 25.7 us  [call(): pl.pallas_call(body, out_shape=out_shapes, in_specs=specs, out_specs=out_...]
    ppermute x30, starting transfers between devices: 36 us -> 34.8 us  [run(): lax.ppermute(m, names, route)]
    ppermute x30, waiting for transfers between devices: 16.5 us -> 15.5 us  [run(): lax.ppermute(m, names, route)]
  transfers between devices with their start and end apart: 31 -> 31, of which waited for: 8 -> 7; matrix products, arithmetic and copies ran while one was open for 0% -> 0% of each run, Pallas kernels for 3% -> 5%
where the time goes in v3:
time: 80 us; the launch traced here: 79.8 us
  starting transfers between devices  34.9 us (44%)
  Pallas kernels  25.7 us (32%)
  waiting for transfers between devices  15.6 us (20%)
  between operations  2.17 us (3%)
    ppermute x30, starting transfers between devices, run(): lax.ppermute(m, names, route)  34.8 us
    pallas_call x11, Pallas kernels, call(): pl.pallas_call(body, out_shape=out_shapes, in_specs=specs, out_specs=out_...  25.7 us
    ppermute x30, waiting for transfers between devices, run(): lax.ppermute(m, names, route)  15.5 us
  transfers between devices with their start and end apart: 31, of which 7 were waited for; matrix products, arithmetic and copies ran while one was open for 0% of the time, Pallas kernels for 5%

profile of v3, /device:TPU:0, one launch (start us, length us, event | category | flops | bytes accessed | tf_op | source)
XLA Modules:
  0.0 79.8 jit_solution(8949119513129962853)
XLA Ops:
  0.6 1.5 %shard_map.148 = (f32[112,8,128]{2,1,0:T(8,128)S(1)}, f32[28,24,128]{2,1,0:T(8,128)S(1)}, f32[28,24,128]{2,1,0:T(8,128)S(1)}, f32[4,8,128]{2,1,0:T(8,128)S(1)}, f32[4,8,128]{2,1,0:T(8,128)S(1)}) custom-call(f32[1,32,24,128]{3,2,1,0:T(8,128)} %s0.3, f32[1,32,24,128]{3,2,1,0:T(8,128)} %s1_.3, f32[1,32,24,128]{3,2,1,0:T(8,128)} %r0.3, f32[1,32,24,128]{3,2,1,0:T(8,128)} %r1.3, ...), custom_call_target="tpu_custom_call" | custom-call | tf_op jit(solution)/shard_map/pallas_call | solution.py:87
  2.1 3.0 %collective-permute-start = (f32[112,8,128]{2,1,0:T(8,128)S(1)}, f32[112,8,128]{2,1,0:T(8,128)S(1)}, u32[]{:S(2)}, u32[]{:S(2)}) collective-permute-start(f32[112,8,128]{2,1,0:T(8,128)S(1)} %get-tuple-element.89), channel_id=1, source_target_pairs={{0,2},{1,3},{2,0},{3,1},{4,6},{5,7},{6,4},{7,5},{8,10},{9,11},{10,... | collective-permute-start | bytes 1376264 | tf_op jit(solution)/shard_map/ppermute | solution.py:480
  5.2 1.6 %collective-permute-start.1 = (f32[28,24,128]{2,1,0:T(8,128)S(1)}, f32[28,24,128]{2,1,0:T(8,128)S(1)}, u32[]{:S(2)}, u32[]{:S(2)}) collective-permute-start(f32[28,24,128]{2,1,0:T(8,128)S(1)} %get-tuple-element.90), channel_id=1, source_target_pairs={{0,4},{1,5},{2,6},{3,7},{4,0},{5,1},{6,2},{7,3},{8,12},{9,13},{10,... | collective-permute-start | bytes 1032200 | tf_op jit(solution)/shard_map/ppermute | solution.py:480
  6.7 0.0 collective-permute-start.2
  6.7 3.1 %collective-permute-start.3 = (f32[4,8,128]{2,1,0:T(8,128)S(1)}, f32[4,8,128]{2,1,0:T(8,128)S(1)}, u32[]{:S(2)}, u32[]{:S(2)}) collective-permute-start(f32[4,8,128]{2,1,0:T(8,128)S(1)} %get-tuple-element.92), channel_id=1, source_target_pairs={{0,6},{1,7},{2,4},{3,5},{4,2},{5,3},{6,0},{7,1},{8,14},{9,15},{10,... | collective-permute-start | bytes 49160 | tf_op jit(solution)/shard_map/ppermute | solution.py:480
  9.9 1.7 %shard_map.146 = (f32[48,32,128]{2,1,0:T(8,128)S(1)}, f32[48,32,128]{2,1,0:T(8,128)S(1)}, f32[48,32,128]{2,1,0:T(8,128)S(1)}, f32[48,32,128]{2,1,0:T(8,128)S(1)}...) custom-call(f32[1,32,24,128]{3,2,1,0:T(8,128)} %s0.3, f32[1,32,24,128]{3,2,1,0:T(8,128)} %s1_.3, ...), custom_call_target="tpu_custom_call" | custom-call | tf_op jit(solution)/shard_map/pallas_call | solution.py:87
  12.8 0.0 copy-start
  12.9 0.0 copy-start.1
  12.9 0.0 copy-start.2
  12.9 0.6 copy-done
  13.5 0.0 copy-done.1
  13.5 0.0 copy-done.2
  13.5 1.5 %shard_map.147 = (f32[48,32,128]{2,1,0:T(8,128)S(1)}, f32[8,128]{1,0:T(8,128)S(1)}) custom-call(s32[1,64]{1,0:T(1,128)S(1)} %copy-done, s32[1,64]{1,0:T(1,128)S(1)} %copy-done.1, f32[1,12,64]{2,1,0:T(8,128)S(1)} %copy.46.traces, f32[1,12]{1,0:T(1,128)S(1)} %copy-done.2), custom_call_target="tpu_custom_call" | custom-call | tf_op jit(solution)/shard_map/pallas_call | solution.py:87
  15.0 0.0 collective-permute-done.3.refs_11_
  15.0 0.0 collective-permute-done.1.refs_9_
  15.0 0.0 collective-permute-done.2.refs_10_
  15.1 1.0 %collective-permute-done.refs_8_ = f32[112,8,128]{2,1,0:T(8,128)S(1)} collective-permute-done((f32[112,8,128]{2,1,0:T(8,128)S(1)}, f32[112,8,128]{2,1,0:T(8,128)S(1)}, u32[]{:S(2)}, u32[]{:S(2)}) %collective-permute-start) | collective-permute-done | bytes 458784 | tf_op jit(solution)/shard_map/ppermute | solution.py:480
  16.0 3.5 %shard_map.149 = (f32[48,32,128]{2,1,0:T(8,128)S(1)}, f32[48,32,128]{2,1,0:T(8,128)S(1)}, f32[48,32,128]{2,1,0:T(8,128)S(1)}, f32[48,32,128]{2,1,0:T(8,128)S(1)}...) custom-call(f32[48,32,128]{2,1,0:T(8,128)S(1)} %get-tuple-element.81, ...), custom_call_target="tpu_custom_call", output_to_operand_aliasing={{0}: (0, {}), {1}: (1, {}), {2}: (2, {}), {3}: (3, {}), {4}... | custom-call | tf_op jit(solution)/shard_map/pallas_call | solution.py:87
  19.5 1.7 %collective-permute-start.5 = (f32[64,8,128]{2,1,0:T(8,128)S(1)}, f32[64,8,128]{2,1,0:T(8,128)S(1)}, u32[]{:S(2)}, u32[]{:S(2)}) collective-permute-start(f32[64,8,128]{2,1,0:T(8,128)S(1)} %get-tuple-element.101), channel_id=1, source_target_pairs={{0,2},{1,3},{2,0},{3,1},{4,6},{5,7},{6,4},{7,5},{8,10},{9,11},{10,... | collective-permute-start | bytes 786440 | tf_op jit(solution)/shard_map/ppermute | solution.py:480
  21.2 2.0 %collective-permute-start.6 = (f32[16,24,128]{2,1,0:T(8,128)S(1)}, f32[16,24,128]{2,1,0:T(8,128)S(1)}, u32[]{:S(2)}, u32[]{:S(2)}) collective-permute-start(f32[16,24,128]{2,1,0:T(8,128)S(1)} %get-tuple-element.102), channel_id=1, source_target_pairs={{0,4},{1,5},{2,6},{3,7},{4,0},{5,1},{6,2},{7,3},{8,12},{9,13},{10,... | collective-permute-start | bytes 589832 | tf_op jit(solution)/shard_map/ppermute | solution.py:480
  23.2 2.7 %collective-permute-start.8 = (f32[4,8,128]{2,1,0:T(8,128)S(1)}, f32[4,8,128]{2,1,0:T(8,128)S(1)}, u32[]{:S(2)}, u32[]{:S(2)}) collective-permute-start(f32[4,8,128]{2,1,0:T(8,128)S(1)} %get-tuple-element.104), channel_id=1, source_target_pairs={{0,6},{1,7},{2,4},{3,5},{4,2},{5,3},{6,0},{7,1},{8,14},{9,15},{10,... | collective-permute-start | bytes 49160 | tf_op jit(solution)/shard_map/ppermute | solution.py:480
  25.9 1.9 %collective-permute-done.8.refs_13_ = f32[4,8,128]{2,1,0:T(8,128)S(1)} collective-permute-done((f32[4,8,128]{2,1,0:T(8,128)S(1)}, f32[4,8,128]{2,1,0:T(8,128)S(1)}, u32[]{:S(2)}, u32[]{:S(2)}) %collective-permute-start.8) | collective-permute-done | bytes 16416 | tf_op jit(solution)/shard_map/ppermute | solution.py:480
  27.9 3.2 %shard_map.150 = (f32[48,32,128]{2,1,0:T(8,128)S(1)}, f32[48,32,128]{2,1,0:T(8,128)S(1)}, f32[48,32,128]{2,1,0:T(8,128)S(1)}, f32[48,32,128]{2,1,0:T(8,128)S(1)}...) custom-call(f32[48,32,128]{2,1,0:T(8,128)S(1)} %get-tuple-element.94, ...), custom_call_target="tpu_custom_call", output_to_operand_aliasing={{0}: (0, {}), {1}: (1, {}), {2}: (2, {}), {3}: (3, {}), {4}... | custom-call | tf_op jit(solution)/shard_map/pallas_call | solution.py:87
  31.1 1.3 %collective-permute-start.10 = (f32[64,8,128]{2,1,0:T(8,128)S(1)}, f32[64,8,128]{2,1,0:T(8,128)S(1)}, u32[]{:S(2)}, u32[]{:S(2)}) collective-permute-start(f32[64,8,128]{2,1,0:T(8,128)S(1)} %get-tuple-element.111), channel_id=1, source_target_pairs={{0,2},{1,3},{2,0},{3,1},{4,6},{5,7},{6,4},{7,5},{8,10},{9,11},{10,... | collective-permute-start | bytes 786440 | tf_op jit(solution)/shard_map/ppermute | solution.py:480
  32.4 2.3 %collective-permute-start.11 = (f32[16,24,128]{2,1,0:T(8,128)S(1)}, f32[16,24,128]{2,1,0:T(8,128)S(1)}, u32[]{:S(2)}, u32[]{:S(2)}) collective-permute-start(f32[16,24,128]{2,1,0:T(8,128)S(1)} %get-tuple-element.112), channel_id=1, source_target_pairs={{0,4},{1,5},{2,6},{3,7},{4,0},{5,1},{6,2},{7,3},{8,12},{9,13},{10,... | collective-permute-start | bytes 589832 | tf_op jit(solution)/shard_map/ppermute | solution.py:480
  34.7 2.0 %collective-permute-start.13 = (f32[4,8,128]{2,1,0:T(8,128)S(1)}, f32[4,8,128]{2,1,0:T(8,128)S(1)}, u32[]{:S(2)}, u32[]{:S(2)}) collective-permute-start(f32[4,8,128]{2,1,0:T(8,128)S(1)} %get-tuple-element.114), channel_id=1, source_target_pairs={{0,6},{1,7},{2,4},{3,5},{4,2},{5,3},{6,0},{7,1},{8,14},{9,15},{10,... | collective-permute-start | bytes 49160 | tf_op jit(solution)/shard_map/ppermute | solution.py:480
  36.7 2.8 %collective-permute-done.13.refs_13_ = f32[4,8,128]{2,1,0:T(8,128)S(1)} collective-permute-done((f32[4,8,128]{2,1,0:T(8,128)S(1)}, f32[4,8,128]{2,1,0:T(8,128)S(1)}, u32[]{:S(2)}, u32[]{:S(2)}) %collective-permute-start.13) | collective-permute-done | bytes 16416 | tf_op jit(solution)/shard_map/ppermute | solution.py:480
  39.5 3.3 %shard_map.151 = (f32[48,32,128]{2,1,0:T(8,128)S(1)}, f32[48,32,128]{2,1,0:T(8,128)S(1)}, f32[48,32,128]{2,1,0:T(8,128)S(1)}, f32[48,32,128]{2,1,0:T(8,128)S(1)}...) custom-call(f32[48,32,128]{2,1,0:T(8,128)S(1)} %get-tuple-element.10, ...), custom_call_target="tpu_custom_call", output_to_operand_aliasing={{0}: (0, {}), {1}: (1, {}), {2}: (2, {}), {3}: (3, {}), {4}... | custom-call | tf_op jit(solution)/shard_map/pallas_call | solution.py:87
  42.8 1.1 %collective-permute-start.15 = (f32[64,8,128]{2,1,0:T(8,128)S(1)}, f32[64,8,128]{2,1,0:T(8,128)S(1)}, u32[]{:S(2)}, u32[]{:S(2)}) collective-permute-start(f32[64,8,128]{2,1,0:T(8,128)S(1)} %get-tuple-element.121), channel_id=1, source_target_pairs={{0,2},{1,3},{2,0},{3,1},{4,6},{5,7},{6,4},{7,5},{8,10},{9,11},{10,... | collective-permute-start | bytes 786440 | tf_op jit(solution)/shard_map/ppermute | solution.py:480
  43.9 2.1 %collective-permute-start.16 = (f32[16,24,128]{2,1,0:T(8,128)S(1)}, f32[16,24,128]{2,1,0:T(8,128)S(1)}, u32[]{:S(2)}, u32[]{:S(2)}) collective-permute-start(f32[16,24,128]{2,1,0:T(8,128)S(1)} %get-tuple-element.122), channel_id=1, source_target_pairs={{0,4},{1,5},{2,6},{3,7},{4,0},{5,1},{6,2},{7,3},{8,12},{9,13},{10,... | collective-permute-start | bytes 589832 | tf_op jit(solution)/shard_map/ppermute | solution.py:480
  46.1 2.0 %collective-permute-start.18 = (f32[4,8,128]{2,1,0:T(8,128)S(1)}, f32[4,8,128]{2,1,0:T(8,128)S(1)}, u32[]{:S(2)}, u32[]{:S(2)}) collective-permute-start(f32[4,8,128]{2,1,0:T(8,128)S(1)} %get-tuple-element.124), channel_id=1, source_target_pairs={{0,6},{1,7},{2,4},{3,5},{4,2},{5,3},{6,0},{7,1},{8,14},{9,15},{10,... | collective-permute-start | bytes 49160 | tf_op jit(solution)/shard_map/ppermute | solution.py:480
  48.1 3.3 %collective-permute-done.18.refs_13_ = f32[4,8,128]{2,1,0:T(8,128)S(1)} collective-permute-done((f32[4,8,128]{2,1,0:T(8,128)S(1)}, f32[4,8,128]{2,1,0:T(8,128)S(1)}, u32[]{:S(2)}, u32[]{:S(2)}) %collective-permute-start.18) | collective-permute-done | bytes 16416 | tf_op jit(solution)/shard_map/ppermute | solution.py:480
  51.4 3.4 %shard_map.152 = (f32[48,32,128]{2,1,0:T(8,128)S(1)}, f32[48,32,128]{2,1,0:T(8,128)S(1)}, f32[48,32,128]{2,1,0:T(8,128)S(1)}, f32[48,32,128]{2,1,0:T(8,128)S(1)}...) custom-call(f32[48,32,128]{2,1,0:T(8,128)S(1)} %get-tuple-element.11, ...), custom_call_target="tpu_custom_call", output_to_operand_aliasing={{0}: (0, {}), {1}: (1, {}), {2}: (2, {}), {3}: (3, {}), {4}... | custom-call | tf_op jit(solution)/shard_map/pallas_call | solution.py:87
  54.8 0.7 collective-permute-start.20
  55.5 2.3 %collective-permute-start.21 = (f32[16,24,128]{2,1,0:T(8,128)S(1)}, f32[16,24,128]{2,1,0:T(8,128)S(1)}, u32[]{:S(2)}, u32[]{:S(2)}) collective-permute-start(f32[16,24,128]{2,1,0:T(8,128)S(1)} %get-tuple-element.132), channel_id=1, source_target_pairs={{0,4},{1,5},{2,6},{3,7},{4,0},{5,1},{6,2},{7,3},{8,12},{9,13},{10,... | collective-permute-start | bytes 589832 | tf_op jit(solution)/shard_map/ppermute | solution.py:480
  57.8 2.0 %collective-permute-start.23 = (f32[4,8,128]{2,1,0:T(8,128)S(1)}, f32[4,8,128]{2,1,0:T(8,128)S(1)}, u32[]{:S(2)}, u32[]{:S(2)}) collective-permute-start(f32[4,8,128]{2,1,0:T(8,128)S(1)} %get-tuple-element.134), channel_id=1, source_target_pairs={{0,6},{1,7},{2,4},{3,5},{4,2},{5,3},{6,0},{7,1},{8,14},{9,15},{10,... | collective-permute-start | bytes 49160 | tf_op jit(solution)/shard_map/ppermute | solution.py:480
  59.8 3.3 %collective-permute-done.23.refs_13_ = f32[4,8,128]{2,1,0:T(8,128)S(1)} collective-permute-done((f32[4,8,128]{2,1,0:T(8,128)S(1)}, f32[4,8,128]{2,1,0:T(8,128)S(1)}, u32[]{:S(2)}, u32[]{:S(2)}) %collective-permute-start.23) | collective-permute-done | bytes 16416 | tf_op jit(solution)/shard_map/ppermute | solution.py:480
  63.1 3.2 %shard_map.153 = (f32[48,32,128]{2,1,0:T(8,128)S(1)}, f32[48,32,128]{2,1,0:T(8,128)S(1)}, f32[48,32,128]{2,1,0:T(8,128)S(1)}, f32[48,32,128]{2,1,0:T(8,128)S(1)}...) custom-call(f32[48,32,128]{2,1,0:T(8,128)S(1)} %get-tuple-element.12, ...), custom_call_target="tpu_custom_call", output_to_operand_aliasing={{0}: (0, {}), {1}: (1, {}), {2}: (2, {}), {3}: (3, {}), {4}... | custom-call | tf_op jit(solution)/shard_map/pallas_call | solution.py:87
  66.3 0.7 collective-permute-start.25
  67.0 2.3 %collective-permute-start.26 = (f32[16,24,128]{2,1,0:T(8,128)S(1)}, f32[16,24,128]{2,1,0:T(8,128)S(1)}, u32[]{:S(2)}, u32[]{:S(2)}) collective-permute-start(f32[16,24,128]{2,1,0:T(8,128)S(1)} %get-tuple-element.142), channel_id=1, source_target_pairs={{0,4},{1,5},{2,6},{3,7},{4,0},{5,1},{6,2},{7,3},{8,12},{9,13},{10,... | collective-permute-start | bytes 589832 | tf_op jit(solution)/shard_map/ppermute | solution.py:480
  69.3 1.9 %collective-permute-start.28 = (f32[4,8,128]{2,1,0:T(8,128)S(1)}, f32[4,8,128]{2,1,0:T(8,128)S(1)}, u32[]{:S(2)}, u32[]{:S(2)}) collective-permute-start(f32[4,8,128]{2,1,0:T(8,128)S(1)} %get-tuple-element.144), channel_id=1, source_target_pairs={{0,6},{1,7},{2,4},{3,5},{4,2},{5,3},{6,0},{7,1},{8,14},{9,15},{10,... | collective-permute-start | bytes 49160 | tf_op jit(solution)/shard_map/ppermute | solution.py:480
  71.2 3.1 %collective-permute-done.28.refs_13_ = f32[4,8,128]{2,1,0:T(8,128)S(1)} collective-permute-done((f32[4,8,128]{2,1,0:T(8,128)S(1)}, f32[4,8,128]{2,1,0:T(8,128)S(1)}, u32[]{:S(2)}, u32[]{:S(2)}) %collective-permute-start.28) | collective-permute-done | bytes 16416 | tf_op jit(solution)/shard_map/ppermute | solution.py:480
  74.3 3.1 %shard_map.154 = (f32[48,32,128]{2,1,0:T(8,128)S(1)}, f32[48,32,128]{2,1,0:T(8,128)S(1)}, f32[48,32,128]{2,1,0:T(8,128)S(1)}, f32[48,32,128]{2,1,0:T(8,128)S(1)}, f32[40,32,128]{2,1,0:T(8,128)S(1)}) custom-call(f32[48,32,128]{2,1,0:T(8,128)S(1)} %get-tuple-element.136.refs_0_, ...), custom_call_target="tpu_custom_call", output_to_operand_aliasing={{0}: (0, {}), {1}: (1, {}), {2}: (2, {}), {3}: (3, {}), {4}... | custom-call | tf_op jit(solution)/shard_map/pallas_call | solution.py:87
  77.4 0.1 shard_map.156
  77.6 0.1 collective-permute-start.30
  77.6 1.2 %shard_map.155 = (f32[1,32,24,128]{3,2,1,0:T(8,128)}, f32[1,32,24,128]{3,2,1,0:T(8,128)}, f32[1,32,24,128]{3,2,1,0:T(8,128)}, f32[1,32,24,128]{3,2,1,0:T(8,128)}) custom-call(f32[48,32,128]{2,1,0:T(8,128)S(1)} %get-tuple-element.146.us, f32[48,32,128]{2,1,0:T(8,128)S(1)} %get-tuple-element.147.ur, f32[48,32,128]{2,1,0:T(8,128)S(1)} %get-tuple-element.148.ps, ...), custom_call_target="tpu_custom_call" | custom-call | tf_op jit(solution)/shard_map/pallas_call | solution.py:87
  78.9 0.2 collective-permute-done.30
  79.1 0.7 add_multiply_fusion
  (35 shorter events, 0.1 us)
Async XLA Ops:
  2.1 13.9 %collective-permute-start = (f32[112,8,128]{2,1,0:T(8,128)S(1)}, f32[112,8,128]{2,1,0:T(8,128)S(1)}, u32[]{:S(2)}, u32[]{:S(2)}) collective-permute-start(f32[112,8,128]{2,1,0:T(8,128)S(1)} %get-tuple-element.89), channel_id=1, source_target_pairs={{0,2},{1,3},{2,0},{3,1},{4,6},{5,7},{6,4},{7,5},{8,10},{9,11},{10,... | collective-permute-start | bytes 1376264 | tf_op jit(solution)/shard_map/ppermute | solution.py:480
  5.2 9.9 %collective-permute-start.1 = (f32[28,24,128]{2,1,0:T(8,128)S(1)}, f32[28,24,128]{2,1,0:T(8,128)S(1)}, u32[]{:S(2)}, u32[]{:S(2)}) collective-permute-start(f32[28,24,128]{2,1,0:T(8,128)S(1)} %get-tuple-element.90), channel_id=1, source_target_pairs={{0,4},{1,5},{2,6},{3,7},{4,0},{5,1},{6,2},{7,3},{8,12},{9,13},{10,... | collective-permute-start | bytes 1032200 | tf_op jit(solution)/shard_map/ppermute | solution.py:480
  6.7 8.3 %collective-permute-start.2 = (f32[28,24,128]{2,1,0:T(8,128)S(1)}, f32[28,24,128]{2,1,0:T(8,128)S(1)}, u32[]{:S(2)}, u32[]{:S(2)}) collective-permute-start(f32[28,24,128]{2,1,0:T(8,128)S(1)} %get-tuple-element.91), channel_id=1, source_target_pairs={{0,1},{1,0},{2,3},{3,2},{4,8},{5,9},{6,10},{7,11},{8,4},{9,5},{10,... | collective-permute-start | bytes 1032200 | tf_op jit(solution)/shard_map/ppermute | solution.py:480
  6.7 8.3 %collective-permute-start.3 = (f32[4,8,128]{2,1,0:T(8,128)S(1)}, f32[4,8,128]{2,1,0:T(8,128)S(1)}, u32[]{:S(2)}, u32[]{:S(2)}) collective-permute-start(f32[4,8,128]{2,1,0:T(8,128)S(1)} %get-tuple-element.92), channel_id=1, source_target_pairs={{0,6},{1,7},{2,4},{3,5},{4,2},{5,3},{6,0},{7,1},{8,14},{9,15},{10,... | collective-permute-start | bytes 49160 | tf_op jit(solution)/shard_map/ppermute | solution.py:480
  9.9 5.2 %collective-permute-start.4 = (f32[4,8,128]{2,1,0:T(8,128)S(1)}, f32[4,8,128]{2,1,0:T(8,128)S(1)}, u32[]{:S(2)}, u32[]{:S(2)}) collective-permute-start(f32[4,8,128]{2,1,0:T(8,128)S(1)} %get-tuple-element.93), channel_id=1, source_target_pairs={{0,1},{1,0},{2,3},{3,2},{4,10},{5,11},{6,8},{7,9},{8,6},{9,7},{10,... | collective-permute-start | bytes 49160 | tf_op jit(solution)/shard_map/ppermute | solution.py:480
  9.9 3.0 %copy-start.3 = (f32[1,12,64]{2,0,1:T(1,128)S(1)}, f32[1,12,64]{2,0,1:T(1,128)}, u32[]{:S(2)}) copy-start(f32[1,12,64]{2,0,1:T(1,128)} %param.17) | copy-start | bytes 9220
  12.8 0.7 copy-start
  12.9 0.7 copy-start.1
  12.9 0.7 copy-start.2
  19.5 8.4 %collective-permute-start.5 = (f32[64,8,128]{2,1,0:T(8,128)S(1)}, f32[64,8,128]{2,1,0:T(8,128)S(1)}, u32[]{:S(2)}, u32[]{:S(2)}) collective-permute-start(f32[64,8,128]{2,1,0:T(8,128)S(1)} %get-tuple-element.101), channel_id=1, source_target_pairs={{0,2},{1,3},{2,0},{3,1},{4,6},{5,7},{6,4},{7,5},{8,10},{9,11},{10,... | collective-permute-start | bytes 786440 | tf_op jit(solution)/shard_map/ppermute | solution.py:480
  21.2 6.7 %collective-permute-start.6 = (f32[16,24,128]{2,1,0:T(8,128)S(1)}, f32[16,24,128]{2,1,0:T(8,128)S(1)}, u32[]{:S(2)}, u32[]{:S(2)}) collective-permute-start(f32[16,24,128]{2,1,0:T(8,128)S(1)} %get-tuple-element.102), channel_id=1, source_target_pairs={{0,4},{1,5},{2,6},{3,7},{4,0},{5,1},{6,2},{7,3},{8,12},{9,13},{10,... | collective-permute-start | bytes 589832 | tf_op jit(solution)/shard_map/ppermute | solution.py:480
  23.2 4.7 %collective-permute-start.7 = (f32[16,24,128]{2,1,0:T(8,128)S(1)}, f32[16,24,128]{2,1,0:T(8,128)S(1)}, u32[]{:S(2)}, u32[]{:S(2)}) collective-permute-start(f32[16,24,128]{2,1,0:T(8,128)S(1)} %get-tuple-element.103), channel_id=1, source_target_pairs={{0,1},{1,0},{2,3},{3,2},{4,8},{5,9},{6,10},{7,11},{8,4},{9,5},{10,... | collective-permute-start | bytes 589832 | tf_op jit(solution)/shard_map/ppermute | solution.py:480
  23.2 4.6 %collective-permute-start.8 = (f32[4,8,128]{2,1,0:T(8,128)S(1)}, f32[4,8,128]{2,1,0:T(8,128)S(1)}, u32[]{:S(2)}, u32[]{:S(2)}) collective-permute-start(f32[4,8,128]{2,1,0:T(8,128)S(1)} %get-tuple-element.104), channel_id=1, source_target_pairs={{0,6},{1,7},{2,4},{3,5},{4,2},{5,3},{6,0},{7,1},{8,14},{9,15},{10,... | collective-permute-start | bytes 49160 | tf_op jit(solution)/shard_map/ppermute | solution.py:480
  25.9 2.0 %collective-permute-start.9 = (f32[4,8,128]{2,1,0:T(8,128)S(1)}, f32[4,8,128]{2,1,0:T(8,128)S(1)}, u32[]{:S(2)}, u32[]{:S(2)}) collective-permute-start(f32[4,8,128]{2,1,0:T(8,128)S(1)} %get-tuple-element.105), channel_id=1, source_target_pairs={{0,1},{1,0},{2,3},{3,2},{4,10},{5,11},{6,8},{7,9},{8,6},{9,7},{10,... | collective-permute-start | bytes 49160 | tf_op jit(solution)/shard_map/ppermute | solution.py:480
  31.1 8.4 %collective-permute-start.10 = (f32[64,8,128]{2,1,0:T(8,128)S(1)}, f32[64,8,128]{2,1,0:T(8,128)S(1)}, u32[]{:S(2)}, u32[]{:S(2)}) collective-permute-start(f32[64,8,128]{2,1,0:T(8,128)S(1)} %get-tuple-element.111), channel_id=1, source_target_pairs={{0,2},{1,3},{2,0},{3,1},{4,6},{5,7},{6,4},{7,5},{8,10},{9,11},{10,... | collective-permute-start | bytes 786440 | tf_op jit(solution)/shard_map/ppermute | solution.py:480
  32.4 7.1 %collective-permute-start.11 = (f32[16,24,128]{2,1,0:T(8,128)S(1)}, f32[16,24,128]{2,1,0:T(8,128)S(1)}, u32[]{:S(2)}, u32[]{:S(2)}) collective-permute-start(f32[16,24,128]{2,1,0:T(8,128)S(1)} %get-tuple-element.112), channel_id=1, source_target_pairs={{0,4},{1,5},{2,6},{3,7},{4,0},{5,1},{6,2},{7,3},{8,12},{9,13},{10,... | collective-permute-start | bytes 589832 | tf_op jit(solution)/shard_map/ppermute | solution.py:480
  34.7 4.8 %collective-permute-start.12 = (f32[16,24,128]{2,1,0:T(8,128)S(1)}, f32[16,24,128]{2,1,0:T(8,128)S(1)}, u32[]{:S(2)}, u32[]{:S(2)}) collective-permute-start(f32[16,24,128]{2,1,0:T(8,128)S(1)} %get-tuple-element.113), channel_id=1, source_target_pairs={{0,1},{1,0},{2,3},{3,2},{4,8},{5,9},{6,10},{7,11},{8,4},{9,5},{10,... | collective-permute-start | bytes 589832 | tf_op jit(solution)/shard_map/ppermute | solution.py:480
  34.7 4.8 %collective-permute-start.13 = (f32[4,8,128]{2,1,0:T(8,128)S(1)}, f32[4,8,128]{2,1,0:T(8,128)S(1)}, u32[]{:S(2)}, u32[]{:S(2)}) collective-permute-start(f32[4,8,128]{2,1,0:T(8,128)S(1)} %get-tuple-element.114), channel_id=1, source_target_pairs={{0,6},{1,7},{2,4},{3,5},{4,2},{5,3},{6,0},{7,1},{8,14},{9,15},{10,... | collective-permute-start | bytes 49160 | tf_op jit(solution)/shard_map/ppermute | solution.py:480
  36.7 2.8 %collective-permute-start.14 = (f32[4,8,128]{2,1,0:T(8,128)S(1)}, f32[4,8,128]{2,1,0:T(8,128)S(1)}, u32[]{:S(2)}, u32[]{:S(2)}) collective-permute-start(f32[4,8,128]{2,1,0:T(8,128)S(1)} %get-tuple-element.115), channel_id=1, source_target_pairs={{0,1},{1,0},{2,3},{3,2},{4,10},{5,11},{6,8},{7,9},{8,6},{9,7},{10,... | collective-permute-start | bytes 49160 | tf_op jit(solution)/shard_map/ppermute | solution.py:480
  42.8 8.6 %collective-permute-start.15 = (f32[64,8,128]{2,1,0:T(8,128)S(1)}, f32[64,8,128]{2,1,0:T(8,128)S(1)}, u32[]{:S(2)}, u32[]{:S(2)}) collective-permute-start(f32[64,8,128]{2,1,0:T(8,128)S(1)} %get-tuple-element.121), channel_id=1, source_target_pairs={{0,2},{1,3},{2,0},{3,1},{4,6},{5,7},{6,4},{7,5},{8,10},{9,11},{10,... | collective-permute-start | bytes 786440 | tf_op jit(solution)/shard_map/ppermute | solution.py:480
  43.9 7.4 %collective-permute-start.16 = (f32[16,24,128]{2,1,0:T(8,128)S(1)}, f32[16,24,128]{2,1,0:T(8,128)S(1)}, u32[]{:S(2)}, u32[]{:S(2)}) collective-permute-start(f32[16,24,128]{2,1,0:T(8,128)S(1)} %get-tuple-element.122), channel_id=1, source_target_pairs={{0,4},{1,5},{2,6},{3,7},{4,0},{5,1},{6,2},{7,3},{8,12},{9,13},{10,... | collective-permute-start | bytes 589832 | tf_op jit(solution)/shard_map/ppermute | solution.py:480
  46.1 5.3 %collective-permute-start.17 = (f32[16,24,128]{2,1,0:T(8,128)S(1)}, f32[16,24,128]{2,1,0:T(8,128)S(1)}, u32[]{:S(2)}, u32[]{:S(2)}) collective-permute-start(f32[16,24,128]{2,1,0:T(8,128)S(1)} %get-tuple-element.123), channel_id=1, source_target_pairs={{0,1},{1,0},{2,3},{3,2},{4,8},{5,9},{6,10},{7,11},{8,4},{9,5},{10,... | collective-permute-start | bytes 589832 | tf_op jit(solution)/shard_map/ppermute | solution.py:480
  46.1 5.3 %collective-permute-start.18 = (f32[4,8,128]{2,1,0:T(8,128)S(1)}, f32[4,8,128]{2,1,0:T(8,128)S(1)}, u32[]{:S(2)}, u32[]{:S(2)}) collective-permute-start(f32[4,8,128]{2,1,0:T(8,128)S(1)} %get-tuple-element.124), channel_id=1, source_target_pairs={{0,6},{1,7},{2,4},{3,5},{4,2},{5,3},{6,0},{7,1},{8,14},{9,15},{10,... | collective-permute-start | bytes 49160 | tf_op jit(solution)/shard_map/ppermute | solution.py:480
  48.1 3.3 %collective-permute-start.19 = (f32[4,8,128]{2,1,0:T(8,128)S(1)}, f32[4,8,128]{2,1,0:T(8,128)S(1)}, u32[]{:S(2)}, u32[]{:S(2)}) collective-permute-start(f32[4,8,128]{2,1,0:T(8,128)S(1)} %get-tuple-element.125), channel_id=1, source_target_pairs={{0,1},{1,0},{2,3},{3,2},{4,10},{5,11},{6,8},{7,9},{8,6},{9,7},{10,... | collective-permute-start | bytes 49160 | tf_op jit(solution)/shard_map/ppermute | solution.py:480
  54.8 8.3 %collective-permute-start.20 = (f32[64,8,128]{2,1,0:T(8,128)S(1)}, f32[64,8,128]{2,1,0:T(8,128)S(1)}, u32[]{:S(2)}, u32[]{:S(2)}) collective-permute-start(f32[64,8,128]{2,1,0:T(8,128)S(1)} %get-tuple-element.131), channel_id=1, source_target_pairs={{0,2},{1,3},{2,0},{3,1},{4,6},{5,7},{6,4},{7,5},{8,10},{9,11},{10,... | collective-permute-start | bytes 786440 | tf_op jit(solution)/shard_map/ppermute | solution.py:480
  55.5 7.6 %collective-permute-start.21 = (f32[16,24,128]{2,1,0:T(8,128)S(1)}, f32[16,24,128]{2,1,0:T(8,128)S(1)}, u32[]{:S(2)}, u32[]{:S(2)}) collective-permute-start(f32[16,24,128]{2,1,0:T(8,128)S(1)} %get-tuple-element.132), channel_id=1, source_target_pairs={{0,4},{1,5},{2,6},{3,7},{4,0},{5,1},{6,2},{7,3},{8,12},{9,13},{10,... | collective-permute-start | bytes 589832 | tf_op jit(solution)/shard_map/ppermute | solution.py:480
  57.8 5.3 %collective-permute-start.22 = (f32[16,24,128]{2,1,0:T(8,128)S(1)}, f32[16,24,128]{2,1,0:T(8,128)S(1)}, u32[]{:S(2)}, u32[]{:S(2)}) collective-permute-start(f32[16,24,128]{2,1,0:T(8,128)S(1)} %get-tuple-element.133), channel_id=1, source_target_pairs={{0,1},{1,0},{2,3},{3,2},{4,8},{5,9},{6,10},{7,11},{8,4},{9,5},{10,... | collective-permute-start | bytes 589832 | tf_op jit(solution)/shard_map/ppermute | solution.py:480
  57.8 5.3 %collective-permute-start.23 = (f32[4,8,128]{2,1,0:T(8,128)S(1)}, f32[4,8,128]{2,1,0:T(8,128)S(1)}, u32[]{:S(2)}, u32[]{:S(2)}) collective-permute-start(f32[4,8,128]{2,1,0:T(8,128)S(1)} %get-tuple-element.134), channel_id=1, source_target_pairs={{0,6},{1,7},{2,4},{3,5},{4,2},{5,3},{6,0},{7,1},{8,14},{9,15},{10,... | collective-permute-start | bytes 49160 | tf_op jit(solution)/shard_map/ppermute | solution.py:480
  59.8 3.3 %collective-permute-start.24 = (f32[4,8,128]{2,1,0:T(8,128)S(1)}, f32[4,8,128]{2,1,0:T(8,128)S(1)}, u32[]{:S(2)}, u32[]{:S(2)}) collective-permute-start(f32[4,8,128]{2,1,0:T(8,128)S(1)} %get-tuple-element.135), channel_id=1, source_target_pairs={{0,1},{1,0},{2,3},{3,2},{4,10},{5,11},{6,8},{7,9},{8,6},{9,7},{10,... | collective-permute-start | bytes 49160 | tf_op jit(solution)/shard_map/ppermute | solution.py:480
  66.3 8.0 %collective-permute-start.25 = (f32[64,8,128]{2,1,0:T(8,128)S(1)}, f32[64,8,128]{2,1,0:T(8,128)S(1)}, u32[]{:S(2)}, u32[]{:S(2)}) collective-permute-start(f32[64,8,128]{2,1,0:T(8,128)S(1)} %get-tuple-element.141), channel_id=1, source_target_pairs={{0,2},{1,3},{2,0},{3,1},{4,6},{5,7},{6,4},{7,5},{8,10},{9,11},{10,... | collective-permute-start | bytes 786440 | tf_op jit(solution)/shard_map/ppermute | solution.py:480
  67.0 7.3 %collective-permute-start.26 = (f32[16,24,128]{2,1,0:T(8,128)S(1)}, f32[16,24,128]{2,1,0:T(8,128)S(1)}, u32[]{:S(2)}, u32[]{:S(2)}) collective-permute-start(f32[16,24,128]{2,1,0:T(8,128)S(1)} %get-tuple-element.142), channel_id=1, source_target_pairs={{0,4},{1,5},{2,6},{3,7},{4,0},{5,1},{6,2},{7,3},{8,12},{9,13},{10,... | collective-permute-start | bytes 589832 | tf_op jit(solution)/shard_map/ppermute | solution.py:480
  69.3 5.0 %collective-permute-start.27 = (f32[16,24,128]{2,1,0:T(8,128)S(1)}, f32[16,24,128]{2,1,0:T(8,128)S(1)}, u32[]{:S(2)}, u32[]{:S(2)}) collective-permute-start(f32[16,24,128]{2,1,0:T(8,128)S(1)} %get-tuple-element.143), channel_id=1, source_target_pairs={{0,1},{1,0},{2,3},{3,2},{4,8},{5,9},{6,10},{7,11},{8,4},{9,5},{10,... | collective-permute-start | bytes 589832 | tf_op jit(solution)/shard_map/ppermute | solution.py:480
  69.3 5.0 %collective-permute-start.28 = (f32[4,8,128]{2,1,0:T(8,128)S(1)}, f32[4,8,128]{2,1,0:T(8,128)S(1)}, u32[]{:S(2)}, u32[]{:S(2)}) collective-permute-start(f32[4,8,128]{2,1,0:T(8,128)S(1)} %get-tuple-element.144), channel_id=1, source_target_pairs={{0,6},{1,7},{2,4},{3,5},{4,2},{5,3},{6,0},{7,1},{8,14},{9,15},{10,... | collective-permute-start | bytes 49160 | tf_op jit(solution)/shard_map/ppermute | solution.py:480
  71.2 3.1 %collective-permute-start.29 = (f32[4,8,128]{2,1,0:T(8,128)S(1)}, f32[4,8,128]{2,1,0:T(8,128)S(1)}, u32[]{:S(2)}, u32[]{:S(2)}) collective-permute-start(f32[4,8,128]{2,1,0:T(8,128)S(1)} %get-tuple-element.145), channel_id=1, source_target_pairs={{0,1},{1,0},{2,3},{3,2},{4,10},{5,11},{6,8},{7,9},{8,6},{9,7},{10,... | collective-permute-start | bytes 49160 | tf_op jit(solution)/shard_map/ppermute | solution.py:480
  77.6 1.5 %collective-permute-start.30 = (f32[16,24,128]{2,1,0:T(8,128)S(1)}, f32[16,24,128]{2,1,0:T(8,128)S(1)}, u32[]{:S(2)}, u32[]{:S(2)}) collective-permute-start(f32[16,24,128]{2,1,0:T(8,128)S(1)} %get-tuple-element.156), channel_id=1, source_target_pairs={{0,1},{1,0},{2,3},{3,2},{4,5},{5,4},{6,7},{7,6},{8,9},{9,8},{10,11... | collective-permute-start | bytes 589832 | tf_op jit(solution)/shard_map/ppermute | solution.py:541

commit v4 on v3

--- a/solution.py
+++ b/solution.py
@@ -16,8 +16,6 @@
 SUB = 8
 DEEP = 2
 HALO = RADIUS * DEEP
-TRIPS = 1
-FAR = (3, 4)
 RATIOS = [c / COEFFS[1] for c in COEFFS]
 GENERAL_BLOCK = 4
 GENERAL_BLOCKS = 3
@@ -247,9 +245,6 @@
             d = jnp.where(gap == k, RATIOS[k], d)
         dw[0:LANES, :] = d.astype(jnp.bfloat16)
         dw[LANES : 2 * LANES, :] = d.astype(jnp.bfloat16)
-        for i, k in enumerate(FAR):
-            at = (2 + i) * LANES
-            dw[at : at + LANES, :] = jnp.where(gap == 0, RATIOS[k], 0.0).astype(jnp.bfloat16)
         zero = jnp.zeros((geo.win, LANES), F32)
         for f, u in enumerate(targets):
             for x in range(nx):
@@ -306,26 +301,24 @@
     return body
 
 
-def update_planes(geo, count, pairs, cc, ee, dw, x, moment, gg, corr, fresh):
+def update_planes(geo, count, pairs, cc, ee, dw, x, moment, gg, corr, fresh, masked):
     jn, span = geo.jn, count * geo.win
     sub = lax.broadcasted_iota(jnp.int32, (SUB, LANES), 0)
     at_depth = lax.broadcasted_iota(jnp.int32, (SUB, LANES), 1) == REC_DEPTH
     first, last = sub == 0, sub == SUB - 1
-    parts = []
-    for u, _ in pairs:
-        rows = u[pl.ds(x - RADIUS, count + 2 * RADIUS)].reshape(span + 2 * RADIUS * geo.win, LANES)
-        near_hi = rows.astype(jnp.bfloat16)
-        shifted = lambda k: near_hi[(RADIUS + k) * geo.win : (RADIUS + k) * geo.win + span]
-        hi = shifted(0)
-        lo = (rows[RADIUS * geo.win : RADIUS * geo.win + span] - hi.astype(F32)).astype(jnp.bfloat16)
-        parts.append(jnp.concatenate([hi, lo] + [shifted(k) + shifted(-k) for k in FAR], axis=1))
-    deep = jnp.dot(jnp.concatenate(parts, axis=0), dw[...], preferred_element_type=F32)
+    rows = jnp.concatenate([u[pl.ds(x, count)].reshape(span, LANES) for u, _ in pairs], axis=0)
+    hi = rows.astype(jnp.bfloat16)
+    lo = (rows - hi.astype(F32)).astype(jnp.bfloat16)
+    deep = jnp.dot(jnp.concatenate([hi, lo], axis=1), dw[...], preferred_element_type=F32)
     for i in range(count):
         news = []
         for f, (u, prior) in enumerate(pairs):
             mid = [u[x + i, SUB * j : SUB * j + SUB, :] for j in range(jn)]
-            below = [jnp.where(first, 0.0, pltpu.roll(v, 1, 0)) for v in mid]
-            above = [jnp.where(last, 0.0, pltpu.roll(v, SUB - 1, 0)) for v in mid]
+            below = [pltpu.roll(v, 1, 0) for v in mid]
+            above = [pltpu.roll(v, SUB - 1, 0) for v in mid]
+            if masked:
+                below = [jnp.where(first, 0.0, v) for v in below]
+                above = [jnp.where(last, 0.0, v) for v in above]
             line = below + mid + above
             for j in range(jn):
                 tile = slice(SUB * j, SUB * j + SUB)
@@ -335,30 +328,23 @@
                     fed = pltpu.roll(gg[x + i, tile, :], (REC_DEPTH - moment) % LANES, 1)
                     acc = acc + jnp.where(at_depth, fed, 0.0)
                 for k in range(1, RADIUS + 1):
-                    near = line[jn + j + k] + line[jn + j - k]
-                    if k not in FAR:
-                        near = (u[x + i + k, tile, :] + u[x + i - k, tile, :]) + near
+                    near = (u[x + i + k, tile, :] + u[x + i - k, tile, :]) + (line[jn + j + k] + line[jn + j - k])
                     acc = acc + (near if k == 1 else RATIOS[k] * near)
                 new = (ee[x + i, tile, :] * mid[j] - prior[x + i, tile, :]) + cc[x + i, tile, :] * acc
                 prior[x + i, tile, :] = new
                 news.append(new)
-        for j in range(jn):
-            tile = slice(SUB * j, SUB * j + SUB)
-            product = news[j] * news[jn + j]
-            if not fresh:
-                product = product + corr[x + i - HALO + RADIUS, tile, :]
-            corr[x + i - HALO + RADIUS, tile, :] = product
-
-
-def one_step(geo, moment, us, ur, ps, pr, cc, ee, gg, corr, dw, wav, src, first, count, fresh):
-    group_planes = count // TRIPS
-
-    def group(i, carry):
-        x = first + i * group_planes
-        update_planes(geo, group_planes, ((us, ps), (ur, pr)), cc, ee, dw, x, moment, gg, corr, fresh)
-        return carry
-
-    lax.fori_loop(0, TRIPS, group, 0)
+        at = x + i - HALO
+        if 0 <= at < geo.nx:
+            for j in range(jn):
+                tile = slice(SUB * j, SUB * j + SUB)
+                product = news[j] * news[jn + j]
+                if not fresh:
+                    product = product + corr[at, tile, :]
+                corr[at, tile, :] = product
+
+
+def one_step(geo, moment, us, ur, ps, pr, cc, ee, gg, corr, dw, wav, src, first, count, fresh, masked):
+    update_planes(geo, count, ((us, ps), (ur, pr)), cc, ee, dw, first, moment, gg, corr, fresh, masked)
     xs, row, ok = src
 
     @pl.when(ok & (xs >= first) & (xs < first + count))
@@ -367,8 +353,11 @@
         shot = jnp.where(lane == SRC_DEPTH, pltpu.roll(wav[...], (SRC_DEPTH - moment) % LANES, 1), 0.0)
         add = cc[xs, pl.ds(row, 1), :] * shot[0:1]
         ps[xs, pl.ds(row, 1), :] = ps[xs, pl.ds(row, 1), :] + add
-        at = xs - HALO + RADIUS
-        corr[at, pl.ds(row, 1), :] = corr[at, pl.ds(row, 1), :] + add * pr[xs, pl.ds(row, 1), :]
+
+        @pl.when((xs >= HALO) & (xs < geo.nx + HALO))
+        def _():
+            at = xs - HALO
+            corr[at, pl.ds(row, 1), :] = corr[at, pl.ds(row, 1), :] + add * pr[xs, pl.ds(row, 1), :]
 
 
 def round_kernel(geo, block, last):
@@ -400,16 +389,19 @@
         unpack(geo, (us, ur), (ps, pr, cc) if first_round else (), inputs)
         if first_round:
 
+            sub = lax.broadcasted_iota(jnp.int32, (geo.win, LANES), 0) & (SUB - 1)
+            outer = sub == (SUB - 1) * (1 - p)
+
             def scale(x, carry):
                 speed = cc[x]
-                ee[x] = 2.0 + (3.0 * COEFFS[0]) * speed
+                ee[x] = jnp.where(outer, 0.0, 2.0 + (3.0 * COEFFS[0]) * speed)
                 cc[x] = COEFFS[1] * speed
                 return carry
 
             lax.fori_loop(0, geo.xe, scale, 0, unroll=2)
         common = (cc, ee, gg, corr, dw, wav, src)
-        one_step(geo, DEEP * block, us, ur, ps, pr, *common, HALO - RADIUS, geo.nx + 2 * RADIUS, first_round)
-        one_step(geo, DEEP * block + 1, ps, pr, us, ur, *common, HALO, geo.nx, False)
+        one_step(geo, DEEP * block, us, ur, ps, pr, *common, HALO - RADIUS, geo.nx + 2 * RADIUS, first_round, True)
+        one_step(geo, DEEP * block + 1, ps, pr, us, ur, *common, HALO, geo.nx, False, False)
         if not last:
             pack_y(geo, (us, ur), outs[0])
             pack_x(geo, (us, ur), outs[1:])
@@ -426,7 +418,7 @@
 
         def turn(x, carry):
             for j in range(geo.jn):
-                pad[x, pl.ds(j, SUB, stride=geo.jn), :] = corr[x + RADIUS, SUB * j : SUB * j + SUB, :]
+                pad[x, pl.ds(j, SUB, stride=geo.jn), :] = corr[x, SUB * j : SUB * j + SUB, :]
             return carry
 
         lax.fori_loop(0, geo.nx, turn, 0, unroll=4)
@@ -491,7 +483,7 @@
         )
         us, ur, ps, pr, cc, dw = call(
             load_kernel(geo),
-            [state] * 5 + [jax.ShapeDtypeStruct(((2 + len(FAR)) * LANES, LANES), jnp.bfloat16)],
+            [state] * 5 + [jax.ShapeDtypeStruct((2 * LANES, LANES), jnp.bfloat16)],
             [HBM] * 5,
             given,
             scratch=[pltpu.VMEM((5, nx, geo.win, nz), F32), pltpu.SemaphoreType.DMA((5,))],
@@ -504,7 +496,7 @@
             (ri, rc, traces, wavelet),
             scratch=[pltpu.VMEM((LANES, nrec), F32)],
         )
-        corr_shape = shape(nx + 2 * RADIUS, geo.win, nz)
+        corr_shape = shape(nx, geo.win, nz)
         corr = ee = None
         blocks = STEPS // DEEP
         for block in range(blocks):

time: 80 us -> 79.9 us (level)
  starting transfers between devices: 34.9 us -> 36 us
  Pallas kernels: 25.7 us -> 24.7 us
    ppermute x30, starting transfers between devices: 34.8 us -> 35.9 us  [run(): lax.ppermute(m, names, route)]
    pallas_call x11, Pallas kernels: 25.7 us -> 24.7 us  [call(): pl.pallas_call(body, out_shape=out_shapes, in_specs=specs, out_specs=out_...]
  transfers between devices with their start and end apart: 31 -> 31, of which waited for: 7 -> 7; matrix products, arithmetic and copies ran while one was open for 0% -> 0% of each run, Pallas kernels for 5% -> 6%
where the time goes in v4:
time: 79.9 us; the launch traced here: 79.6 us
  starting transfers between devices  36 us (45%)
  Pallas kernels  24.7 us (31%)
  waiting for transfers between devices  15.3 us (19%)
  between operations  2.18 us (3%)
    ppermute x30, starting transfers between devices, run(): lax.ppermute(m, names, route)  35.9 us
    pallas_call x11, Pallas kernels, call(): pl.pallas_call(body, out_shape=out_shapes, in_specs=specs, out_specs=out_...  24.7 us
    ppermute x30, waiting for transfers between devices, run(): lax.ppermute(m, names, route)  15.1 us
  transfers between devices with their start and end apart: 31, of which 7 were waited for; matrix products, arithmetic and copies ran while one was open for 0% of the time, Pallas kernels for 6%

profile of v4, /device:TPU:0, one launch (start us, length us, event | category | flops | bytes accessed | tf_op | source)
XLA Modules:
  0.0 79.6 jit_solution(13518406981706543788)
XLA Ops:
  0.6 1.5 %shard_map.148 = (f32[112,8,128]{2,1,0:T(8,128)S(1)}, f32[28,24,128]{2,1,0:T(8,128)S(1)}, f32[28,24,128]{2,1,0:T(8,128)S(1)}, f32[4,8,128]{2,1,0:T(8,128)S(1)}, f32[4,8,128]{2,1,0:T(8,128)S(1)}) custom-call(f32[1,32,24,128]{3,2,1,0:T(8,128)} %s0.3, f32[1,32,24,128]{3,2,1,0:T(8,128)} %s1_.3, f32[1,32,24,128]{3,2,1,0:T(8,128)} %r0.3, f32[1,32,24,128]{3,2,1,0:T(8,128)} %r1.3, ...), custom_call_target="tpu_custom_call" | custom-call | tf_op jit(solution)/shard_map/pallas_call | solution.py:85
  2.1 3.0 %collective-permute-start = (f32[112,8,128]{2,1,0:T(8,128)S(1)}, f32[112,8,128]{2,1,0:T(8,128)S(1)}, u32[]{:S(2)}, u32[]{:S(2)}) collective-permute-start(f32[112,8,128]{2,1,0:T(8,128)S(1)} %get-tuple-element.89), channel_id=1, source_target_pairs={{0,2},{1,3},{2,0},{3,1},{4,6},{5,7},{6,4},{7,5},{8,10},{9,11},{10,... | collective-permute-start | bytes 1376264 | tf_op jit(solution)/shard_map/ppermute | solution.py:472
  5.2 1.6 %collective-permute-start.1 = (f32[28,24,128]{2,1,0:T(8,128)S(1)}, f32[28,24,128]{2,1,0:T(8,128)S(1)}, u32[]{:S(2)}, u32[]{:S(2)}) collective-permute-start(f32[28,24,128]{2,1,0:T(8,128)S(1)} %get-tuple-element.90), channel_id=1, source_target_pairs={{0,4},{1,5},{2,6},{3,7},{4,0},{5,1},{6,2},{7,3},{8,12},{9,13},{10,... | collective-permute-start | bytes 1032200 | tf_op jit(solution)/shard_map/ppermute | solution.py:472
  6.7 3.1 %collective-permute-start.3 = (f32[4,8,128]{2,1,0:T(8,128)S(1)}, f32[4,8,128]{2,1,0:T(8,128)S(1)}, u32[]{:S(2)}, u32[]{:S(2)}) collective-permute-start(f32[4,8,128]{2,1,0:T(8,128)S(1)} %get-tuple-element.92), channel_id=1, source_target_pairs={{0,6},{1,7},{2,4},{3,5},{4,2},{5,3},{6,0},{7,1},{8,14},{9,15},{10,... | collective-permute-start | bytes 49160 | tf_op jit(solution)/shard_map/ppermute | solution.py:472
  9.9 1.7 %shard_map.146 = (f32[48,32,128]{2,1,0:T(8,128)S(1)}, f32[48,32,128]{2,1,0:T(8,128)S(1)}, f32[48,32,128]{2,1,0:T(8,128)S(1)}, f32[48,32,128]{2,1,0:T(8,128)S(1)}...) custom-call(f32[1,32,24,128]{3,2,1,0:T(8,128)} %s0.3, f32[1,32,24,128]{3,2,1,0:T(8,128)} %s1_.3, ...), custom_call_target="tpu_custom_call" | custom-call | tf_op jit(solution)/shard_map/pallas_call | solution.py:85
  12.8 0.0 copy-start
  12.9 0.0 copy-start.1
  12.9 0.0 copy-start.2
  12.9 0.6 copy-done
  13.5 0.0 copy-done.1
  13.5 0.0 copy-done.2
  13.5 1.5 %shard_map.147 = (f32[48,32,128]{2,1,0:T(8,128)S(1)}, f32[8,128]{1,0:T(8,128)S(1)}) custom-call(s32[1,64]{1,0:T(1,128)S(1)} %copy-done, s32[1,64]{1,0:T(1,128)S(1)} %copy-done.1, f32[1,12,64]{2,1,0:T(8,128)S(1)} %copy.46.traces, f32[1,12]{1,0:T(1,128)S(1)} %copy-done.2), custom_call_target="tpu_custom_call" | custom-call | tf_op jit(solution)/shard_map/pallas_call | solution.py:85
  15.0 0.0 collective-permute-done.3.refs_11_
  15.0 0.0 collective-permute-done.4.refs_12_
  15.0 0.0 collective-permute-done.2.refs_10_
  15.1 1.0 %collective-permute-done.refs_8_ = f32[112,8,128]{2,1,0:T(8,128)S(1)} collective-permute-done((f32[112,8,128]{2,1,0:T(8,128)S(1)}, f32[112,8,128]{2,1,0:T(8,128)S(1)}, u32[]{:S(2)}, u32[]{:S(2)}) %collective-permute-start) | collective-permute-done | bytes 458784 | tf_op jit(solution)/shard_map/ppermute | solution.py:472
  16.0 3.4 %shard_map.149 = (f32[48,32,128]{2,1,0:T(8,128)S(1)}, f32[48,32,128]{2,1,0:T(8,128)S(1)}, f32[48,32,128]{2,1,0:T(8,128)S(1)}, f32[48,32,128]{2,1,0:T(8,128)S(1)}...) custom-call(f32[48,32,128]{2,1,0:T(8,128)S(1)} %get-tuple-element.81, ...), custom_call_target="tpu_custom_call", output_to_operand_aliasing={{0}: (0, {}), {1}: (1, {}), {2}: (2, {}), {3}: (3, {}), {4}... | custom-call | tf_op jit(solution)/shard_map/pallas_call | solution.py:85
  19.4 1.8 %collective-permute-start.5 = (f32[64,8,128]{2,1,0:T(8,128)S(1)}, f32[64,8,128]{2,1,0:T(8,128)S(1)}, u32[]{:S(2)}, u32[]{:S(2)}) collective-permute-start(f32[64,8,128]{2,1,0:T(8,128)S(1)} %get-tuple-element.101), channel_id=1, source_target_pairs={{0,2},{1,3},{2,0},{3,1},{4,6},{5,7},{6,4},{7,5},{8,10},{9,11},{10,... | collective-permute-start | bytes 786440 | tf_op jit(solution)/shard_map/ppermute | solution.py:472
  21.2 2.0 %collective-permute-start.6 = (f32[16,24,128]{2,1,0:T(8,128)S(1)}, f32[16,24,128]{2,1,0:T(8,128)S(1)}, u32[]{:S(2)}, u32[]{:S(2)}) collective-permute-start(f32[16,24,128]{2,1,0:T(8,128)S(1)} %get-tuple-element.102), channel_id=1, source_target_pairs={{0,4},{1,5},{2,6},{3,7},{4,0},{5,1},{6,2},{7,3},{8,12},{9,13},{10,... | collective-permute-start | bytes 589832 | tf_op jit(solution)/shard_map/ppermute | solution.py:472
  23.2 0.0 collective-permute-start.7
  23.3 2.7 %collective-permute-start.8 = (f32[4,8,128]{2,1,0:T(8,128)S(1)}, f32[4,8,128]{2,1,0:T(8,128)S(1)}, u32[]{:S(2)}, u32[]{:S(2)}) collective-permute-start(f32[4,8,128]{2,1,0:T(8,128)S(1)} %get-tuple-element.104), channel_id=1, source_target_pairs={{0,6},{1,7},{2,4},{3,5},{4,2},{5,3},{6,0},{7,1},{8,14},{9,15},{10,... | collective-permute-start | bytes 49160 | tf_op jit(solution)/shard_map/ppermute | solution.py:472
  25.9 1.9 %collective-permute-done.8.refs_13_ = f32[4,8,128]{2,1,0:T(8,128)S(1)} collective-permute-done((f32[4,8,128]{2,1,0:T(8,128)S(1)}, f32[4,8,128]{2,1,0:T(8,128)S(1)}, u32[]{:S(2)}, u32[]{:S(2)}) %collective-permute-start.8) | collective-permute-done | bytes 16416 | tf_op jit(solution)/shard_map/ppermute | solution.py:472
  27.9 3.0 %shard_map.150 = (f32[48,32,128]{2,1,0:T(8,128)S(1)}, f32[48,32,128]{2,1,0:T(8,128)S(1)}, f32[48,32,128]{2,1,0:T(8,128)S(1)}, f32[48,32,128]{2,1,0:T(8,128)S(1)}...) custom-call(f32[48,32,128]{2,1,0:T(8,128)S(1)} %get-tuple-element.94, ...), custom_call_target="tpu_custom_call", output_to_operand_aliasing={{0}: (0, {}), {1}: (1, {}), {2}: (2, {}), {3}: (3, {}), {4}... | custom-call | tf_op jit(solution)/shard_map/pallas_call | solution.py:85
  31.0 1.3 %collective-permute-start.10 = (f32[64,8,128]{2,1,0:T(8,128)S(1)}, f32[64,8,128]{2,1,0:T(8,128)S(1)}, u32[]{:S(2)}, u32[]{:S(2)}) collective-permute-start(f32[64,8,128]{2,1,0:T(8,128)S(1)} %get-tuple-element.111), channel_id=1, source_target_pairs={{0,2},{1,3},{2,0},{3,1},{4,6},{5,7},{6,4},{7,5},{8,10},{9,11},{10,... | collective-permute-start | bytes 786440 | tf_op jit(solution)/shard_map/ppermute | solution.py:472
  32.3 2.3 %collective-permute-start.11 = (f32[16,24,128]{2,1,0:T(8,128)S(1)}, f32[16,24,128]{2,1,0:T(8,128)S(1)}, u32[]{:S(2)}, u32[]{:S(2)}) collective-permute-start(f32[16,24,128]{2,1,0:T(8,128)S(1)} %get-tuple-element.112), channel_id=1, source_target_pairs={{0,4},{1,5},{2,6},{3,7},{4,0},{5,1},{6,2},{7,3},{8,12},{9,13},{10,... | collective-permute-start | bytes 589832 | tf_op jit(solution)/shard_map/ppermute | solution.py:472
  34.6 2.1 %collective-permute-start.13 = (f32[4,8,128]{2,1,0:T(8,128)S(1)}, f32[4,8,128]{2,1,0:T(8,128)S(1)}, u32[]{:S(2)}, u32[]{:S(2)}) collective-permute-start(f32[4,8,128]{2,1,0:T(8,128)S(1)} %get-tuple-element.114), channel_id=1, source_target_pairs={{0,6},{1,7},{2,4},{3,5},{4,2},{5,3},{6,0},{7,1},{8,14},{9,15},{10,... | collective-permute-start | bytes 49160 | tf_op jit(solution)/shard_map/ppermute | solution.py:472
  36.7 2.8 %collective-permute-done.13.refs_13_ = f32[4,8,128]{2,1,0:T(8,128)S(1)} collective-permute-done((f32[4,8,128]{2,1,0:T(8,128)S(1)}, f32[4,8,128]{2,1,0:T(8,128)S(1)}, u32[]{:S(2)}, u32[]{:S(2)}) %collective-permute-start.13) | collective-permute-done | bytes 16416 | tf_op jit(solution)/shard_map/ppermute | solution.py:472
  39.5 3.1 %shard_map.151 = (f32[48,32,128]{2,1,0:T(8,128)S(1)}, f32[48,32,128]{2,1,0:T(8,128)S(1)}, f32[48,32,128]{2,1,0:T(8,128)S(1)}, f32[48,32,128]{2,1,0:T(8,128)S(1)}...) custom-call(f32[48,32,128]{2,1,0:T(8,128)S(1)} %get-tuple-element.10, ...), custom_call_target="tpu_custom_call", output_to_operand_aliasing={{0}: (0, {}), {1}: (1, {}), {2}: (2, {}), {3}: (3, {}), {4}... | custom-call | tf_op jit(solution)/shard_map/pallas_call | solution.py:85
  42.6 1.3 %collective-permute-start.15 = (f32[64,8,128]{2,1,0:T(8,128)S(1)}, f32[64,8,128]{2,1,0:T(8,128)S(1)}, u32[]{:S(2)}, u32[]{:S(2)}) collective-permute-start(f32[64,8,128]{2,1,0:T(8,128)S(1)} %get-tuple-element.121), channel_id=1, source_target_pairs={{0,2},{1,3},{2,0},{3,1},{4,6},{5,7},{6,4},{7,5},{8,10},{9,11},{10,... | collective-permute-start | bytes 786440 | tf_op jit(solution)/shard_map/ppermute | solution.py:472
  43.9 2.1 %collective-permute-start.16 = (f32[16,24,128]{2,1,0:T(8,128)S(1)}, f32[16,24,128]{2,1,0:T(8,128)S(1)}, u32[]{:S(2)}, u32[]{:S(2)}) collective-permute-start(f32[16,24,128]{2,1,0:T(8,128)S(1)} %get-tuple-element.122), channel_id=1, source_target_pairs={{0,4},{1,5},{2,6},{3,7},{4,0},{5,1},{6,2},{7,3},{8,12},{9,13},{10,... | collective-permute-start | bytes 589832 | tf_op jit(solution)/shard_map/ppermute | solution.py:472
  45.9 2.2 %collective-permute-start.18 = (f32[4,8,128]{2,1,0:T(8,128)S(1)}, f32[4,8,128]{2,1,0:T(8,128)S(1)}, u32[]{:S(2)}, u32[]{:S(2)}) collective-permute-start(f32[4,8,128]{2,1,0:T(8,128)S(1)} %get-tuple-element.124), channel_id=1, source_target_pairs={{0,6},{1,7},{2,4},{3,5},{4,2},{5,3},{6,0},{7,1},{8,14},{9,15},{10,... | collective-permute-start | bytes 49160 | tf_op jit(solution)/shard_map/ppermute | solution.py:472
  48.1 3.2 %collective-permute-done.18.refs_13_ = f32[4,8,128]{2,1,0:T(8,128)S(1)} collective-permute-done((f32[4,8,128]{2,1,0:T(8,128)S(1)}, f32[4,8,128]{2,1,0:T(8,128)S(1)}, u32[]{:S(2)}, u32[]{:S(2)}) %collective-permute-start.18) | collective-permute-done | bytes 16416 | tf_op jit(solution)/shard_map/ppermute | solution.py:472
  51.3 3.3 %shard_map.152 = (f32[48,32,128]{2,1,0:T(8,128)S(1)}, f32[48,32,128]{2,1,0:T(8,128)S(1)}, f32[48,32,128]{2,1,0:T(8,128)S(1)}, f32[48,32,128]{2,1,0:T(8,128)S(1)}...) custom-call(f32[48,32,128]{2,1,0:T(8,128)S(1)} %get-tuple-element.11, ...), custom_call_target="tpu_custom_call", output_to_operand_aliasing={{0}: (0, {}), {1}: (1, {}), {2}: (2, {}), {3}: (3, {}), {4}... | custom-call | tf_op jit(solution)/shard_map/pallas_call | solution.py:85
  54.6 0.8 %collective-permute-start.20 = (f32[64,8,128]{2,1,0:T(8,128)S(1)}, f32[64,8,128]{2,1,0:T(8,128)S(1)}, u32[]{:S(2)}, u32[]{:S(2)}) collective-permute-start(f32[64,8,128]{2,1,0:T(8,128)S(1)} %get-tuple-element.131), channel_id=1, source_target_pairs={{0,2},{1,3},{2,0},{3,1},{4,6},{5,7},{6,4},{7,5},{8,10},{9,11},{10,... | collective-permute-start | bytes 786440 | tf_op jit(solution)/shard_map/ppermute | solution.py:472
  55.4 2.2 %collective-permute-start.21 = (f32[16,24,128]{2,1,0:T(8,128)S(1)}, f32[16,24,128]{2,1,0:T(8,128)S(1)}, u32[]{:S(2)}, u32[]{:S(2)}) collective-permute-start(f32[16,24,128]{2,1,0:T(8,128)S(1)} %get-tuple-element.132), channel_id=1, source_target_pairs={{0,4},{1,5},{2,6},{3,7},{4,0},{5,1},{6,2},{7,3},{8,12},{9,13},{10,... | collective-permute-start | bytes 589832 | tf_op jit(solution)/shard_map/ppermute | solution.py:472
  57.7 2.1 %collective-permute-start.23 = (f32[4,8,128]{2,1,0:T(8,128)S(1)}, f32[4,8,128]{2,1,0:T(8,128)S(1)}, u32[]{:S(2)}, u32[]{:S(2)}) collective-permute-start(f32[4,8,128]{2,1,0:T(8,128)S(1)} %get-tuple-element.134), channel_id=1, source_target_pairs={{0,6},{1,7},{2,4},{3,5},{4,2},{5,3},{6,0},{7,1},{8,14},{9,15},{10,... | collective-permute-start | bytes 49160 | tf_op jit(solution)/shard_map/ppermute | solution.py:472
  59.8 3.3 %collective-permute-done.23.refs_13_ = f32[4,8,128]{2,1,0:T(8,128)S(1)} collective-permute-done((f32[4,8,128]{2,1,0:T(8,128)S(1)}, f32[4,8,128]{2,1,0:T(8,128)S(1)}, u32[]{:S(2)}, u32[]{:S(2)}) %collective-permute-start.23) | collective-permute-done | bytes 16416 | tf_op jit(solution)/shard_map/ppermute | solution.py:472
  63.1 3.1 %shard_map.153 = (f32[48,32,128]{2,1,0:T(8,128)S(1)}, f32[48,32,128]{2,1,0:T(8,128)S(1)}, f32[48,32,128]{2,1,0:T(8,128)S(1)}, f32[48,32,128]{2,1,0:T(8,128)S(1)}...) custom-call(f32[48,32,128]{2,1,0:T(8,128)S(1)} %get-tuple-element.12, ...), custom_call_target="tpu_custom_call", output_to_operand_aliasing={{0}: (0, {}), {1}: (1, {}), {2}: (2, {}), {3}: (3, {}), {4}... | custom-call | tf_op jit(solution)/shard_map/pallas_call | solution.py:85
  66.2 0.7 collective-permute-start.25
  66.9 2.1 %collective-permute-start.26 = (f32[16,24,128]{2,1,0:T(8,128)S(1)}, f32[16,24,128]{2,1,0:T(8,128)S(1)}, u32[]{:S(2)}, u32[]{:S(2)}) collective-permute-start(f32[16,24,128]{2,1,0:T(8,128)S(1)} %get-tuple-element.142), channel_id=1, source_target_pairs={{0,4},{1,5},{2,6},{3,7},{4,0},{5,1},{6,2},{7,3},{8,12},{9,13},{10,... | collective-permute-start | bytes 589832 | tf_op jit(solution)/shard_map/ppermute | solution.py:472
  69.0 2.4 %collective-permute-start.28 = (f32[4,8,128]{2,1,0:T(8,128)S(1)}, f32[4,8,128]{2,1,0:T(8,128)S(1)}, u32[]{:S(2)}, u32[]{:S(2)}) collective-permute-start(f32[4,8,128]{2,1,0:T(8,128)S(1)} %get-tuple-element.144), channel_id=1, source_target_pairs={{0,6},{1,7},{2,4},{3,5},{4,2},{5,3},{6,0},{7,1},{8,14},{9,15},{10,... | collective-permute-start | bytes 49160 | tf_op jit(solution)/shard_map/ppermute | solution.py:472
  71.4 2.9 %collective-permute-done.28.refs_13_ = f32[4,8,128]{2,1,0:T(8,128)S(1)} collective-permute-done((f32[4,8,128]{2,1,0:T(8,128)S(1)}, f32[4,8,128]{2,1,0:T(8,128)S(1)}, u32[]{:S(2)}, u32[]{:S(2)}) %collective-permute-start.28) | collective-permute-done | bytes 16416 | tf_op jit(solution)/shard_map/ppermute | solution.py:472
  74.3 2.9 %shard_map.154 = (f32[48,32,128]{2,1,0:T(8,128)S(1)}, f32[48,32,128]{2,1,0:T(8,128)S(1)}, f32[48,32,128]{2,1,0:T(8,128)S(1)}, f32[48,32,128]{2,1,0:T(8,128)S(1)}, f32[32,32,128]{2,1,0:T(8,128)S(1)}) custom-call(f32[48,32,128]{2,1,0:T(8,128)S(1)} %get-tuple-element.136.refs_0_, ...), custom_call_target="tpu_custom_call", output_to_operand_aliasing={{0}: (0, {}), {1}: (1, {}), {2}: (2, {}), {3}: (3, {}), {4}... | custom-call | tf_op jit(solution)/shard_map/pallas_call | solution.py:85
  77.2 0.1 shard_map.156
  77.3 0.1 collective-permute-start.30
  77.4 1.2 %shard_map.155 = (f32[1,32,24,128]{3,2,1,0:T(8,128)}, f32[1,32,24,128]{3,2,1,0:T(8,128)}, f32[1,32,24,128]{3,2,1,0:T(8,128)}, f32[1,32,24,128]{3,2,1,0:T(8,128)}) custom-call(f32[48,32,128]{2,1,0:T(8,128)S(1)} %get-tuple-element.146.us, f32[48,32,128]{2,1,0:T(8,128)S(1)} %get-tuple-element.147.ur, f32[48,32,128]{2,1,0:T(8,128)S(1)} %get-tuple-element.148.ps, ...), custom_call_target="tpu_custom_call" | custom-call | tf_op jit(solution)/shard_map/pallas_call | solution.py:85
  78.7 0.2 collective-permute-done.30
  78.9 0.7 add_multiply_fusion
  (35 shorter events, 0.1 us)
Async XLA Ops:
  2.1 13.9 %collective-permute-start = (f32[112,8,128]{2,1,0:T(8,128)S(1)}, f32[112,8,128]{2,1,0:T(8,128)S(1)}, u32[]{:S(2)}, u32[]{:S(2)}) collective-permute-start(f32[112,8,128]{2,1,0:T(8,128)S(1)} %get-tuple-element.89), channel_id=1, source_target_pairs={{0,2},{1,3},{2,0},{3,1},{4,6},{5,7},{6,4},{7,5},{8,10},{9,11},{10,... | collective-permute-start | bytes 1376264 | tf_op jit(solution)/shard_map/ppermute | solution.py:472
  5.2 9.9 %collective-permute-start.1 = (f32[28,24,128]{2,1,0:T(8,128)S(1)}, f32[28,24,128]{2,1,0:T(8,128)S(1)}, u32[]{:S(2)}, u32[]{:S(2)}) collective-permute-start(f32[28,24,128]{2,1,0:T(8,128)S(1)} %get-tuple-element.90), channel_id=1, source_target_pairs={{0,4},{1,5},{2,6},{3,7},{4,0},{5,1},{6,2},{7,3},{8,12},{9,13},{10,... | collective-permute-start | bytes 1032200 | tf_op jit(solution)/shard_map/ppermute | solution.py:472
  6.7 8.3 %collective-permute-start.2 = (f32[28,24,128]{2,1,0:T(8,128)S(1)}, f32[28,24,128]{2,1,0:T(8,128)S(1)}, u32[]{:S(2)}, u32[]{:S(2)}) collective-permute-start(f32[28,24,128]{2,1,0:T(8,128)S(1)} %get-tuple-element.91), channel_id=1, source_target_pairs={{0,1},{1,0},{2,3},{3,2},{4,8},{5,9},{6,10},{7,11},{8,4},{9,5},{10,... | collective-permute-start | bytes 1032200 | tf_op jit(solution)/shard_map/ppermute | solution.py:472
  6.7 8.3 %collective-permute-start.3 = (f32[4,8,128]{2,1,0:T(8,128)S(1)}, f32[4,8,128]{2,1,0:T(8,128)S(1)}, u32[]{:S(2)}, u32[]{:S(2)}) collective-permute-start(f32[4,8,128]{2,1,0:T(8,128)S(1)} %get-tuple-element.92), channel_id=1, source_target_pairs={{0,6},{1,7},{2,4},{3,5},{4,2},{5,3},{6,0},{7,1},{8,14},{9,15},{10,... | collective-permute-start | bytes 49160 | tf_op jit(solution)/shard_map/ppermute | solution.py:472
  9.9 5.2 %collective-permute-start.4 = (f32[4,8,128]{2,1,0:T(8,128)S(1)}, f32[4,8,128]{2,1,0:T(8,128)S(1)}, u32[]{:S(2)}, u32[]{:S(2)}) collective-permute-start(f32[4,8,128]{2,1,0:T(8,128)S(1)} %get-tuple-element.93), channel_id=1, source_target_pairs={{0,1},{1,0},{2,3},{3,2},{4,10},{5,11},{6,8},{7,9},{8,6},{9,7},{10,... | collective-permute-start | bytes 49160 | tf_op jit(solution)/shard_map/ppermute | solution.py:472
  9.9 3.0 %copy-start.3 = (f32[1,12,64]{2,0,1:T(1,128)S(1)}, f32[1,12,64]{2,0,1:T(1,128)}, u32[]{:S(2)}) copy-start(f32[1,12,64]{2,0,1:T(1,128)} %param.17) | copy-start | bytes 9220
  12.8 0.7 copy-start
  12.9 0.7 copy-start.1
  12.9 0.7 copy-start.2
  19.4 8.5 %collective-permute-start.5 = (f32[64,8,128]{2,1,0:T(8,128)S(1)}, f32[64,8,128]{2,1,0:T(8,128)S(1)}, u32[]{:S(2)}, u32[]{:S(2)}) collective-permute-start(f32[64,8,128]{2,1,0:T(8,128)S(1)} %get-tuple-element.101), channel_id=1, source_target_pairs={{0,2},{1,3},{2,0},{3,1},{4,6},{5,7},{6,4},{7,5},{8,10},{9,11},{10,... | collective-permute-start | bytes 786440 | tf_op jit(solution)/shard_map/ppermute | solution.py:472
  21.2 6.7 %collective-permute-start.6 = (f32[16,24,128]{2,1,0:T(8,128)S(1)}, f32[16,24,128]{2,1,0:T(8,128)S(1)}, u32[]{:S(2)}, u32[]{:S(2)}) collective-permute-start(f32[16,24,128]{2,1,0:T(8,128)S(1)} %get-tuple-element.102), channel_id=1, source_target_pairs={{0,4},{1,5},{2,6},{3,7},{4,0},{5,1},{6,2},{7,3},{8,12},{9,13},{10,... | collective-permute-start | bytes 589832 | tf_op jit(solution)/shard_map/ppermute | solution.py:472
  23.2 4.7 %collective-permute-start.7 = (f32[16,24,128]{2,1,0:T(8,128)S(1)}, f32[16,24,128]{2,1,0:T(8,128)S(1)}, u32[]{:S(2)}, u32[]{:S(2)}) collective-permute-start(f32[16,24,128]{2,1,0:T(8,128)S(1)} %get-tuple-element.103), channel_id=1, source_target_pairs={{0,1},{1,0},{2,3},{3,2},{4,8},{5,9},{6,10},{7,11},{8,4},{9,5},{10,... | collective-permute-start | bytes 589832 | tf_op jit(solution)/shard_map/ppermute | solution.py:472
  23.3 4.6 %collective-permute-start.8 = (f32[4,8,128]{2,1,0:T(8,128)S(1)}, f32[4,8,128]{2,1,0:T(8,128)S(1)}, u32[]{:S(2)}, u32[]{:S(2)}) collective-permute-start(f32[4,8,128]{2,1,0:T(8,128)S(1)} %get-tuple-element.104), channel_id=1, source_target_pairs={{0,6},{1,7},{2,4},{3,5},{4,2},{5,3},{6,0},{7,1},{8,14},{9,15},{10,... | collective-permute-start | bytes 49160 | tf_op jit(solution)/shard_map/ppermute | solution.py:472
  25.9 2.0 %collective-permute-start.9 = (f32[4,8,128]{2,1,0:T(8,128)S(1)}, f32[4,8,128]{2,1,0:T(8,128)S(1)}, u32[]{:S(2)}, u32[]{:S(2)}) collective-permute-start(f32[4,8,128]{2,1,0:T(8,128)S(1)} %get-tuple-element.105), channel_id=1, source_target_pairs={{0,1},{1,0},{2,3},{3,2},{4,10},{5,11},{6,8},{7,9},{8,6},{9,7},{10,... | collective-permute-start | bytes 49160 | tf_op jit(solution)/shard_map/ppermute | solution.py:472
  31.0 8.5 %collective-permute-start.10 = (f32[64,8,128]{2,1,0:T(8,128)S(1)}, f32[64,8,128]{2,1,0:T(8,128)S(1)}, u32[]{:S(2)}, u32[]{:S(2)}) collective-permute-start(f32[64,8,128]{2,1,0:T(8,128)S(1)} %get-tuple-element.111), channel_id=1, source_target_pairs={{0,2},{1,3},{2,0},{3,1},{4,6},{5,7},{6,4},{7,5},{8,10},{9,11},{10,... | collective-permute-start | bytes 786440 | tf_op jit(solution)/shard_map/ppermute | solution.py:472
  32.3 7.2 %collective-permute-start.11 = (f32[16,24,128]{2,1,0:T(8,128)S(1)}, f32[16,24,128]{2,1,0:T(8,128)S(1)}, u32[]{:S(2)}, u32[]{:S(2)}) collective-permute-start(f32[16,24,128]{2,1,0:T(8,128)S(1)} %get-tuple-element.112), channel_id=1, source_target_pairs={{0,4},{1,5},{2,6},{3,7},{4,0},{5,1},{6,2},{7,3},{8,12},{9,13},{10,... | collective-permute-start | bytes 589832 | tf_op jit(solution)/shard_map/ppermute | solution.py:472
  34.6 4.9 %collective-permute-start.12 = (f32[16,24,128]{2,1,0:T(8,128)S(1)}, f32[16,24,128]{2,1,0:T(8,128)S(1)}, u32[]{:S(2)}, u32[]{:S(2)}) collective-permute-start(f32[16,24,128]{2,1,0:T(8,128)S(1)} %get-tuple-element.113), channel_id=1, source_target_pairs={{0,1},{1,0},{2,3},{3,2},{4,8},{5,9},{6,10},{7,11},{8,4},{9,5},{10,... | collective-permute-start | bytes 589832 | tf_op jit(solution)/shard_map/ppermute | solution.py:472
  34.6 4.9 %collective-permute-start.13 = (f32[4,8,128]{2,1,0:T(8,128)S(1)}, f32[4,8,128]{2,1,0:T(8,128)S(1)}, u32[]{:S(2)}, u32[]{:S(2)}) collective-permute-start(f32[4,8,128]{2,1,0:T(8,128)S(1)} %get-tuple-element.114), channel_id=1, source_target_pairs={{0,6},{1,7},{2,4},{3,5},{4,2},{5,3},{6,0},{7,1},{8,14},{9,15},{10,... | collective-permute-start | bytes 49160 | tf_op jit(solution)/shard_map/ppermute | solution.py:472
  36.7 2.8 %collective-permute-start.14 = (f32[4,8,128]{2,1,0:T(8,128)S(1)}, f32[4,8,128]{2,1,0:T(8,128)S(1)}, u32[]{:S(2)}, u32[]{:S(2)}) collective-permute-start(f32[4,8,128]{2,1,0:T(8,128)S(1)} %get-tuple-element.115), channel_id=1, source_target_pairs={{0,1},{1,0},{2,3},{3,2},{4,10},{5,11},{6,8},{7,9},{8,6},{9,7},{10,... | collective-permute-start | bytes 49160 | tf_op jit(solution)/shard_map/ppermute | solution.py:472
  42.6 8.7 %collective-permute-start.15 = (f32[64,8,128]{2,1,0:T(8,128)S(1)}, f32[64,8,128]{2,1,0:T(8,128)S(1)}, u32[]{:S(2)}, u32[]{:S(2)}) collective-permute-start(f32[64,8,128]{2,1,0:T(8,128)S(1)} %get-tuple-element.121), channel_id=1, source_target_pairs={{0,2},{1,3},{2,0},{3,1},{4,6},{5,7},{6,4},{7,5},{8,10},{9,11},{10,... | collective-permute-start | bytes 786440 | tf_op jit(solution)/shard_map/ppermute | solution.py:472
  43.9 7.5 %collective-permute-start.16 = (f32[16,24,128]{2,1,0:T(8,128)S(1)}, f32[16,24,128]{2,1,0:T(8,128)S(1)}, u32[]{:S(2)}, u32[]{:S(2)}) collective-permute-start(f32[16,24,128]{2,1,0:T(8,128)S(1)} %get-tuple-element.122), channel_id=1, source_target_pairs={{0,4},{1,5},{2,6},{3,7},{4,0},{5,1},{6,2},{7,3},{8,12},{9,13},{10,... | collective-permute-start | bytes 589832 | tf_op jit(solution)/shard_map/ppermute | solution.py:472
  45.9 5.4 %collective-permute-start.17 = (f32[16,24,128]{2,1,0:T(8,128)S(1)}, f32[16,24,128]{2,1,0:T(8,128)S(1)}, u32[]{:S(2)}, u32[]{:S(2)}) collective-permute-start(f32[16,24,128]{2,1,0:T(8,128)S(1)} %get-tuple-element.123), channel_id=1, source_target_pairs={{0,1},{1,0},{2,3},{3,2},{4,8},{5,9},{6,10},{7,11},{8,4},{9,5},{10,... | collective-permute-start | bytes 589832 | tf_op jit(solution)/shard_map/ppermute | solution.py:472
  45.9 5.4 %collective-permute-start.18 = (f32[4,8,128]{2,1,0:T(8,128)S(1)}, f32[4,8,128]{2,1,0:T(8,128)S(1)}, u32[]{:S(2)}, u32[]{:S(2)}) collective-permute-start(f32[4,8,128]{2,1,0:T(8,128)S(1)} %get-tuple-element.124), channel_id=1, source_target_pairs={{0,6},{1,7},{2,4},{3,5},{4,2},{5,3},{6,0},{7,1},{8,14},{9,15},{10,... | collective-permute-start | bytes 49160 | tf_op jit(solution)/shard_map/ppermute | solution.py:472
  48.1 3.2 %collective-permute-start.19 = (f32[4,8,128]{2,1,0:T(8,128)S(1)}, f32[4,8,128]{2,1,0:T(8,128)S(1)}, u32[]{:S(2)}, u32[]{:S(2)}) collective-permute-start(f32[4,8,128]{2,1,0:T(8,128)S(1)} %get-tuple-element.125), channel_id=1, source_target_pairs={{0,1},{1,0},{2,3},{3,2},{4,10},{5,11},{6,8},{7,9},{8,6},{9,7},{10,... | collective-permute-start | bytes 49160 | tf_op jit(solution)/shard_map/ppermute | solution.py:472
  54.6 8.5 %collective-permute-start.20 = (f32[64,8,128]{2,1,0:T(8,128)S(1)}, f32[64,8,128]{2,1,0:T(8,128)S(1)}, u32[]{:S(2)}, u32[]{:S(2)}) collective-permute-start(f32[64,8,128]{2,1,0:T(8,128)S(1)} %get-tuple-element.131), channel_id=1, source_target_pairs={{0,2},{1,3},{2,0},{3,1},{4,6},{5,7},{6,4},{7,5},{8,10},{9,11},{10,... | collective-permute-start | bytes 786440 | tf_op jit(solution)/shard_map/ppermute | solution.py:472
  55.4 7.6 %collective-permute-start.21 = (f32[16,24,128]{2,1,0:T(8,128)S(1)}, f32[16,24,128]{2,1,0:T(8,128)S(1)}, u32[]{:S(2)}, u32[]{:S(2)}) collective-permute-start(f32[16,24,128]{2,1,0:T(8,128)S(1)} %get-tuple-element.132), channel_id=1, source_target_pairs={{0,4},{1,5},{2,6},{3,7},{4,0},{5,1},{6,2},{7,3},{8,12},{9,13},{10,... | collective-permute-start | bytes 589832 | tf_op jit(solution)/shard_map/ppermute | solution.py:472
  57.7 5.4 %collective-permute-start.22 = (f32[16,24,128]{2,1,0:T(8,128)S(1)}, f32[16,24,128]{2,1,0:T(8,128)S(1)}, u32[]{:S(2)}, u32[]{:S(2)}) collective-permute-start(f32[16,24,128]{2,1,0:T(8,128)S(1)} %get-tuple-element.133), channel_id=1, source_target_pairs={{0,1},{1,0},{2,3},{3,2},{4,8},{5,9},{6,10},{7,11},{8,4},{9,5},{10,... | collective-permute-start | bytes 589832 | tf_op jit(solution)/shard_map/ppermute | solution.py:472
  57.7 5.4 %collective-permute-start.23 = (f32[4,8,128]{2,1,0:T(8,128)S(1)}, f32[4,8,128]{2,1,0:T(8,128)S(1)}, u32[]{:S(2)}, u32[]{:S(2)}) collective-permute-start(f32[4,8,128]{2,1,0:T(8,128)S(1)} %get-tuple-element.134), channel_id=1, source_target_pairs={{0,6},{1,7},{2,4},{3,5},{4,2},{5,3},{6,0},{7,1},{8,14},{9,15},{10,... | collective-permute-start | bytes 49160 | tf_op jit(solution)/shard_map/ppermute | solution.py:472
  59.8 3.3 %collective-permute-start.24 = (f32[4,8,128]{2,1,0:T(8,128)S(1)}, f32[4,8,128]{2,1,0:T(8,128)S(1)}, u32[]{:S(2)}, u32[]{:S(2)}) collective-permute-start(f32[4,8,128]{2,1,0:T(8,128)S(1)} %get-tuple-element.135), channel_id=1, source_target_pairs={{0,1},{1,0},{2,3},{3,2},{4,10},{5,11},{6,8},{7,9},{8,6},{9,7},{10,... | collective-permute-start | bytes 49160 | tf_op jit(solution)/shard_map/ppermute | solution.py:472
  66.2 8.1 %collective-permute-start.25 = (f32[64,8,128]{2,1,0:T(8,128)S(1)}, f32[64,8,128]{2,1,0:T(8,128)S(1)}, u32[]{:S(2)}, u32[]{:S(2)}) collective-permute-start(f32[64,8,128]{2,1,0:T(8,128)S(1)} %get-tuple-element.141), channel_id=1, source_target_pairs={{0,2},{1,3},{2,0},{3,1},{4,6},{5,7},{6,4},{7,5},{8,10},{9,11},{10,... | collective-permute-start | bytes 786440 | tf_op jit(solution)/shard_map/ppermute | solution.py:472
  66.9 7.4 %collective-permute-start.26 = (f32[16,24,128]{2,1,0:T(8,128)S(1)}, f32[16,24,128]{2,1,0:T(8,128)S(1)}, u32[]{:S(2)}, u32[]{:S(2)}) collective-permute-start(f32[16,24,128]{2,1,0:T(8,128)S(1)} %get-tuple-element.142), channel_id=1, source_target_pairs={{0,4},{1,5},{2,6},{3,7},{4,0},{5,1},{6,2},{7,3},{8,12},{9,13},{10,... | collective-permute-start | bytes 589832 | tf_op jit(solution)/shard_map/ppermute | solution.py:472
  69.0 5.3 %collective-permute-start.27 = (f32[16,24,128]{2,1,0:T(8,128)S(1)}, f32[16,24,128]{2,1,0:T(8,128)S(1)}, u32[]{:S(2)}, u32[]{:S(2)}) collective-permute-start(f32[16,24,128]{2,1,0:T(8,128)S(1)} %get-tuple-element.143), channel_id=1, source_target_pairs={{0,1},{1,0},{2,3},{3,2},{4,8},{5,9},{6,10},{7,11},{8,4},{9,5},{10,... | collective-permute-start | bytes 589832 | tf_op jit(solution)/shard_map/ppermute | solution.py:472
  69.0 5.3 %collective-permute-start.28 = (f32[4,8,128]{2,1,0:T(8,128)S(1)}, f32[4,8,128]{2,1,0:T(8,128)S(1)}, u32[]{:S(2)}, u32[]{:S(2)}) collective-permute-start(f32[4,8,128]{2,1,0:T(8,128)S(1)} %get-tuple-element.144), channel_id=1, source_target_pairs={{0,6},{1,7},{2,4},{3,5},{4,2},{5,3},{6,0},{7,1},{8,14},{9,15},{10,... | collective-permute-start | bytes 49160 | tf_op jit(solution)/shard_map/ppermute | solution.py:472
  71.4 2.9 %collective-permute-start.29 = (f32[4,8,128]{2,1,0:T(8,128)S(1)}, f32[4,8,128]{2,1,0:T(8,128)S(1)}, u32[]{:S(2)}, u32[]{:S(2)}) collective-permute-start(f32[4,8,128]{2,1,0:T(8,128)S(1)} %get-tuple-element.145), channel_id=1, source_target_pairs={{0,1},{1,0},{2,3},{3,2},{4,10},{5,11},{6,8},{7,9},{8,6},{9,7},{10,... | collective-permute-start | bytes 49160 | tf_op jit(solution)/shard_map/ppermute | solution.py:472
  77.3 1.5 %collective-permute-start.30 = (f32[16,24,128]{2,1,0:T(8,128)S(1)}, f32[16,24,128]{2,1,0:T(8,128)S(1)}, u32[]{:S(2)}, u32[]{:S(2)}) collective-permute-start(f32[16,24,128]{2,1,0:T(8,128)S(1)} %get-tuple-element.156), channel_id=1, source_target_pairs={{0,1},{1,0},{2,3},{3,2},{4,5},{5,4},{6,7},{7,6},{8,9},{9,8},{10,11... | collective-permute-start | bytes 589832 | tf_op jit(solution)/shard_map/ppermute | solution.py:533
